TPU v7x, 768 devices: a whole 4x8x12 slice. The times are simulated.
768 devices in a mesh: pipe: 64 (over y, z_hi, core), expert: 12 (over x, z_lo).
Axes of the slice: x: 4, y: 8, z: 12 (z_hi: 4, z_lo: 3; z = z_hi * 3 + z_lo), core: 2. Of those that a mesh axis runs over, the one named last changes fastest.
Arguments:
- flowing: bfloat16 [2, 1152, 14336], P(None, 'expert', 'pipe'), may hold values from -6 to 6
- norm_gain: float32 [14336], P('pipe'), may hold values from 0.5 to 1.5
- gate_up: bfloat16 [12, 64, 896, 1024], P('expert', 'pipe'), may hold values from -0.0625 to 0.0625
- down_proj: bfloat16 [12, 64, 896, 512], P('expert', 'pipe'), may hold values from -0.125 to 0.125
- down_step: bfloat16 [12, 64, 896, 512], P('expert', 'pipe'), may hold values from -0.0625 to 0.0625
- step_rate: float32 [12, 2], P('expert'), may hold values from 0.5 to 2
- routes: int32 [2, 2, 2, 1152, 2], P(None, None, None, 'expert'), may hold values from 0 to 11, all different within a row; in each aligned block of 96 rows (0 to 95, 96 to 191, ..., all dimensions but the last counted through in order) at most 18 rows name the same one
- scores: float32 [2, 2, 2, 1152, 2], P(None, None, None, 'expert'), may hold values from 0.05 to 1
Outputs:
- flowing_out: bfloat16 [2, 1152, 14336], P(None, 'expert', 'pipe')
Inputs may be any that keep to these rules, and one draw needn't show every extreme that they name: `routes`: each token names 2 different experts. In each aligned block of 96 rows (the tokens of one expert rank for one step, section and direction) no expert is named by more than 18 rows.
All inputs are finite; a program needn't handle non-finite values.
Results may differ from a plain program's by a relative error of at most 0.02.
Values may be sent and summed in bfloat16 or wider, within the bound.
No kernel may reach another device: no remote copies, remote signals or barrier semaphores. Data moves between devices by JAX's collectives and lax.ppermute only.
A program may use at most 32 MiB of HBM per device.

v0:
```python
import jax
import jax.numpy as jnp
from jax import lax
from jax.sharding import PartitionSpec as P

D = 7168
FF = 2048


EPS = 1e-06
ROUTE_SCALE = 2.5


def from_partner(x, axis, apart):
    return lax.ppermute(x, axis, [(i, i ^ 1 << apart) for i in range(lax.axis_size(axis))])


def from_behind(block, axis, distance):
    devices = range(lax.axis_size(axis))
    route = [((i - distance) % len(devices), i) for i in devices]
    return lax.ppermute(block, axis, route)


def moe_layer(
    carried,
    route_ids,
    route_scores,
    section_gain,
    w_project,
    w_extrap,
    expert_count,
    capacity,
    col_bits,
    bit_order,
    my_index,
):
    lead_count, row_count, col_count = carried.shape
    pick_count = route_ids.shape[2]
    values = carried.astype(jnp.float32)
    squares = jnp.sum(values * values, axis=2)
    prepared = (values * section_gain).astype(jnp.bfloat16)
    flat_route = route_ids.reshape(lead_count, row_count * pick_count)
    one_hot = (flat_route[:, :, None] == jnp.arange(expert_count, dtype=jnp.int32)).astype(
        jnp.int32
    )
    position = jnp.sum((jnp.cumsum(one_hot, axis=1) - one_hot) * one_hot, axis=2)
    slot_of = flat_route * capacity + position
    slot_ids = jnp.arange(expert_count * capacity, dtype=jnp.int32)
    chosen = (slot_of.reshape(lead_count, row_count, pick_count)[:, :, :, None] == slot_ids).astype(
        jnp.float32
    )
    spread = jnp.sum(chosen, axis=2)
    buffer = jnp.einsum(
        "nrs,nrc->nsc", spread.astype(jnp.bfloat16), prepared, preferred_element_type=jnp.float32
    ).astype(jnp.bfloat16)
    slot_squares = jnp.einsum("nrs,nr->ns", spread, squares, precision=lax.Precision.HIGHEST)
    buffer = buffer.reshape(lead_count, expert_count, capacity, col_count)
    slot_squares = slot_squares.reshape(lead_count, expert_count, capacity)
    arrived, arrived_squares = (
        lax.all_to_all(buffer, "expert", split_axis=1, concat_axis=1, tiled=True),
        lax.all_to_all(
            slot_squares.astype(jnp.bfloat16), "expert", split_axis=1, concat_axis=1, tiled=True
        ).astype(slot_squares.dtype),
    )
    slot_total = lead_count * expert_count * capacity
    rows_here = arrived.reshape(slot_total, col_count)
    sum_squares = arrived_squares.reshape(slot_total)
    for bit_index in col_bits:
        bit_side = my_index >> bit_index & 1
        got_rows, got_squares = (
            from_partner(rows_here, "pipe", bit_index),
            from_partner(sum_squares.astype(jnp.bfloat16), "pipe", bit_index).astype(
                sum_squares.dtype
            ),
        )
        rows_here = jnp.where(
            bit_side == 0,
            jnp.concatenate([rows_here, got_rows], 1),
            jnp.concatenate([got_rows, rows_here], 1),
        )
        sum_squares = sum_squares + got_squares
    partial_value = jnp.dot(rows_here, w_project, preferred_element_type=jnp.float32)
    current = partial_value.reshape(slot_total, 2, -1)
    for bit_index in bit_order:
        half_size = current.shape[2] // 2
        bit_side = my_index >> bit_index & 1
        kept_half = lax.dynamic_slice_in_dim(current, bit_side * half_size, half_size, 2)
        sent_half = lax.dynamic_slice_in_dim(current, (1 - bit_side) * half_size, half_size, 2)
        got_half, got_squares = (
            from_partner(sent_half.astype(jnp.bfloat16), "pipe", bit_index).astype(sent_half.dtype),
            from_partner(sum_squares.astype(jnp.bfloat16), "pipe", bit_index).astype(
                sum_squares.dtype
            ),
        )
        current = kept_half + got_half
        sum_squares = sum_squares + got_squares
    scaling = lax.rsqrt(sum_squares / D + EPS)[:, None]
    activated = (jax.nn.silu(current[:, 0] * scaling) * (current[:, 1] * scaling)).astype(
        jnp.bfloat16
    )
    for bit_index in reversed(bit_order):
        bit_side = my_index >> bit_index & 1
        got_piece = from_partner(activated, "pipe", bit_index)
        activated = jnp.where(
            bit_side == 0,
            jnp.concatenate([activated, got_piece], 1),
            jnp.concatenate([got_piece, activated], 1),
        )
    out_partial = lax.dot_general(
        activated, w_extrap, (((1,), (1,)), ((), ())), preferred_element_type=jnp.float32
    )
    for bit_index in reversed(col_bits):
        half_size = out_partial.shape[1] // 2
        bit_side = my_index >> bit_index & 1
        kept_part = lax.dynamic_slice_in_dim(out_partial, bit_side * half_size, half_size, 1)
        sent_part = lax.dynamic_slice_in_dim(out_partial, (1 - bit_side) * half_size, half_size, 1)
        got_part = from_partner(sent_part.astype(jnp.bfloat16), "pipe", bit_index).astype(
            sent_part.dtype
        )
        out_partial = kept_part + got_part
    expert_out = out_partial.astype(jnp.bfloat16).reshape(
        lead_count, expert_count, capacity, col_count
    )
    returned = lax.all_to_all(expert_out, "expert", split_axis=1, concat_axis=1, tiled=True)
    returned = returned.reshape(lead_count, expert_count * capacity, col_count)
    gathered = jnp.take_along_axis(returned, slot_of[:, :, None], axis=1)
    mixing = ROUTE_SCALE * route_scores / jnp.sum(route_scores, axis=2, keepdims=True)
    mixed = jnp.sum(
        mixing[..., None]
        * gathered.astype(jnp.float32).reshape(lead_count, row_count, pick_count, col_count),
        axis=2,
    )
    return (values + mixed).astype(jnp.bfloat16)


def body(flowing, norm_gain, gate_up, down_proj, down_step, step_rate, routes, scores):
    shards = lax.axis_size("pipe") // step_rate.shape[1]
    bit_count = shards.bit_length() - 1
    hidden_groups = 2 * FF // gate_up.shape[3]
    col_count_bits = hidden_groups.bit_length() - 1
    my_index = lax.axis_index("pipe")
    section_index = my_index // shards
    expert_count = lax.axis_size("expert")
    row_count = flowing.shape[1]
    pick_count = routes.shape[-1]
    capacity = row_count * pick_count // expert_count + 2
    factor = lax.dynamic_index_in_dim(step_rate[0], section_index, 0, keepdims=False)
    w_project = gate_up[0, 0]
    w_extrap = (
        down_proj[0, 0].astype(jnp.float32) + factor * down_step[0, 0].astype(jnp.float32)
    ).astype(jnp.bfloat16)
    route_here = lax.dynamic_index_in_dim(routes, section_index, 1, keepdims=False)
    score_here = lax.dynamic_index_in_dim(scores, section_index, 1, keepdims=False)
    col_bits = list(range(col_count_bits))
    bit_order = list(range(bit_count - 1, col_count_bits - 1, -1))
    tick_count = routes.shape[0]
    carried = flowing
    for tick_index in range(tick_count):
        route_now = route_here[tick_index]
        score_now = score_here[tick_index]
        layer_out = moe_layer(
            carried,
            route_now,
            score_now,
            norm_gain,
            w_project,
            w_extrap,
            expert_count,
            capacity,
            col_bits,
            bit_order,
            my_index,
        )
        if tick_index + 1 < tick_count:
            upward = from_behind(layer_out[0], "pipe", shards)
            downward = from_behind(layer_out[1], "pipe", -shards)
            layer_out = jnp.stack([upward, downward])
        carried = layer_out
    return carried


def solution(mesh):
    placed = (
        P(None, "expert", "pipe"),
        P("pipe"),
        P("expert", "pipe", None, None),
        P("expert", "pipe", None, None),
        P("expert", "pipe", None, None),
        P("expert", None),
        P(None, None, None, "expert", None),
        P(None, None, None, "expert", None),
    )
    return jax.shard_map(
        body, mesh=mesh, in_specs=placed, out_specs=P(None, "expert", "pipe"), check_vma=False
    )
```

profile of v0, /device:TPU:1, one launch (start us, length us, event | category | flops | bytes accessed | tf_op | source)
XLA Modules:
  0.0 424.4 jit_solution(3869278717508219462)
XLA Ops:
  1.1 1.2 reduce-window.14
  5.1 8.5 %all-to-all-start = ((bf16[2,12,18,224]{3,0,2,1:T(2,128)(2,1)}), bf16[2,12,18,224]{3,0,2,1:T(2,128)(2,1)S(1)}, u32[]{:S(2)}, u32[]{:S(2)}) async-start(bf16[2,12,18,224]{3,0,2,1:T(2,128)(2,1)} %bitcast.5), calls=%async_computation | async-start | bytes 442368 | tf_op jit(solution)/shard_map/all_to_all | solution.py:60
  13.7 7.1 %all-to-all-done = bf16[2,12,18,224]{3,0,2,1:T(2,128)(2,1)S(1)} async-done(((bf16[2,12,18,224]{3,0,2,1:T(2,128)(2,1)}), bf16[2,12,18,224]{3,0,2,1:T(2,128)(2,1)S(1)}, u32[]{:S(2)}, u32[]{:S(2)}) %all-to-all-start) | async-done | bytes 193568 | tf_op jit(solution)/shard_map/all_to_all | solution.py:60
  21.0 8.5 %collective-permute-start = (bf16[432,224]{1,0:T(8,128)(2,1)S(1)}, bf16[432,224]{1,0:T(8,128)(2,1)S(1)}, u32[]{:S(2)}, u32[]{:S(2)}) collective-permute-start(bf16[432,224]{1,0:T(8,128)(2,1)S(1)} %reshape.185), channel_id=1, source_target_pairs={{0,12},{12,0},{24,36},{36,24},{48,60},{60,48},{72,84},{84,72},{96,... | collective-permute-start | bytes 580616 | tf_op jit(solution)/shard_map/ppermute | solution.py:15
  30.5 3.5 all-to-all-start.1
  34.3 5.7 %collective-permute-start.1 = (bf16[432,448]{1,0:T(8,128)(2,1)S(1)}, bf16[432,448]{1,0:T(8,128)(2,1)S(1)}, u32[]{:S(2)}, u32[]{:S(2)}) collective-permute-start(bf16[432,448]{1,0:T(8,128)(2,1)S(1)} %maximum_select_fusion.2), channel_id=1, source_target_pairs={{0,24},{12,36},{24,0},{36,12},{48,72},{60,84},{72,48},{84,60},{96,... | collective-permute-start | bytes 1161224 | tf_op jit(solution)/shard_map/ppermute | solution.py:15
  40.2 2.7 collective-permute-start.5
  42.9 2.5 copy.80
  45.4 6.9 %collective-permute-start.6 = (bf16[432]{0:T(512)(128)(2,1)S(1)}, bf16[432]{0:T(512)(128)(2,1)S(1)}, u32[]{:S(2)}, u32[]{:S(2)}) collective-permute-start(bf16[432]{0:T(512)(128)(2,1)S(1)} %fusion.59), channel_id=1, source_target_pairs={{0,24},{12,36},{24,0},{36,12},{48,72},{60,84},{72,48},{84,60},{96,... | collective-permute-start | bytes 2600 | tf_op jit(solution)/shard_map/ppermute | solution.py:15
  52.3 17.2 %collective-permute-done.1 = bf16[432,448]{1,0:T(8,128)(2,1)S(1)} collective-permute-done((bf16[432,448]{1,0:T(8,128)(2,1)S(1)}, bf16[432,448]{1,0:T(8,128)(2,1)S(1)}, u32[]{:S(2)}, u32[]{:S(2)}) %collective-permute-start.1) | collective-permute-done | bytes 387104 | tf_op jit(solution)/shard_map/ppermute | solution.py:15
  69.6 2.7 fusion.2
  72.3 4.2 collective-permute-start.2
  76.6 2.0 collective-permute-start.7
  78.8 17.0 %collective-permute-done.7 = bf16[432]{0:T(512)(128)(2,1)S(1)} collective-permute-done((bf16[432]{0:T(512)(128)(2,1)S(1)}, bf16[432]{0:T(512)(128)(2,1)S(1)}, u32[]{:S(2)}, u32[]{:S(2)}) %collective-permute-start.7) | collective-permute-done | bytes 896 | tf_op jit(solution)/shard_map/ppermute | solution.py:15
  95.8 3.2 collective-permute-start.8
  99.2 2.0 collective-permute-start.3
  101.3 10.9 %collective-permute-start.9 = (bf16[432]{0:T(512)(128)(2,1)S(1)}, bf16[432]{0:T(512)(128)(2,1)S(1)}, u32[]{:S(2)}, u32[]{:S(2)}) collective-permute-start(bf16[432]{0:T(512)(128)(2,1)S(1)} %fusion.65), channel_id=1, source_target_pairs={{0,48},{12,60},{24,72},{36,84},{48,0},{60,12},{72,24},{84,36},{96,... | collective-permute-start | bytes 2600 | tf_op jit(solution)/shard_map/ppermute | solution.py:15
  112.4 6.2 %collective-permute-start.4 = (bf16[432,2,64]{2,0,1:T(8,128)(2,1)S(1)}, bf16[432,2,64]{2,0,1:T(8,128)(2,1)S(1)}, u32[]{:S(2)}, u32[]{:S(2)}) collective-permute-start(bf16[432,2,64]{2,0,1:T(8,128)(2,1)S(1)} %dynamic-slice_convert_fusion.8), channel_id=1, source_target_pairs={{0,48},{12,60},{24,72},{36,84},{48,0},{60,12},{72,24},{84,36},{96,... | collective-permute-start | bytes 331784 | tf_op jit(solution)/shard_map/ppermute | solution.py:15
  118.6 14.2 %collective-permute-done.4 = bf16[432,2,64]{2,0,1:T(8,128)(2,1)S(1)} collective-permute-done((bf16[432,2,64]{2,0,1:T(8,128)(2,1)S(1)}, bf16[432,2,64]{2,0,1:T(8,128)(2,1)S(1)}, u32[]{:S(2)}, u32[]{:S(2)}) %collective-permute-start.4) | collective-permute-done | bytes 110624 | tf_op jit(solution)/shard_map/ppermute | solution.py:15
  133.1 7.7 %collective-permute-start.10 = (bf16[432,64]{1,0:T(8,128)(2,1)S(1)}, bf16[432,64]{1,0:T(8,128)(2,1)S(1)}, u32[]{:S(2)}, u32[]{:S(2)}) collective-permute-start(bf16[432,64]{1,0:T(8,128)(2,1)S(1)} %fusion.41), channel_id=1, source_target_pairs={{0,48},{12,60},{24,72},{36,84},{48,0},{60,12},{72,24},{84,36},{96,... | collective-permute-start | bytes 165896 | tf_op jit(solution)/shard_map/ppermute | solution.py:15
  141.0 3.9 collective-permute-done.10
  145.1 3.7 collective-permute-start.11
  149.5 1.4 collective-permute-done.11
  151.0 6.2 %collective-permute-start.12 = (bf16[432,256]{1,0:T(8,128)(2,1)S(1)}, bf16[432,256]{1,0:T(8,128)(2,1)S(1)}, u32[]{:S(2)}, u32[]{:S(2)}) collective-permute-start(bf16[432,256]{1,0:T(8,128)(2,1)S(1)} %maximum_select_fusion.8), channel_id=1, source_target_pairs={{0,192},{12,204},{24,216},{36,228},{48,240},{60,252},{72,264},{84,... | collective-permute-start | bytes 663560 | tf_op jit(solution)/shard_map/ppermute | solution.py:15
  158.8 8.0 %collective-permute-done.12 = bf16[432,256]{1,0:T(8,128)(2,1)S(1)} collective-permute-done((bf16[432,256]{1,0:T(8,128)(2,1)S(1)}, bf16[432,256]{1,0:T(8,128)(2,1)S(1)}, u32[]{:S(2)}, u32[]{:S(2)}) %collective-permute-start.12) | collective-permute-done | bytes 221216 | tf_op jit(solution)/shard_map/ppermute | solution.py:15
  166.7 2.6 fusion.19
  169.5 1.9 collective-permute-start.13
  171.8 18.9 %collective-permute-done.13 = bf16[432,448]{1,0:T(8,128)(2,1)S(1)} collective-permute-done((bf16[432,448]{1,0:T(8,128)(2,1)S(1)}, bf16[432,448]{1,0:T(8,128)(2,1)S(1)}, u32[]{:S(2)}, u32[]{:S(2)}) %collective-permute-start.13) | collective-permute-done | bytes 387104 | tf_op jit(solution)/shard_map/ppermute | solution.py:15
  191.1 2.4 collective-permute-start.14
  195.7 3.9 all-to-all-start.2
  200.0 7.2 %all-to-all-done.2 = bf16[2,12,18,224]{3,0,2,1:T(2,128)(2,1)S(1)} async-done(((bf16[2,12,18,224]{3,0,2,1:T(2,128)(2,1)}), bf16[2,12,18,224]{3,0,2,1:T(2,128)(2,1)S(1)}, u32[]{:S(2)}, u32[]{:S(2)}) %all-to-all-start.2) | async-done | bytes 193568 | tf_op jit(solution)/shard_map/all_to_all | solution.py:124
  207.3 3.2 gather_fusion
  211.4 5.9 %collective-permute-start.15 = (bf16[96,224]{1,0:T(8,128)(2,1)S(1)}, bf16[96,224]{1,0:T(8,128)(2,1)S(1)}, u32[]{:S(2)}, u32[]{:S(2)}) collective-permute-start(bf16[96,224]{1,0:T(8,128)(2,1)S(1)} %get-tuple-element.8), channel_id=1, source_target_pairs={{384,0},{396,12},{408,24},{420,36},{432,48},{444,60},{456,72},{468... | collective-permute-start | bytes 129032 | tf_op jit(solution)/shard_map/ppermute | solution.py:21
  217.4 3.4 collective-permute-start.16
  221.0 5.3 %collective-permute-done.16 = bf16[96,224]{1,0:T(8,128)(2,1)S(1)} collective-permute-done((bf16[96,224]{1,0:T(8,128)(2,1)S(1)}, bf16[96,224]{1,0:T(8,128)(2,1)S(1)}, u32[]{:S(2)}, u32[]{:S(2)}) %collective-permute-start.16) | collective-permute-done | bytes 43040 | tf_op jit(solution)/shard_map/ppermute | solution.py:21
  226.7 10.1 %all_to_all.30 = bf16[2,12,18,224]{3,0,2,1:T(2,128)(2,1)S(1)} all-to-all(bf16[2,12,18,224]{3,0,2,1:T(2,128)(2,1)S(1)} %bitcast.128), channel_id=1, replica_groups=mesh['pipe'=64,'expert'=12] {'expert'}, dimensions={1} | all-to-all | bytes 387072 | tf_op jit(solution)/shard_map/all_to_all | solution.py:60
  236.9 6.1 %collective-permute-start.17 = (bf16[432,224]{1,0:T(8,128)(2,1)S(1)}, bf16[432,224]{1,0:T(8,128)(2,1)S(1)}, u32[]{:S(2)}, u32[]{:S(2)}) collective-permute-start(bf16[432,224]{1,0:T(8,128)(2,1)S(1)} %reshape.195), channel_id=1, source_target_pairs={{0,12},{12,0},{24,36},{36,24},{48,60},{60,48},{72,84},{84,72},{96,... | collective-permute-start | bytes 580616 | tf_op jit(solution)/shard_map/ppermute | solution.py:15
  244.4 8.1 %collective-permute-start.18 = (bf16[432,448]{1,0:T(8,128)(2,1)S(1)}, bf16[432,448]{1,0:T(8,128)(2,1)S(1)}, u32[]{:S(2)}, u32[]{:S(2)}) collective-permute-start(bf16[432,448]{1,0:T(8,128)(2,1)S(1)} %maximum_select_fusion.5), channel_id=1, source_target_pairs={{0,24},{12,36},{24,0},{36,12},{48,72},{60,84},{72,48},{84,60},{96,... | collective-permute-start | bytes 1161224 | tf_op jit(solution)/shard_map/ppermute | solution.py:15
  252.8 9.0 %all_to_all.31 = bf16[2,12,18]{2,0,1:T(2,128)(2,1)S(1)} all-to-all(bf16[2,12,18]{2,0,1:T(2,128)(2,1)S(1)} %copy.72), channel_id=1, replica_groups=mesh['pipe'=64,'expert'=12] {'expert'}, dimensions={1} | all-to-all | bytes 1728 | tf_op jit(solution)/shard_map/all_to_all | solution.py:61
  262.0 3.1 collective-permute-start.22
  265.9 12.7 %collective-permute-start.23 = (bf16[432]{0:T(512)(128)(2,1)S(1)}, bf16[432]{0:T(512)(128)(2,1)S(1)}, u32[]{:S(2)}, u32[]{:S(2)}) collective-permute-start(bf16[432]{0:T(512)(128)(2,1)S(1)} %fusion.60), channel_id=1, source_target_pairs={{0,24},{12,36},{24,0},{36,12},{48,72},{60,84},{72,48},{84,60},{96,... | collective-permute-start | bytes 2600 | tf_op jit(solution)/shard_map/ppermute | solution.py:15
  278.6 3.4 collective-permute-done.18
  282.0 1.2 fusion.10
  283.3 1.9 collective-permute-start.19
  285.2 4.3 %collective-permute-start.24 = (bf16[432]{0:T(512)(128)(2,1)S(1)}, bf16[432]{0:T(512)(128)(2,1)S(1)}, u32[]{:S(2)}, u32[]{:S(2)}) collective-permute-start(bf16[432]{0:T(512)(128)(2,1)S(1)} %fusion.73), channel_id=1, source_target_pairs={{0,192},{12,204},{24,216},{36,228},{48,240},{60,252},{72,264},{84,... | collective-permute-start | bytes 2600 | tf_op jit(solution)/shard_map/ppermute | solution.py:15
  289.5 16.4 %collective-permute-done.24 = bf16[432]{0:T(512)(128)(2,1)S(1)} collective-permute-done((bf16[432]{0:T(512)(128)(2,1)S(1)}, bf16[432]{0:T(512)(128)(2,1)S(1)}, u32[]{:S(2)}, u32[]{:S(2)}) %collective-permute-start.24) | collective-permute-done | bytes 896 | tf_op jit(solution)/shard_map/ppermute | solution.py:15
  305.9 1.9 collective-permute-start.25
  308.0 3.4 collective-permute-start.20
  311.4 9.9 %collective-permute-start.26 = (bf16[432]{0:T(512)(128)(2,1)S(1)}, bf16[432]{0:T(512)(128)(2,1)S(1)}, u32[]{:S(2)}, u32[]{:S(2)}) collective-permute-start(bf16[432]{0:T(512)(128)(2,1)S(1)} %fusion.66), channel_id=1, source_target_pairs={{0,48},{12,60},{24,72},{36,84},{48,0},{60,12},{72,24},{84,36},{96,... | collective-permute-start | bytes 2600 | tf_op jit(solution)/shard_map/ppermute | solution.py:15
  321.5 4.8 %collective-permute-start.21 = (bf16[432,2,64]{2,0,1:T(8,128)(2,1)S(1)}, bf16[432,2,64]{2,0,1:T(8,128)(2,1)S(1)}, u32[]{:S(2)}, u32[]{:S(2)}) collective-permute-start(bf16[432,2,64]{2,0,1:T(8,128)(2,1)S(1)} %dynamic-slice_convert_fusion.5), channel_id=1, source_target_pairs={{0,48},{12,60},{24,72},{36,84},{48,0},{60,12},{72,24},{84,36},{96,... | collective-permute-start | bytes 331784 | tf_op jit(solution)/shard_map/ppermute | solution.py:15
  326.3 14.7 %collective-permute-done.21 = bf16[432,2,64]{2,0,1:T(8,128)(2,1)S(1)} collective-permute-done((bf16[432,2,64]{2,0,1:T(8,128)(2,1)S(1)}, bf16[432,2,64]{2,0,1:T(8,128)(2,1)S(1)}, u32[]{:S(2)}, u32[]{:S(2)}) %collective-permute-start.21) | collective-permute-done | bytes 110624 | tf_op jit(solution)/shard_map/ppermute | solution.py:15
  341.4 6.5 %collective-permute-start.27 = (bf16[432,64]{1,0:T(8,128)(2,1)S(1)}, bf16[432,64]{1,0:T(8,128)(2,1)S(1)}, u32[]{:S(2)}, u32[]{:S(2)}) collective-permute-start(bf16[432,64]{1,0:T(8,128)(2,1)S(1)} %fusion.37), channel_id=1, source_target_pairs={{0,48},{12,60},{24,72},{36,84},{48,0},{60,12},{72,24},{84,36},{96,... | collective-permute-start | bytes 165896 | tf_op jit(solution)/shard_map/ppermute | solution.py:15
  347.9 5.7 %collective-permute-done.27 = bf16[432,64]{1,0:T(8,128)(2,1)S(1)} collective-permute-done((bf16[432,64]{1,0:T(8,128)(2,1)S(1)}, bf16[432,64]{1,0:T(8,128)(2,1)S(1)}, u32[]{:S(2)}, u32[]{:S(2)}) %collective-permute-start.27) | collective-permute-done | bytes 55328 | tf_op jit(solution)/shard_map/ppermute | solution.py:15
  353.8 2.7 collective-permute-start.28
  356.5 2.7 collective-permute-done.28
  359.3 4.6 %collective-permute-start.29 = (bf16[432,256]{1,0:T(8,128)(2,1)S(1)}, bf16[432,256]{1,0:T(8,128)(2,1)S(1)}, u32[]{:S(2)}, u32[]{:S(2)}) collective-permute-start(bf16[432,256]{1,0:T(8,128)(2,1)S(1)} %maximum_select_fusion.9), channel_id=1, source_target_pairs={{0,192},{12,204},{24,216},{36,228},{48,240},{60,252},{72,264},{84,... | collective-permute-start | bytes 663560 | tf_op jit(solution)/shard_map/ppermute | solution.py:15
  363.9 10.4 %collective-permute-done.29 = bf16[432,256]{1,0:T(8,128)(2,1)S(1)} collective-permute-done((bf16[432,256]{1,0:T(8,128)(2,1)S(1)}, bf16[432,256]{1,0:T(8,128)(2,1)S(1)}, u32[]{:S(2)}, u32[]{:S(2)}) %collective-permute-start.29) | collective-permute-done | bytes 221216 | tf_op jit(solution)/shard_map/ppermute | solution.py:15
  374.3 1.4 fusion.25
  375.9 3.9 collective-permute-start.30
  379.7 23.4 %collective-permute-done.30 = bf16[432,448]{1,0:T(8,128)(2,1)S(1)} collective-permute-done((bf16[432,448]{1,0:T(8,128)(2,1)S(1)}, bf16[432,448]{1,0:T(8,128)(2,1)S(1)}, u32[]{:S(2)}, u32[]{:S(2)}) %collective-permute-start.30) | collective-permute-done | bytes 387104 | tf_op jit(solution)/shard_map/ppermute | solution.py:15
  403.6 2.4 collective-permute-start.31
  408.3 3.5 all-to-all-start.5
  412.1 7.5 %all-to-all-done.5 = bf16[2,12,18,224]{3,0,2,1:T(2,128)(2,1)S(1)} async-done(((bf16[2,12,18,224]{3,0,2,1:T(2,128)(2,1)}), bf16[2,12,18,224]{3,0,2,1:T(2,128)(2,1)S(1)}, u32[]{:S(2)}, u32[]{:S(2)}) %all-to-all-start.5) | async-done | bytes 193568 | tf_op jit(solution)/shard_map/all_to_all | solution.py:124
  419.6 3.2 gather_fusion.1
  (161 shorter events, 22.6 us)
Async XLA Ops:
  0.0 148.9 %copy-start = (f32[1,2]{1,0:T(1,128)S(1)}, f32[1,2]{1,0:T(1,128)}, u32[]{:S(2)}) copy-start(f32[1,2]{1,0:T(1,128)} %param.15) | copy-start | bytes 28
  0.0 13.6 %copy-start.3 = (bf16[2,96,224]{2,1,0:T(8,128)(2,1)S(1)}, bf16[2,96,224]{2,1,0:T(8,128)(2,1)}, u32[]{:S(2)}) copy-start(bf16[2,96,224]{2,1,0:T(8,128)(2,1)} %param.10) | copy-start | bytes 258052
  4.3 38.7 %copy-start.1 = (bf16[1,1,896,1024]{3,2,1,0:T(8,128)(2,1)S(1)}, bf16[1,1,896,1024]{3,2,1,0:T(8,128)(2,1)}, u32[]{:S(2)}) copy-start(bf16[1,1,896,1024]{3,2,1,0:T(8,128)(2,1)} %param.12) | copy-start | bytes 5505028
  5.1 15.8 %all-to-all-start = ((bf16[2,12,18,224]{3,0,2,1:T(2,128)(2,1)}), bf16[2,12,18,224]{3,0,2,1:T(2,128)(2,1)S(1)}, u32[]{:S(2)}, u32[]{:S(2)}) async-start(bf16[2,12,18,224]{3,0,2,1:T(2,128)(2,1)} %bitcast.5), calls=%async_computation | async-start | bytes 442368 | tf_op jit(solution)/shard_map/all_to_all | solution.py:60
  21.0 12.9 %collective-permute-start = (bf16[432,224]{1,0:T(8,128)(2,1)S(1)}, bf16[432,224]{1,0:T(8,128)(2,1)S(1)}, u32[]{:S(2)}, u32[]{:S(2)}) collective-permute-start(bf16[432,224]{1,0:T(8,128)(2,1)S(1)} %reshape.185), channel_id=1, source_target_pairs={{0,12},{12,0},{24,36},{36,24},{48,60},{60,48},{72,84},{84,72},{96,... | collective-permute-start | bytes 580616 | tf_op jit(solution)/shard_map/ppermute | solution.py:15
  30.5 9.6 %all-to-all-start.1 = ((bf16[2,12,18]{2,0,1:T(2,128)(2,1)}), bf16[2,12,18]{2,0,1:T(2,128)(2,1)S(1)}, u32[]{:S(2)}, u32[]{:S(2)}) async-start(bf16[2,12,18]{2,0,1:T(2,128)(2,1)} %copy.61), calls=%async_computation.1 | async-start | bytes 12288 | tf_op jit(solution)/shard_map/all_to_all | solution.py:61
  34.3 35.2 %collective-permute-start.1 = (bf16[432,448]{1,0:T(8,128)(2,1)S(1)}, bf16[432,448]{1,0:T(8,128)(2,1)S(1)}, u32[]{:S(2)}, u32[]{:S(2)}) collective-permute-start(bf16[432,448]{1,0:T(8,128)(2,1)S(1)} %maximum_select_fusion.2), channel_id=1, source_target_pairs={{0,24},{12,36},{24,0},{36,12},{48,72},{60,84},{72,48},{84,60},{96,... | collective-permute-start | bytes 1161224 | tf_op jit(solution)/shard_map/ppermute | solution.py:15
  40.2 5.2 %collective-permute-start.5 = (bf16[432]{0:T(512)(128)(2,1)S(1)}, bf16[432]{0:T(512)(128)(2,1)S(1)}, u32[]{:S(2)}, u32[]{:S(2)}) collective-permute-start(bf16[432]{0:T(512)(128)(2,1)S(1)} %reshape.186), channel_id=1, source_target_pairs={{0,12},{12,0},{24,36},{36,24},{48,60},{60,48},{72,84},{84,72},{96,... | collective-permute-start | bytes 2600 | tf_op jit(solution)/shard_map/ppermute | solution.py:15
  45.4 31.1 %collective-permute-start.6 = (bf16[432]{0:T(512)(128)(2,1)S(1)}, bf16[432]{0:T(512)(128)(2,1)S(1)}, u32[]{:S(2)}, u32[]{:S(2)}) collective-permute-start(bf16[432]{0:T(512)(128)(2,1)S(1)} %fusion.59), channel_id=1, source_target_pairs={{0,24},{12,36},{24,0},{36,12},{48,72},{60,84},{72,48},{84,60},{96,... | collective-permute-start | bytes 2600 | tf_op jit(solution)/shard_map/ppermute | solution.py:15
  72.3 26.7 %collective-permute-start.2 = (bf16[432,2,256]{2,0,1:T(8,128)(2,1)S(1)}, bf16[432,2,256]{2,0,1:T(8,128)(2,1)S(1)}, u32[]{:S(2)}, u32[]{:S(2)}) collective-permute-start(bf16[432,2,256]{2,0,1:T(8,128)(2,1)S(1)} %dynamic-slice_convert_fusion.3), channel_id=1, source_target_pairs={{0,192},{12,204},{24,216},{36,228},{48,240},{60,252},{72,264},{84,... | collective-permute-start | bytes 1327112 | tf_op jit(solution)/shard_map/ppermute | solution.py:15
  76.6 19.2 %collective-permute-start.7 = (bf16[432]{0:T(512)(128)(2,1)S(1)}, bf16[432]{0:T(512)(128)(2,1)S(1)}, u32[]{:S(2)}, u32[]{:S(2)}) collective-permute-start(bf16[432]{0:T(512)(128)(2,1)S(1)} %fusion.72), channel_id=1, source_target_pairs={{0,192},{12,204},{24,216},{36,228},{48,240},{60,252},{72,264},{84,... | collective-permute-start | bytes 2600 | tf_op jit(solution)/shard_map/ppermute | solution.py:15
  95.8 5.5 %collective-permute-start.8 = (bf16[432]{0:T(512)(128)(2,1)S(1)}, bf16[432]{0:T(512)(128)(2,1)S(1)}, u32[]{:S(2)}, u32[]{:S(2)}) collective-permute-start(bf16[432]{0:T(512)(128)(2,1)S(1)} %fusion.62), channel_id=1, source_target_pairs={{0,96},{12,108},{24,120},{36,132},{48,144},{60,156},{72,168},{84,1... | collective-permute-start | bytes 2600 | tf_op jit(solution)/shard_map/ppermute | solution.py:15
  99.2 12.9 %collective-permute-start.3 = (bf16[432,2,128]{2,0,1:T(8,128)(2,1)S(1)}, bf16[432,2,128]{2,0,1:T(8,128)(2,1)S(1)}, u32[]{:S(2)}, u32[]{:S(2)}) collective-permute-start(bf16[432,2,128]{2,0,1:T(8,128)(2,1)S(1)} %dynamic-slice_convert_fusion.9), channel_id=1, source_target_pairs={{0,96},{12,108},{24,120},{36,132},{48,144},{60,156},{72,168},{84,1... | collective-permute-start | bytes 663560 | tf_op jit(solution)/shard_map/ppermute | solution.py:15
  101.3 17.3 %collective-permute-start.9 = (bf16[432]{0:T(512)(128)(2,1)S(1)}, bf16[432]{0:T(512)(128)(2,1)S(1)}, u32[]{:S(2)}, u32[]{:S(2)}) collective-permute-start(bf16[432]{0:T(512)(128)(2,1)S(1)} %fusion.65), channel_id=1, source_target_pairs={{0,48},{12,60},{24,72},{36,84},{48,0},{60,12},{72,24},{84,36},{96,... | collective-permute-start | bytes 2600 | tf_op jit(solution)/shard_map/ppermute | solution.py:15
  112.2 54.5 %copy-start.6 = (bf16[1,1,896,512]{3,2,1,0:T(8,128)(2,1)S(1)}, bf16[1,1,896,512]{3,2,1,0:T(8,128)(2,1)}, u32[]{:S(2)}) copy-start(bf16[1,1,896,512]{3,2,1,0:T(8,128)(2,1)} %param.14) | copy-start | bytes 2752516
  112.4 20.4 %collective-permute-start.4 = (bf16[432,2,64]{2,0,1:T(8,128)(2,1)S(1)}, bf16[432,2,64]{2,0,1:T(8,128)(2,1)S(1)}, u32[]{:S(2)}, u32[]{:S(2)}) collective-permute-start(bf16[432,2,64]{2,0,1:T(8,128)(2,1)S(1)} %dynamic-slice_convert_fusion.8), channel_id=1, source_target_pairs={{0,48},{12,60},{24,72},{36,84},{48,0},{60,12},{72,24},{84,36},{96,... | collective-permute-start | bytes 331784 | tf_op jit(solution)/shard_map/ppermute | solution.py:15
  133.1 11.8 %collective-permute-start.10 = (bf16[432,64]{1,0:T(8,128)(2,1)S(1)}, bf16[432,64]{1,0:T(8,128)(2,1)S(1)}, u32[]{:S(2)}, u32[]{:S(2)}) collective-permute-start(bf16[432,64]{1,0:T(8,128)(2,1)S(1)} %fusion.41), channel_id=1, source_target_pairs={{0,48},{12,60},{24,72},{36,84},{48,0},{60,12},{72,24},{84,36},{96,... | collective-permute-start | bytes 165896 | tf_op jit(solution)/shard_map/ppermute | solution.py:15
  145.1 5.9 %collective-permute-start.11 = (bf16[432,128]{1,0:T(8,128)(2,1)S(1)}, bf16[432,128]{1,0:T(8,128)(2,1)S(1)}, u32[]{:S(2)}, u32[]{:S(2)}) collective-permute-start(bf16[432,128]{1,0:T(8,128)(2,1)S(1)} %maximum_select_fusion.10), channel_id=1, source_target_pairs={{0,96},{12,108},{24,120},{36,132},{48,144},{60,156},{72,168},{84,1... | collective-permute-start | bytes 331784 | tf_op jit(solution)/shard_map/ppermute | solution.py:15
  151.0 15.7 %collective-permute-start.12 = (bf16[432,256]{1,0:T(8,128)(2,1)S(1)}, bf16[432,256]{1,0:T(8,128)(2,1)S(1)}, u32[]{:S(2)}, u32[]{:S(2)}) collective-permute-start(bf16[432,256]{1,0:T(8,128)(2,1)S(1)} %maximum_select_fusion.8), channel_id=1, source_target_pairs={{0,192},{12,204},{24,216},{36,228},{48,240},{60,252},{72,264},{84,... | collective-permute-start | bytes 663560 | tf_op jit(solution)/shard_map/ppermute | solution.py:15
  166.7 5.0 %copy-start.4 = (f32[2,2,2,96,2]{3,4,2,1,0:T(2,128)S(1)}, f32[2,2,2,96,2]{3,4,2,1,0:T(2,128)}, u32[]{:S(2)}) copy-start(f32[2,2,2,96,2]{3,4,2,1,0:T(2,128)} %param.17) | copy-start | bytes 18436
  169.5 21.1 %collective-permute-start.13 = (bf16[432,448]{1,0:T(8,128)(2,1)S(1)}, bf16[432,448]{1,0:T(8,128)(2,1)S(1)}, u32[]{:S(2)}, u32[]{:S(2)}) collective-permute-start(bf16[432,448]{1,0:T(8,128)(2,1)S(1)} %dynamic-slice_convert_fusion.2), channel_id=1, source_target_pairs={{0,24},{12,36},{24,0},{36,12},{48,72},{60,84},{72,48},{84,60},{96,... | collective-permute-start | bytes 1161224 | tf_op jit(solution)/shard_map/ppermute | solution.py:15
  191.1 3.5 collective-permute-start.14
  195.7 11.5 %all-to-all-start.2 = ((bf16[2,12,18,224]{3,0,2,1:T(2,128)(2,1)}), bf16[2,12,18,224]{3,0,2,1:T(2,128)(2,1)S(1)}, u32[]{:S(2)}, u32[]{:S(2)}) async-start(bf16[2,12,18,224]{3,0,2,1:T(2,128)(2,1)} %copy.63), calls=%async_computation.2 | async-start | bytes 442368 | tf_op jit(solution)/shard_map/all_to_all | solution.py:124
  210.5 15.8 %copy-start.5 = (f32[224]{0:T(256)S(1)}, f32[224]{0:T(256)}, u32[]{:S(2)}) copy-start(f32[224]{0:T(256)} %param.11) | copy-start | bytes 2692
  211.4 9.5 %collective-permute-start.15 = (bf16[96,224]{1,0:T(8,128)(2,1)S(1)}, bf16[96,224]{1,0:T(8,128)(2,1)S(1)}, u32[]{:S(2)}, u32[]{:S(2)}) collective-permute-start(bf16[96,224]{1,0:T(8,128)(2,1)S(1)} %get-tuple-element.8), channel_id=1, source_target_pairs={{384,0},{396,12},{408,24},{420,36},{432,48},{444,60},{456,72},{468... | collective-permute-start | bytes 129032 | tf_op jit(solution)/shard_map/ppermute | solution.py:21
  217.4 8.8 %collective-permute-start.16 = (bf16[96,224]{1,0:T(8,128)(2,1)S(1)}, bf16[96,224]{1,0:T(8,128)(2,1)S(1)}, u32[]{:S(2)}, u32[]{:S(2)}) collective-permute-start(bf16[96,224]{1,0:T(8,128)(2,1)S(1)} %get-tuple-element.9), channel_id=1, source_target_pairs={{384,0},{396,12},{408,24},{420,36},{432,48},{444,60},{456,72},{468... | collective-permute-start | bytes 129032 | tf_op jit(solution)/shard_map/ppermute | solution.py:21
  226.2 55.8 %copy-start.2 = (bf16[1024,896]{1,0:T(8,128)(2,1)S(1)}, bf16[1024,896]{1,0:T(8,128)(2,1)}, u32[]{:S(2)}) copy-start(bf16[1024,896]{1,0:T(8,128)(2,1)} %copy.80) | copy-start | bytes 5505028
  236.9 7.2 %collective-permute-start.17 = (bf16[432,224]{1,0:T(8,128)(2,1)S(1)}, bf16[432,224]{1,0:T(8,128)(2,1)S(1)}, u32[]{:S(2)}, u32[]{:S(2)}) collective-permute-start(bf16[432,224]{1,0:T(8,128)(2,1)S(1)} %reshape.195), channel_id=1, source_target_pairs={{0,12},{12,0},{24,36},{36,24},{48,60},{60,48},{72,84},{84,72},{96,... | collective-permute-start | bytes 580616 | tf_op jit(solution)/shard_map/ppermute | solution.py:15
  244.4 37.6 %collective-permute-start.18 = (bf16[432,448]{1,0:T(8,128)(2,1)S(1)}, bf16[432,448]{1,0:T(8,128)(2,1)S(1)}, u32[]{:S(2)}, u32[]{:S(2)}) collective-permute-start(bf16[432,448]{1,0:T(8,128)(2,1)S(1)} %maximum_select_fusion.5), channel_id=1, source_target_pairs={{0,24},{12,36},{24,0},{36,12},{48,72},{60,84},{72,48},{84,60},{96,... | collective-permute-start | bytes 1161224 | tf_op jit(solution)/shard_map/ppermute | solution.py:15
  262.0 3.9 collective-permute-start.22
  265.9 19.3 %collective-permute-start.23 = (bf16[432]{0:T(512)(128)(2,1)S(1)}, bf16[432]{0:T(512)(128)(2,1)S(1)}, u32[]{:S(2)}, u32[]{:S(2)}) collective-permute-start(bf16[432]{0:T(512)(128)(2,1)S(1)} %fusion.60), channel_id=1, source_target_pairs={{0,24},{12,36},{24,0},{36,12},{48,72},{60,84},{72,48},{84,60},{96,... | collective-permute-start | bytes 2600 | tf_op jit(solution)/shard_map/ppermute | solution.py:15
  283.3 24.5 %collective-permute-start.19 = (bf16[432,2,256]{2,0,1:T(8,128)(2,1)S(1)}, bf16[432,2,256]{2,0,1:T(8,128)(2,1)S(1)}, u32[]{:S(2)}, u32[]{:S(2)}) collective-permute-start(bf16[432,2,256]{2,0,1:T(8,128)(2,1)S(1)} %dynamic-slice_convert_fusion.1), channel_id=1, source_target_pairs={{0,192},{12,204},{24,216},{36,228},{48,240},{60,252},{72,264},{84,... | collective-permute-start | bytes 1327112 | tf_op jit(solution)/shard_map/ppermute | solution.py:15
  285.2 20.6 %collective-permute-start.24 = (bf16[432]{0:T(512)(128)(2,1)S(1)}, bf16[432]{0:T(512)(128)(2,1)S(1)}, u32[]{:S(2)}, u32[]{:S(2)}) collective-permute-start(bf16[432]{0:T(512)(128)(2,1)S(1)} %fusion.73), channel_id=1, source_target_pairs={{0,192},{12,204},{24,216},{36,228},{48,240},{60,252},{72,264},{84,... | collective-permute-start | bytes 2600 | tf_op jit(solution)/shard_map/ppermute | solution.py:15
  305.9 5.5 %collective-permute-start.25 = (bf16[432]{0:T(512)(128)(2,1)S(1)}, bf16[432]{0:T(512)(128)(2,1)S(1)}, u32[]{:S(2)}, u32[]{:S(2)}) collective-permute-start(bf16[432]{0:T(512)(128)(2,1)S(1)} %fusion.63), channel_id=1, source_target_pairs={{0,96},{12,108},{24,120},{36,132},{48,144},{60,156},{72,168},{84,1... | collective-permute-start | bytes 2600 | tf_op jit(solution)/shard_map/ppermute | solution.py:15
  308.0 13.3 %collective-permute-start.20 = (bf16[432,2,128]{2,0,1:T(8,128)(2,1)S(1)}, bf16[432,2,128]{2,0,1:T(8,128)(2,1)S(1)}, u32[]{:S(2)}, u32[]{:S(2)}) collective-permute-start(bf16[432,2,128]{2,0,1:T(8,128)(2,1)S(1)} %dynamic-slice_convert_fusion.6), channel_id=1, source_target_pairs={{0,96},{12,108},{24,120},{36,132},{48,144},{60,156},{72,168},{84,1... | collective-permute-start | bytes 663560 | tf_op jit(solution)/shard_map/ppermute | solution.py:15
  311.4 62.9 %copy-start.7 = (bf16[1,1,896,512]{3,2,1,0:T(8,128)(2,1)S(1)}, bf16[1,1,896,512]{3,2,1,0:T(8,128)(2,1)}, u32[]{:S(2)}) copy-start(bf16[1,1,896,512]{3,2,1,0:T(8,128)(2,1)} %param.14) | copy-start | bytes 2752516
  311.4 62.9 %copy-start.8 = (bf16[1,1,896,512]{3,2,1,0:T(8,128)(2,1)S(1)}, bf16[1,1,896,512]{3,2,1,0:T(8,128)(2,1)}, u32[]{:S(2)}) copy-start(bf16[1,1,896,512]{3,2,1,0:T(8,128)(2,1)} %param.13) | copy-start | bytes 2752516
  311.4 14.9 %collective-permute-start.26 = (bf16[432]{0:T(512)(128)(2,1)S(1)}, bf16[432]{0:T(512)(128)(2,1)S(1)}, u32[]{:S(2)}, u32[]{:S(2)}) collective-permute-start(bf16[432]{0:T(512)(128)(2,1)S(1)} %fusion.66), channel_id=1, source_target_pairs={{0,48},{12,60},{24,72},{36,84},{48,0},{60,12},{72,24},{84,36},{96,... | collective-permute-start | bytes 2600 | tf_op jit(solution)/shard_map/ppermute | solution.py:15
  321.5 19.5 %collective-permute-start.21 = (bf16[432,2,64]{2,0,1:T(8,128)(2,1)S(1)}, bf16[432,2,64]{2,0,1:T(8,128)(2,1)S(1)}, u32[]{:S(2)}, u32[]{:S(2)}) collective-permute-start(bf16[432,2,64]{2,0,1:T(8,128)(2,1)S(1)} %dynamic-slice_convert_fusion.5), channel_id=1, source_target_pairs={{0,48},{12,60},{24,72},{36,84},{48,0},{60,12},{72,24},{84,36},{96,... | collective-permute-start | bytes 331784 | tf_op jit(solution)/shard_map/ppermute | solution.py:15
  341.4 12.2 %collective-permute-start.27 = (bf16[432,64]{1,0:T(8,128)(2,1)S(1)}, bf16[432,64]{1,0:T(8,128)(2,1)S(1)}, u32[]{:S(2)}, u32[]{:S(2)}) collective-permute-start(bf16[432,64]{1,0:T(8,128)(2,1)S(1)} %fusion.37), channel_id=1, source_target_pairs={{0,48},{12,60},{24,72},{36,84},{48,0},{60,12},{72,24},{84,36},{96,... | collective-permute-start | bytes 165896 | tf_op jit(solution)/shard_map/ppermute | solution.py:15
  353.8 5.5 %collective-permute-start.28 = (bf16[432,128]{1,0:T(8,128)(2,1)S(1)}, bf16[432,128]{1,0:T(8,128)(2,1)S(1)}, u32[]{:S(2)}, u32[]{:S(2)}) collective-permute-start(bf16[432,128]{1,0:T(8,128)(2,1)S(1)} %maximum_select_fusion.11), channel_id=1, source_target_pairs={{0,96},{12,108},{24,120},{36,132},{48,144},{60,156},{72,168},{84,1... | collective-permute-start | bytes 331784 | tf_op jit(solution)/shard_map/ppermute | solution.py:15
  359.3 15.0 %collective-permute-start.29 = (bf16[432,256]{1,0:T(8,128)(2,1)S(1)}, bf16[432,256]{1,0:T(8,128)(2,1)S(1)}, u32[]{:S(2)}, u32[]{:S(2)}) collective-permute-start(bf16[432,256]{1,0:T(8,128)(2,1)S(1)} %maximum_select_fusion.9), channel_id=1, source_target_pairs={{0,192},{12,204},{24,216},{36,228},{48,240},{60,252},{72,264},{84,... | collective-permute-start | bytes 663560 | tf_op jit(solution)/shard_map/ppermute | solution.py:15
  375.9 27.3 %collective-permute-start.30 = (bf16[432,448]{1,0:T(8,128)(2,1)S(1)}, bf16[432,448]{1,0:T(8,128)(2,1)S(1)}, u32[]{:S(2)}, u32[]{:S(2)}) collective-permute-start(bf16[432,448]{1,0:T(8,128)(2,1)S(1)} %dynamic-slice_convert_fusion), channel_id=1, source_target_pairs={{0,24},{12,36},{24,0},{36,12},{48,72},{60,84},{72,48},{84,60},{96,... | collective-permute-start | bytes 1161224 | tf_op jit(solution)/shard_map/ppermute | solution.py:15
  403.6 3.5 collective-permute-start.31
  408.3 11.3 %all-to-all-start.5 = ((bf16[2,12,18,224]{3,0,2,1:T(2,128)(2,1)}), bf16[2,12,18,224]{3,0,2,1:T(2,128)(2,1)S(1)}, u32[]{:S(2)}, u32[]{:S(2)}) async-start(bf16[2,12,18,224]{3,0,2,1:T(2,128)(2,1)} %copy.74), calls=%async_computation.5 | async-start | bytes 442368 | tf_op jit(solution)/shard_map/all_to_all | solution.py:124
where the time goes:
time: 426 us; the launch traced here: 424 us
  waiting for transfers between devices  188 us (44%)
  starting transfers between devices  179 us (42%)
  blocking collectives  19.1 us (4%)
  local copies, waits for them, and re-layouts  18.4 us (4%)
  matrix products  9.6 us (2%)
  other arithmetic  8.56 us (2%)
    ppermute x30, waiting for transfers between devices, from_partner(): lax.ppermute(x, axis, [(i, i ^ 1 << apart) for i in range(lax.axis_size(a...  161 us
    ppermute x30, starting transfers between devices, from_partner(): lax.ppermute(x, axis, [(i, i ^ 1 << apart) for i in range(lax.axis_size(a...  151 us
    all_to_all x2, waiting for transfers between devices, moe_layer(): lax.all_to_all(expert_out, 'expert', split_axis=1, concat_axis=1, tiled=T...  14.7 us
    all_to_all x1, blocking collectives, moe_layer(): lax.all_to_all(buffer, 'expert', split_axis=1, concat_axis=1, tiled=True)  10.1 us
    ppermute x2, starting transfers between devices, from_behind(): return lax.ppermute(block, axis, route)  9.37 us
    all_to_all x1, blocking collectives, moe_layer(): lax.all_to_all(slot_squares.astype(jnp.bfloat16), 'expert', split_axis=1,...  9 us
  transfers between devices with their start and end apart: 36, of which 22 were waited for; matrix products, arithmetic and copies ran while one was open for 3% of the time, Pallas kernels for 0%

commit v1 on v0

v1 whole, which is shorter than its diff:
```python
import jax
import jax.numpy as jnp
from jax import lax
from jax.experimental import pallas as pl
from jax.experimental.pallas import tpu as pltpu
from jax.sharding import PartitionSpec as P

D = 7168
FF = 2048
EPS = 1e-06
ROUTE_SCALE = 2.5
LANES = 256
SQ_TILE = 16
DOT_ROWS = (((1,), (1,)), ((), ()))


def exchange(x, bit):
    size = lax.axis_size("pipe")
    return lax.ppermute(x, "pipe", [(i, i ^ (1 << bit)) for i in range(size)])


def other_section(x):
    size = lax.axis_size("pipe")
    return lax.ppermute(x, "pipe", [(i, (i + size // 2) % size) for i in range(size)])


def weight_kernel(where, gate_up, down, step, rate, w_in, w_out):
    h, y = where[0], where[1]
    cols = gate_up.shape[0] // 4
    w_in[...] = jnp.zeros_like(w_in)
    w_out[...] = jnp.zeros_like(w_out)
    for block in range(4):
        rows = pl.ds(pl.multiple_of((h ^ ((block & 1) * 2 + (block >> 1))) * cols, 32), cols)
        for place, rel in enumerate((0, 2, 1, 3)):
            at = pl.multiple_of((y ^ rel) * 128, 128)
            to = slice(block * LANES, block * LANES + cols)
            w_in[to, place * 256 : place * 256 + 128] = gate_up[rows, pl.ds(at, 128)]
            w_in[to, place * 256 + 128 : place * 256 + 256] = gate_up[
                rows, pl.ds(pl.multiple_of(512 + at, 128), 128)
            ]
            w_out[to, place * 128 : place * 128 + 128] = (
                down[rows, pl.ds(at, 128)].astype(jnp.float32)
                + rate[0] * step[rows, pl.ds(at, 128)].astype(jnp.float32)
            ).astype(jnp.bfloat16)


def arrange_weights(where, rate, gate_up, down, step):
    vmem = pl.BlockSpec(memory_space=pltpu.VMEM)
    smem = pl.BlockSpec(memory_space=pltpu.SMEM)
    return pl.pallas_call(
        weight_kernel,
        out_shape=(
            jax.ShapeDtypeStruct((4 * LANES, gate_up.shape[1]), jnp.bfloat16),
            jax.ShapeDtypeStruct((4 * LANES, down.shape[1]), jnp.bfloat16),
        ),
        in_specs=[smem, vmem, vmem, vmem, smem],
        out_specs=(vmem, vmem),
        cost_estimate=pl.CostEstimate(flops=2000000, bytes_accessed=8000000, transcendentals=0),
    )(where, gate_up, down, step, rate)


def routing(route_ids, route_scores, expert_count, capacity):
    lead, rows, picks = route_ids.shape
    flat = route_ids.reshape(lead, rows * picks)
    one_hot = (flat[:, :, None] == jnp.arange(expert_count, dtype=jnp.int32)).astype(jnp.int32)
    position = jnp.sum((jnp.cumsum(one_hot, axis=1) - one_hot) * one_hot, axis=2)
    slot = (flat * capacity + position).reshape(lead, rows, picks)
    slot_ids = jnp.arange(expert_count * capacity, dtype=jnp.int32)
    chosen = (slot[..., None] == slot_ids).astype(jnp.float32)
    mixing = ROUTE_SCALE * route_scores / jnp.sum(route_scores, axis=2, keepdims=True)
    mix = jnp.sum(mixing[..., None] * chosen, axis=2)
    return jnp.sum(chosen, axis=2).astype(jnp.bfloat16), mix


def layer(state, spread, mix, gain, w_in, w_out, expert_count, capacity):
    lead, rows, cols = state.shape
    values = state.astype(jnp.float32)
    squares = jnp.sum(values * values, axis=2, keepdims=True)
    high = squares.astype(jnp.bfloat16)
    low = (squares - high.astype(jnp.float32)).astype(jnp.bfloat16)
    tail = jnp.zeros((lead, rows, LANES - cols - 2), jnp.bfloat16)
    prepared = jnp.concatenate([(values * gain).astype(jnp.bfloat16), high, low, tail], axis=2)
    both = jnp.concatenate([prepared, exchange(prepared, 1)], axis=2)
    buffer = jnp.einsum("nrs,nrc->nsc", spread, both, preferred_element_type=jnp.float32)
    buffer = buffer.astype(jnp.bfloat16).reshape(lead, expert_count, capacity, 2 * LANES)
    arrived = lax.all_to_all(
        buffer.transpose(1, 0, 2, 3), "expert", split_axis=0, concat_axis=0, tiled=True
    )
    slots = expert_count * lead * capacity
    arrived = arrived.reshape(slots, 2 * LANES)
    inputs = jnp.concatenate([arrived, exchange(arrived, 0)], axis=1)
    lane = jnp.arange(4 * LANES) % LANES
    marks = ((lane == cols) | (lane == cols + 1)).astype(jnp.bfloat16)
    marks = jnp.broadcast_to(marks[None], (SQ_TILE, 4 * LANES))
    half = LANES
    sums = [
        lax.dot_general(marks, part, DOT_ROWS, preferred_element_type=jnp.float32)
        for part in (inputs[:half], inputs[half:])
    ]
    sums[1] = jnp.pad(sums[1], ((0, 0), (0, 2 * half - slots)))
    index = jnp.arange(SQ_TILE)[:, None]
    sums = jnp.where(index == 0, sums[0], jnp.where(index == 1, sums[1], 0.0))
    partial = jnp.dot(inputs, w_in, preferred_element_type=jnp.float32)
    width = partial.shape[1]
    for bit in (3, 4):
        width //= 2
        message = jnp.concatenate(
            [
                partial[:, width:].astype(jnp.bfloat16),
                jnp.pad(sums, ((0, 0), (0, width - half))).astype(jnp.bfloat16),
            ],
            axis=0,
        )
        got = exchange(message, bit).astype(jnp.float32)
        partial = partial[:, :width] + got[:slots]
        sums = sums + got[slots:, :half]
    message = jnp.concatenate([partial, sums], axis=0).astype(jnp.bfloat16)
    got = exchange(message, 2).astype(jnp.float32)
    partial = partial + got[:slots]
    sums = sums + got[slots:]
    scaling = lax.rsqrt(jnp.concatenate([sums[0], sums[1, : slots - half]]) / D + EPS)[:, None]
    projected = partial * scaling
    activated = (jax.nn.silu(projected[:, :128]) * projected[:, 128:]).astype(jnp.bfloat16)
    for bit in (4, 3):
        activated = jnp.concatenate([activated, exchange(activated, bit)], axis=1)
    partial = lax.dot_general(activated, w_out, DOT_ROWS, preferred_element_type=jnp.float32)
    got = exchange(partial[:, 2 * LANES :].astype(jnp.bfloat16), 0)
    expert_out = (partial[:, : 2 * LANES] + got.astype(jnp.float32)).astype(jnp.bfloat16)
    expert_out = expert_out.reshape(expert_count, lead, capacity, 2 * LANES)
    returned = lax.all_to_all(expert_out, "expert", split_axis=0, concat_axis=0, tiled=True)
    returned = returned.transpose(1, 0, 2, 3).reshape(lead, expert_count * capacity, 2 * LANES)
    mix_high = mix.astype(jnp.bfloat16)
    mix_low = (mix - mix_high.astype(jnp.float32)).astype(jnp.bfloat16)
    mixed = sum(
        jnp.einsum("nrs,nsc->nrc", part, returned, preferred_element_type=jnp.float32)
        for part in (mix_high, mix_low)
    )
    got = exchange(mixed[:, :, LANES:].astype(jnp.bfloat16), 1)
    mixed = mixed[:, :, :cols] + got[:, :, :cols].astype(jnp.float32)
    return (values + mixed).astype(jnp.bfloat16)


def body(flowing, norm_gain, gate_up, down_proj, down_step, step_rate, routes, scores):
    shards = lax.axis_size("pipe") // step_rate.shape[1]
    my_index = lax.axis_index("pipe")
    section = my_index // shards
    expert_count = lax.axis_size("expert")
    capacity = flowing.shape[1] * routes.shape[-1] // expert_count + 2
    where = jnp.stack([my_index & 3, (my_index >> 3) & 3]).astype(jnp.int32)
    rate = lax.dynamic_slice_in_dim(step_rate[0], section, 1, 0)
    w_in, w_out = arrange_weights(where, rate, gate_up[0, 0], down_proj[0, 0], down_step[0, 0])
    route_here = lax.dynamic_index_in_dim(routes, section, 1, keepdims=False)
    score_here = lax.dynamic_index_in_dim(scores, section, 1, keepdims=False)
    ticks = routes.shape[0]
    state = flowing
    for tick in range(ticks):
        spread, mix = routing(route_here[tick], score_here[tick], expert_count, capacity)
        state = layer(state, spread, mix, norm_gain, w_in, w_out, expert_count, capacity)
        if tick + 1 < ticks:
            state = other_section(state)
    return state


def solution(mesh):
    placed = (
        P(None, "expert", "pipe"),
        P("pipe"),
        P("expert", "pipe", None, None),
        P("expert", "pipe", None, None),
        P("expert", "pipe", None, None),
        P("expert", None),
        P(None, None, None, "expert", None),
        P(None, None, None, "expert", None),
    )
    return jax.shard_map(
        body, mesh=mesh, in_specs=placed, out_specs=P(None, "expert", "pipe"), check_vma=False
    )
```

time: 426 us -> 312 us (0.73)
  waiting for transfers between devices: 188 us -> 117 us
  starting transfers between devices: 179 us -> 138 us
  local copies, waits for them, and re-layouts: 18.4 us -> 7.78 us
  blocking collectives: 19.1 us -> 25.8 us
  Pallas kernels: 0 us -> 5.11 us
    ppermute x32 -> x19, waiting for transfers between devices: 166 us -> 98.9 us  [the longest x18 96.1 us: exchange(): return lax.ppermute(x, 'pipe', [(i, i ^ 1 << bit) for i in range(size)])]
    ppermute x32 -> x19, starting transfers between devices: 160 us -> 118 us  [the longest x18 112 us: exchange(): return lax.ppermute(x, 'pipe', [(i, i ^ 1 << bit) for i in range(size)])]
    all_to_all x2, blocking collectives: 19.1 us -> 25.8 us  [the longest x1 14.1 us: layer(): lax.all_to_all(expert_out, 'expert', split_axis=0, concat_axis=0, tiled=T...]
    gather x4 -> x0, local copies, waits for them, and re-layouts: 6.55 us -> none  [moe_layer(): gathered = jnp.take_along_axis(returned, slot_of[:, :, None], axis=1)]
    pallas_call x0 -> x1, Pallas kernels: none -> 5.11 us  [arrange_weights(): pl.pallas_call(weight_kernel, out_shape=(jax.ShapeDtypeStruct((4 * LANES,...]
    all_to_all x4 -> x2, waiting for transfers between devices: 21.9 us -> 17.8 us  [the longest x1 9.35 us: layer(): lax.all_to_all(buffer.transpose(1, 0, 2, 3), 'expert', split_axis=0, conc...]
    dot_general x8 -> x14, matrix products: 9.6 us -> 9.07 us  [the longest x2 5.38 us: layer(): partial = jnp.dot(inputs, w_in, preferred_element_type=jnp.float32)]
    all_to_all x4 -> x2, starting transfers between devices: 19.4 us -> 19.7 us  [the longest x1 10.3 us: layer(): lax.all_to_all(expert_out, 'expert', split_axis=0, concat_axis=0, tiled=T...]
  transfers between devices with their start and end apart: 36 -> 21, of which waited for: 22 -> 19; matrix products, arithmetic and copies ran while one was open for 3% -> 2% of each run, Pallas kernels for 0% -> 2%
where the time goes in v1:
time: 312 us; the launch traced here: 311 us
  starting transfers between devices  138 us (44%)
  waiting for transfers between devices  117 us (38%)
  blocking collectives  25.8 us (8%)
  matrix products  9.07 us (3%)
  local copies, waits for them, and re-layouts  7.78 us (2%)
  other arithmetic  7.67 us (2%)
  Pallas kernels  5.11 us (2%)
    ppermute x18, starting transfers between devices, exchange(): return lax.ppermute(x, 'pipe', [(i, i ^ 1 << bit) for i in range(size)])  112 us
    ppermute x18, waiting for transfers between devices, exchange(): return lax.ppermute(x, 'pipe', [(i, i ^ 1 << bit) for i in range(size)])  96.1 us
    all_to_all x1, blocking collectives, layer(): lax.all_to_all(expert_out, 'expert', split_axis=0, concat_axis=0, tiled=T...  14.1 us
    all_to_all x1, blocking collectives, layer(): lax.all_to_all(buffer.transpose(1, 0, 2, 3), 'expert', split_axis=0, conc...  11.7 us
    all_to_all x1, starting transfers between devices, layer(): lax.all_to_all(expert_out, 'expert', split_axis=0, concat_axis=0, tiled=T...  10.3 us
    all_to_all x1, starting transfers between devices, layer(): lax.all_to_all(buffer.transpose(1, 0, 2, 3), 'expert', split_axis=0, conc...  9.45 us
    all_to_all x1, waiting for transfers between devices, layer(): lax.all_to_all(buffer.transpose(1, 0, 2, 3), 'expert', split_axis=0, conc...  9.35 us
    all_to_all x1, waiting for transfers between devices, layer(): lax.all_to_all(expert_out, 'expert', split_axis=0, concat_axis=0, tiled=T...  8.46 us
  transfers between devices with their start and end apart: 21, of which 19 were waited for; matrix products, arithmetic and copies ran while one was open for 2% of the time, Pallas kernels for 2%

profile of v1, /device:TPU:1, one launch (start us, length us, event | category | flops | bytes accessed | tf_op | source)
XLA Modules:
  0.0 310.9 jit_solution(4160933718494575567)
XLA Ops:
  0.0 1.0 fusion.35
  1.5 8.4 %collective-permute-start = (bf16[2,96,256]{2,1,0:T(8,128)(2,1)S(1)}, bf16[2,96,256]{2,1,0:T(8,128)(2,1)S(1)}, u32[]{:S(2)}, u32[]{:S(2)}) collective-permute-start(bf16[2,96,256]{2,1,0:T(8,128)(2,1)S(1)} %pad_maximum_fusion.7), channel_id=1, source_target_pairs={{0,24},{12,36},{24,0},{36,12},{48,72},{60,84},{72,48},{84,60},{96,... | collective-permute-start | bytes 294920 | tf_op jit(solution)/shard_map/ppermute | solution.py:19
  9.9 0.7 constant_dynamic-slice_fusion.3
  11.0 1.2 reduce-window.14
  12.2 0.2 slice_reduce_fusion.1
  13.2 0.3 convolution_convert_fusion.1
  13.6 1.1 copy.86
  14.7 9.5 %all-to-all-start = ((bf16[12,2,18,512]{3,1,2,0:T(2,128)(2,1)}), bf16[12,2,18,512]{3,1,2,0:T(2,128)(2,1)S(1)}, u32[]{:S(2)}, u32[]{:S(2)}) async-start(bf16[12,2,18,512]{3,1,2,0:T(2,128)(2,1)} %bitcast.5), calls=%async_computation | async-start | bytes 884736 | tf_op jit(solution)/shard_map/all_to_all | solution.py:86
  24.1 0.6 constant_dynamic-slice_fusion.1
  24.7 9.4 %all-to-all-done = bf16[12,2,18,512]{3,1,2,0:T(2,128)(2,1)S(1)} async-done(((bf16[12,2,18,512]{3,1,2,0:T(2,128)(2,1)}), bf16[12,2,18,512]{3,1,2,0:T(2,128)(2,1)S(1)}, u32[]{:S(2)}, u32[]{:S(2)}) %all-to-all-start) | async-done | bytes 442400 | tf_op jit(solution)/shard_map/all_to_all | solution.py:86
  34.3 4.5 %collective-permute-start.1 = (bf16[432,512]{1,0:T(8,128)(2,1)S(1)}, bf16[432,512]{1,0:T(8,128)(2,1)S(1)}, u32[]{:S(2)}, u32[]{:S(2)}) collective-permute-start(bf16[432,512]{1,0:T(8,128)(2,1)S(1)} %reshape.214), channel_id=1, source_target_pairs={{0,12},{12,0},{24,36},{36,24},{48,60},{60,48},{72,84},{84,72},{96,... | collective-permute-start | bytes 1327112 | tf_op jit(solution)/shard_map/ppermute | solution.py:19
  38.8 0.6 pad_add_fusion.where
  39.4 5.1 %shard_map.82 = (bf16[1024,1024]{1,0:T(8,128)(2,1)}, bf16[1024,512]{1,0:T(8,128)(2,1)}) custom-call(s32[2]{0:T(128)} %pad_add_fusion.where, bf16[896,1024]{1,0:T(8,128)(2,1)} %bitcast.70, bf16[896,512]{1,0:T(8,128)(2,1)} %bitcast.72, bf16[896,512]{1,0:T(8,128)(2,1)} %bitcast.73, f32[1]{0:T(128)} %bitcast.11.rate), custom_call_target="tpu_custom_call" | custom-call | flops 2000000 | bytes 8000000 | tf_op jit(solution)/shard_map/pallas_call | solution.py:50
  44.6 2.7 fusion.78
  47.6 0.3 fusion.76
  47.9 3.2 %collective-permute-start.2 = (bf16[448,512]{1,0:T(8,128)(2,1)S(1)}, bf16[448,512]{1,0:T(8,128)(2,1)S(1)}, u32[]{:S(2)}, u32[]{:S(2)}) collective-permute-start(bf16[448,512]{1,0:T(8,128)(2,1)S(1)} %fusion.6), channel_id=1, source_target_pairs={{0,96},{12,108},{24,120},{36,132},{48,144},{60,156},{72,168},{84,1... | collective-permute-start | bytes 1376264 | tf_op jit(solution)/shard_map/ppermute | solution.py:19
  51.1 10.7 %collective-permute-done.2 = bf16[448,512]{1,0:T(8,128)(2,1)S(1)} collective-permute-done((bf16[448,512]{1,0:T(8,128)(2,1)S(1)}, bf16[448,512]{1,0:T(8,128)(2,1)S(1)}, u32[]{:S(2)}, u32[]{:S(2)}) %collective-permute-start.2) | collective-permute-done | bytes 458784 | tf_op jit(solution)/shard_map/ppermute | solution.py:19
  62.2 4.2 %collective-permute-start.3 = (bf16[448,256]{1,0:T(8,128)(2,1)S(1)}, bf16[448,256]{1,0:T(8,128)(2,1)S(1)}, u32[]{:S(2)}, u32[]{:S(2)}) collective-permute-start(bf16[448,256]{1,0:T(8,128)(2,1)S(1)} %pad_maximum_fusion), channel_id=1, source_target_pairs={{0,192},{12,204},{24,216},{36,228},{48,240},{60,252},{72,264},{84,... | collective-permute-start | bytes 688136 | tf_op jit(solution)/shard_map/ppermute | solution.py:19
  66.4 10.0 %collective-permute-done.3 = bf16[448,256]{1,0:T(8,128)(2,1)S(1)} collective-permute-done((bf16[448,256]{1,0:T(8,128)(2,1)S(1)}, bf16[448,256]{1,0:T(8,128)(2,1)S(1)}, u32[]{:S(2)}, u32[]{:S(2)}) %collective-permute-start.3) | collective-permute-done | bytes 229408 | tf_op jit(solution)/shard_map/ppermute | solution.py:19
  76.6 13.0 %collective-permute-start.4 = (bf16[448,256]{1,0:T(8,128)(2,1)S(1)}, bf16[448,256]{1,0:T(8,128)(2,1)S(1)}, u32[]{:S(2)}, u32[]{:S(2)}) collective-permute-start(bf16[448,256]{1,0:T(8,128)(2,1)S(1)} %pad_maximum_fusion.1), channel_id=1, source_target_pairs={{0,48},{12,60},{24,72},{36,84},{48,0},{60,12},{72,24},{84,36},{96,... | collective-permute-start | bytes 688136 | tf_op jit(solution)/shard_map/ppermute | solution.py:19
  89.6 4.5 %collective-permute-done.4 = bf16[448,256]{1,0:T(8,128)(2,1)S(1)} collective-permute-done((bf16[448,256]{1,0:T(8,128)(2,1)S(1)}, bf16[448,256]{1,0:T(8,128)(2,1)S(1)}, u32[]{:S(2)}, u32[]{:S(2)}) %collective-permute-start.4) | collective-permute-done | bytes 229408 | tf_op jit(solution)/shard_map/ppermute | solution.py:19
  94.3 1.9 collective-permute-start.5
  96.3 4.5 %collective-permute-done.5 = bf16[432,128]{1,0:T(8,128)(2,1)S(1)} collective-permute-done((bf16[432,128]{1,0:T(8,128)(2,1)S(1)}, bf16[432,128]{1,0:T(8,128)(2,1)S(1)}, u32[]{:S(2)}, u32[]{:S(2)}) %collective-permute-start.5) | collective-permute-done | bytes 110624 | tf_op jit(solution)/shard_map/ppermute | solution.py:19
  100.8 5.1 %collective-permute-start.6 = (bf16[432,256]{1,0:T(8,128)(2,1)S(1)}, bf16[432,256]{1,0:T(8,128)(2,1)S(1)}, u32[]{:S(2)}, u32[]{:S(2)}) collective-permute-start(bf16[432,256]{1,0:T(8,128)(2,1)S(1)} %pad_maximum_fusion.4), channel_id=1, source_target_pairs={{0,96},{12,108},{24,120},{36,132},{48,144},{60,156},{72,168},{84,1... | collective-permute-start | bytes 663560 | tf_op jit(solution)/shard_map/ppermute | solution.py:19
  105.8 3.3 %collective-permute-done.6 = bf16[432,256]{1,0:T(8,128)(2,1)S(1)} collective-permute-done((bf16[432,256]{1,0:T(8,128)(2,1)S(1)}, bf16[432,256]{1,0:T(8,128)(2,1)S(1)}, u32[]{:S(2)}, u32[]{:S(2)}) %collective-permute-start.6) | collective-permute-done | bytes 221216 | tf_op jit(solution)/shard_map/ppermute | solution.py:19
  109.2 0.7 fusion.10
  109.9 7.9 %collective-permute-start.7 = (bf16[432,512]{1,0:T(8,128)(2,1)S(1)}, bf16[432,512]{1,0:T(8,128)(2,1)S(1)}, u32[]{:S(2)}, u32[]{:S(2)}) collective-permute-start(bf16[432,512]{1,0:T(8,128)(2,1)S(1)} %slice.380), channel_id=1, source_target_pairs={{0,12},{12,0},{24,36},{36,24},{48,60},{60,48},{72,84},{84,72},{96,... | collective-permute-start | bytes 1327112 | tf_op jit(solution)/shard_map/ppermute | solution.py:19
  117.8 1.4 collective-permute-done.7
  119.5 1.1 copy.88
  120.6 10.3 %all-to-all-start.1 = ((bf16[12,2,18,512]{3,1,2,0:T(2,128)(2,1)}), bf16[12,2,18,512]{3,1,2,0:T(2,128)(2,1)S(1)}, u32[]{:S(2)}, u32[]{:S(2)}) async-start(bf16[12,2,18,512]{3,1,2,0:T(2,128)(2,1)} %copy.88), calls=%async_computation.1 | async-start | bytes 884736 | tf_op jit(solution)/shard_map/all_to_all | solution.py:130
  131.3 1.2 reduce-window.16
  132.5 0.2 slice_reduce_fusion
  132.9 8.5 %all-to-all-done.1 = bf16[12,2,18,512]{3,1,2,0:T(2,128)(2,1)S(1)} async-done(((bf16[12,2,18,512]{3,1,2,0:T(2,128)(2,1)}), bf16[12,2,18,512]{3,1,2,0:T(2,128)(2,1)S(1)}, u32[]{:S(2)}, u32[]{:S(2)}) %all-to-all-start.1) | async-done | bytes 442400 | tf_op jit(solution)/shard_map/all_to_all | solution.py:130
  141.8 8.6 %collective-permute-start.8 = (bf16[2,96,256]{2,1,0:T(8,128)(2,1)S(1)}, bf16[2,96,256]{2,1,0:T(8,128)(2,1)S(1)}, u32[]{:S(2)}, u32[]{:S(2)}) collective-permute-start(bf16[2,96,256]{2,1,0:T(8,128)(2,1)S(1)} %slice.385), channel_id=1, source_target_pairs={{0,24},{12,36},{24,0},{36,12},{48,72},{60,84},{72,48},{84,60},{96,... | collective-permute-start | bytes 294920 | tf_op jit(solution)/shard_map/ppermute | solution.py:19
  150.6 6.7 %collective-permute-done.8 = bf16[2,96,256]{2,1,0:T(8,128)(2,1)S(1)} collective-permute-done((bf16[2,96,256]{2,1,0:T(8,128)(2,1)S(1)}, bf16[2,96,256]{2,1,0:T(8,128)(2,1)S(1)}, u32[]{:S(2)}, u32[]{:S(2)}) %collective-permute-start.8) | collective-permute-done | bytes 98336 | tf_op jit(solution)/shard_map/ppermute | solution.py:19
  157.3 6.4 %collective-permute-start.9 = (bf16[2,96,224]{2,1,0:T(8,128)(2,1)S(1)}, bf16[2,96,224]{2,1,0:T(8,128)(2,1)S(1)}, u32[]{:S(2)}, u32[]{:S(2)}) collective-permute-start(bf16[2,96,224]{2,1,0:T(8,128)(2,1)S(1)} %fusion.36), channel_id=1, source_target_pairs={{0,384},{12,396},{24,408},{36,420},{48,432},{60,444},{72,456},{84,... | collective-permute-start | bytes 258056 | tf_op jit(solution)/shard_map/ppermute | solution.py:24
  163.9 2.8 collective-permute-done.9
  167.2 1.9 collective-permute-start.10
  169.3 6.0 %collective-permute-done.10 = bf16[2,96,256]{2,1,0:T(8,128)(2,1)S(1)} collective-permute-done((bf16[2,96,256]{2,1,0:T(8,128)(2,1)S(1)}, bf16[2,96,256]{2,1,0:T(8,128)(2,1)S(1)}, u32[]{:S(2)}, u32[]{:S(2)}) %collective-permute-start.10) | collective-permute-done | bytes 98336 | tf_op jit(solution)/shard_map/ppermute | solution.py:19
  175.4 0.3 convolution_convert_fusion
  175.8 0.3 copy.98
  176.1 11.7 %all_to_all.20 = bf16[12,2,18,512]{3,1,2,0:T(2,128)(2,1)S(1)} all-to-all(bf16[12,2,18,512]{3,1,2,0:T(2,128)(2,1)S(1)} %bitcast.71), channel_id=1, replica_groups=mesh['pipe'=64,'expert'=12] {'expert'}, dimensions={0} | all-to-all | bytes 884736 | tf_op jit(solution)/shard_map/all_to_all | solution.py:86
  188.0 7.4 %collective-permute-start.11 = (bf16[432,512]{1,0:T(8,128)(2,1)S(1)}, bf16[432,512]{1,0:T(8,128)(2,1)S(1)}, u32[]{:S(2)}, u32[]{:S(2)}) collective-permute-start(bf16[432,512]{1,0:T(8,128)(2,1)S(1)} %reshape.220), channel_id=1, source_target_pairs={{0,12},{12,0},{24,36},{36,24},{48,60},{60,48},{72,84},{84,72},{96,... | collective-permute-start | bytes 1327112 | tf_op jit(solution)/shard_map/ppermute | solution.py:19
  195.5 1.3 collective-permute-done.11
  196.8 2.7 fusion.79
  199.8 0.2 fusion.77
  200.1 3.9 %collective-permute-start.12 = (bf16[448,512]{1,0:T(8,128)(2,1)S(1)}, bf16[448,512]{1,0:T(8,128)(2,1)S(1)}, u32[]{:S(2)}, u32[]{:S(2)}) collective-permute-start(bf16[448,512]{1,0:T(8,128)(2,1)S(1)} %fusion.7), channel_id=1, source_target_pairs={{0,96},{12,108},{24,120},{36,132},{48,144},{60,156},{72,168},{84,1... | collective-permute-start | bytes 1376264 | tf_op jit(solution)/shard_map/ppermute | solution.py:19
  204.1 10.5 %collective-permute-done.12 = bf16[448,512]{1,0:T(8,128)(2,1)S(1)} collective-permute-done((bf16[448,512]{1,0:T(8,128)(2,1)S(1)}, bf16[448,512]{1,0:T(8,128)(2,1)S(1)}, u32[]{:S(2)}, u32[]{:S(2)}) %collective-permute-start.12) | collective-permute-done | bytes 458784 | tf_op jit(solution)/shard_map/ppermute | solution.py:19
  214.9 4.0 %collective-permute-start.13 = (bf16[448,256]{1,0:T(8,128)(2,1)S(1)}, bf16[448,256]{1,0:T(8,128)(2,1)S(1)}, u32[]{:S(2)}, u32[]{:S(2)}) collective-permute-start(bf16[448,256]{1,0:T(8,128)(2,1)S(1)} %pad_maximum_fusion.2), channel_id=1, source_target_pairs={{0,192},{12,204},{24,216},{36,228},{48,240},{60,252},{72,264},{84,... | collective-permute-start | bytes 688136 | tf_op jit(solution)/shard_map/ppermute | solution.py:19
  218.9 10.4 %collective-permute-done.13 = bf16[448,256]{1,0:T(8,128)(2,1)S(1)} collective-permute-done((bf16[448,256]{1,0:T(8,128)(2,1)S(1)}, bf16[448,256]{1,0:T(8,128)(2,1)S(1)}, u32[]{:S(2)}, u32[]{:S(2)}) %collective-permute-start.13) | collective-permute-done | bytes 229408 | tf_op jit(solution)/shard_map/ppermute | solution.py:19
  229.4 11.1 %collective-permute-start.14 = (bf16[448,256]{1,0:T(8,128)(2,1)S(1)}, bf16[448,256]{1,0:T(8,128)(2,1)S(1)}, u32[]{:S(2)}, u32[]{:S(2)}) collective-permute-start(bf16[448,256]{1,0:T(8,128)(2,1)S(1)} %pad_maximum_fusion.3), channel_id=1, source_target_pairs={{0,48},{12,60},{24,72},{36,84},{48,0},{60,12},{72,24},{84,36},{96,... | collective-permute-start | bytes 688136 | tf_op jit(solution)/shard_map/ppermute | solution.py:19
  240.5 10.6 %collective-permute-done.14 = bf16[448,256]{1,0:T(8,128)(2,1)S(1)} collective-permute-done((bf16[448,256]{1,0:T(8,128)(2,1)S(1)}, bf16[448,256]{1,0:T(8,128)(2,1)S(1)}, u32[]{:S(2)}, u32[]{:S(2)}) %collective-permute-start.14) | collective-permute-done | bytes 229408 | tf_op jit(solution)/shard_map/ppermute | solution.py:19
  251.5 1.9 collective-permute-start.15
  253.4 4.5 %collective-permute-done.15 = bf16[432,128]{1,0:T(8,128)(2,1)S(1)} collective-permute-done((bf16[432,128]{1,0:T(8,128)(2,1)S(1)}, bf16[432,128]{1,0:T(8,128)(2,1)S(1)}, u32[]{:S(2)}, u32[]{:S(2)}) %collective-permute-start.15) | collective-permute-done | bytes 110624 | tf_op jit(solution)/shard_map/ppermute | solution.py:19
  257.9 6.7 %collective-permute-start.16 = (bf16[432,256]{1,0:T(8,128)(2,1)S(1)}, bf16[432,256]{1,0:T(8,128)(2,1)S(1)}, u32[]{:S(2)}, u32[]{:S(2)}) collective-permute-start(bf16[432,256]{1,0:T(8,128)(2,1)S(1)} %pad_maximum_fusion.5), channel_id=1, source_target_pairs={{0,96},{12,108},{24,120},{36,132},{48,144},{60,156},{72,168},{84,1... | collective-permute-start | bytes 663560 | tf_op jit(solution)/shard_map/ppermute | solution.py:19
  264.6 3.3 %collective-permute-done.16 = bf16[432,256]{1,0:T(8,128)(2,1)S(1)} collective-permute-done((bf16[432,256]{1,0:T(8,128)(2,1)S(1)}, bf16[432,256]{1,0:T(8,128)(2,1)S(1)}, u32[]{:S(2)}, u32[]{:S(2)}) %collective-permute-start.16) | collective-permute-done | bytes 221216 | tf_op jit(solution)/shard_map/ppermute | solution.py:19
  267.9 0.7 fusion.16
  268.6 5.0 %collective-permute-start.17 = (bf16[432,512]{1,0:T(8,128)(2,1)S(1)}, bf16[432,512]{1,0:T(8,128)(2,1)S(1)}, u32[]{:S(2)}, u32[]{:S(2)}) collective-permute-start(bf16[432,512]{1,0:T(8,128)(2,1)S(1)} %slice.378), channel_id=1, source_target_pairs={{0,12},{12,0},{24,36},{36,24},{48,60},{60,48},{72,84},{84,72},{96,... | collective-permute-start | bytes 1327112 | tf_op jit(solution)/shard_map/ppermute | solution.py:19
  273.6 1.4 collective-permute-done.17
  275.3 0.3 copy.100
  275.7 14.1 %all_to_all.21 = bf16[12,2,18,512]{3,1,2,0:T(2,128)(2,1)S(1)} all-to-all(bf16[12,2,18,512]{3,1,2,0:T(2,128)(2,1)S(1)} %copy.100), channel_id=1, replica_groups=mesh['pipe'=64,'expert'=12] {'expert'}, dimensions={0} | all-to-all | bytes 884736 | tf_op jit(solution)/shard_map/all_to_all | solution.py:130
  290.2 12.9 %collective-permute-start.18 = (bf16[2,96,256]{2,1,0:T(8,128)(2,1)S(1)}, bf16[2,96,256]{2,1,0:T(8,128)(2,1)S(1)}, u32[]{:S(2)}, u32[]{:S(2)}) collective-permute-start(bf16[2,96,256]{2,1,0:T(8,128)(2,1)S(1)} %slice.384), channel_id=1, source_target_pairs={{0,24},{12,36},{24,0},{36,12},{48,72},{60,84},{72,48},{84,60},{96,... | collective-permute-start | bytes 294920 | tf_op jit(solution)/shard_map/ppermute | solution.py:19
  303.2 7.0 %collective-permute-done.18 = bf16[2,96,256]{2,1,0:T(8,128)(2,1)S(1)} collective-permute-done((bf16[2,96,256]{2,1,0:T(8,128)(2,1)S(1)}, bf16[2,96,256]{2,1,0:T(8,128)(2,1)S(1)}, u32[]{:S(2)}, u32[]{:S(2)}) %collective-permute-start.18) | collective-permute-done | bytes 98336 | tf_op jit(solution)/shard_map/ppermute | solution.py:19
  310.2 0.7 fusion.39
  (121 shorter events, 7.5 us)
Async XLA Ops:
  0.0 24.1 %copy-start = (f32[1,2]{1,0:T(1,128)S(1)}, f32[1,2]{1,0:T(1,128)}, u32[]{:S(2)}) copy-start(f32[1,2]{1,0:T(1,128)} %param.13) | copy-start | bytes 28
  0.0 12.8 %copy-start.3 = (f32[2,2,2,96,2]{3,4,2,1,0:T(2,128)S(1)}, f32[2,2,2,96,2]{3,4,2,1,0:T(2,128)}, u32[]{:S(2)}) copy-start(f32[2,2,2,96,2]{3,4,2,1,0:T(2,128)} %param.15) | copy-start | bytes 18436
  1.5 11.6 %collective-permute-start = (bf16[2,96,256]{2,1,0:T(8,128)(2,1)S(1)}, bf16[2,96,256]{2,1,0:T(8,128)(2,1)S(1)}, u32[]{:S(2)}, u32[]{:S(2)}) collective-permute-start(bf16[2,96,256]{2,1,0:T(8,128)(2,1)S(1)} %pad_maximum_fusion.7), channel_id=1, source_target_pairs={{0,24},{12,36},{24,0},{36,12},{48,72},{60,84},{72,48},{84,60},{96,... | collective-permute-start | bytes 294920 | tf_op jit(solution)/shard_map/ppermute | solution.py:19
  14.7 19.4 %all-to-all-start = ((bf16[12,2,18,512]{3,1,2,0:T(2,128)(2,1)}), bf16[12,2,18,512]{3,1,2,0:T(2,128)(2,1)S(1)}, u32[]{:S(2)}, u32[]{:S(2)}) async-start(bf16[12,2,18,512]{3,1,2,0:T(2,128)(2,1)} %bitcast.5), calls=%async_computation | async-start | bytes 884736 | tf_op jit(solution)/shard_map/all_to_all | solution.py:86
  34.3 10.3 %collective-permute-start.1 = (bf16[432,512]{1,0:T(8,128)(2,1)S(1)}, bf16[432,512]{1,0:T(8,128)(2,1)S(1)}, u32[]{:S(2)}, u32[]{:S(2)}) collective-permute-start(bf16[432,512]{1,0:T(8,128)(2,1)S(1)} %reshape.214), channel_id=1, source_target_pairs={{0,12},{12,0},{24,36},{36,24},{48,60},{60,48},{72,84},{84,72},{96,... | collective-permute-start | bytes 1327112 | tf_op jit(solution)/shard_map/ppermute | solution.py:19
  47.9 14.0 %collective-permute-start.2 = (bf16[448,512]{1,0:T(8,128)(2,1)S(1)}, bf16[448,512]{1,0:T(8,128)(2,1)S(1)}, u32[]{:S(2)}, u32[]{:S(2)}) collective-permute-start(bf16[448,512]{1,0:T(8,128)(2,1)S(1)} %fusion.6), channel_id=1, source_target_pairs={{0,96},{12,108},{24,120},{36,132},{48,144},{60,156},{72,168},{84,1... | collective-permute-start | bytes 1376264 | tf_op jit(solution)/shard_map/ppermute | solution.py:19
  62.2 14.2 %collective-permute-start.3 = (bf16[448,256]{1,0:T(8,128)(2,1)S(1)}, bf16[448,256]{1,0:T(8,128)(2,1)S(1)}, u32[]{:S(2)}, u32[]{:S(2)}) collective-permute-start(bf16[448,256]{1,0:T(8,128)(2,1)S(1)} %pad_maximum_fusion), channel_id=1, source_target_pairs={{0,192},{12,204},{24,216},{36,228},{48,240},{60,252},{72,264},{84,... | collective-permute-start | bytes 688136 | tf_op jit(solution)/shard_map/ppermute | solution.py:19
  76.6 32.6 %copy-start.1 = (bf16[1024,512]{1,0:T(8,128)(2,1)S(1)}, bf16[1024,512]{1,0:T(8,128)(2,1)}, u32[]{:S(2)}) copy-start(bf16[1024,512]{1,0:T(8,128)(2,1)} %get-tuple-element.8) | copy-start | bytes 3145732
  76.6 17.4 %collective-permute-start.4 = (bf16[448,256]{1,0:T(8,128)(2,1)S(1)}, bf16[448,256]{1,0:T(8,128)(2,1)S(1)}, u32[]{:S(2)}, u32[]{:S(2)}) collective-permute-start(bf16[448,256]{1,0:T(8,128)(2,1)S(1)} %pad_maximum_fusion.1), channel_id=1, source_target_pairs={{0,48},{12,60},{24,72},{36,84},{48,0},{60,12},{72,24},{84,36},{96,... | collective-permute-start | bytes 688136 | tf_op jit(solution)/shard_map/ppermute | solution.py:19
  94.3 6.4 %collective-permute-start.5 = (bf16[432,128]{1,0:T(8,128)(2,1)S(1)}, bf16[432,128]{1,0:T(8,128)(2,1)S(1)}, u32[]{:S(2)}, u32[]{:S(2)}) collective-permute-start(bf16[432,128]{1,0:T(8,128)(2,1)S(1)} %fusion.33), channel_id=1, source_target_pairs={{0,192},{12,204},{24,216},{36,228},{48,240},{60,252},{72,264},{84,... | collective-permute-start | bytes 331784 | tf_op jit(solution)/shard_map/ppermute | solution.py:19
  100.8 8.4 %collective-permute-start.6 = (bf16[432,256]{1,0:T(8,128)(2,1)S(1)}, bf16[432,256]{1,0:T(8,128)(2,1)S(1)}, u32[]{:S(2)}, u32[]{:S(2)}) collective-permute-start(bf16[432,256]{1,0:T(8,128)(2,1)S(1)} %pad_maximum_fusion.4), channel_id=1, source_target_pairs={{0,96},{12,108},{24,120},{36,132},{48,144},{60,156},{72,168},{84,1... | collective-permute-start | bytes 663560 | tf_op jit(solution)/shard_map/ppermute | solution.py:19
  109.9 9.3 %collective-permute-start.7 = (bf16[432,512]{1,0:T(8,128)(2,1)S(1)}, bf16[432,512]{1,0:T(8,128)(2,1)S(1)}, u32[]{:S(2)}, u32[]{:S(2)}) collective-permute-start(bf16[432,512]{1,0:T(8,128)(2,1)S(1)} %slice.380), channel_id=1, source_target_pairs={{0,12},{12,0},{24,36},{36,24},{48,60},{60,48},{72,84},{84,72},{96,... | collective-permute-start | bytes 1327112 | tf_op jit(solution)/shard_map/ppermute | solution.py:19
  120.6 20.7 %all-to-all-start.1 = ((bf16[12,2,18,512]{3,1,2,0:T(2,128)(2,1)}), bf16[12,2,18,512]{3,1,2,0:T(2,128)(2,1)S(1)}, u32[]{:S(2)}, u32[]{:S(2)}) async-start(bf16[12,2,18,512]{3,1,2,0:T(2,128)(2,1)} %copy.88), calls=%async_computation.1 | async-start | bytes 884736 | tf_op jit(solution)/shard_map/all_to_all | solution.py:130
  130.9 26.4 %copy-start.2 = (bf16[2,96,224]{2,1,0:T(8,128)(2,1)S(1)}, bf16[2,96,224]{2,1,0:T(8,128)(2,1)}, u32[]{:S(2)}) copy-start(bf16[2,96,224]{2,1,0:T(8,128)(2,1)} %param.8) | copy-start | bytes 258052
  141.3 25.4 %copy-start.4 = (f32[224]{0:T(256)S(1)}, f32[224]{0:T(256)}, u32[]{:S(2)}) copy-start(f32[224]{0:T(256)} %param.9) | copy-start | bytes 2692
  141.8 15.5 %collective-permute-start.8 = (bf16[2,96,256]{2,1,0:T(8,128)(2,1)S(1)}, bf16[2,96,256]{2,1,0:T(8,128)(2,1)S(1)}, u32[]{:S(2)}, u32[]{:S(2)}) collective-permute-start(bf16[2,96,256]{2,1,0:T(8,128)(2,1)S(1)} %slice.385), channel_id=1, source_target_pairs={{0,24},{12,36},{24,0},{36,12},{48,72},{60,84},{72,48},{84,60},{96,... | collective-permute-start | bytes 294920 | tf_op jit(solution)/shard_map/ppermute | solution.py:19
  157.3 9.4 %collective-permute-start.9 = (bf16[2,96,224]{2,1,0:T(8,128)(2,1)S(1)}, bf16[2,96,224]{2,1,0:T(8,128)(2,1)S(1)}, u32[]{:S(2)}, u32[]{:S(2)}) collective-permute-start(bf16[2,96,224]{2,1,0:T(8,128)(2,1)S(1)} %fusion.36), channel_id=1, source_target_pairs={{0,384},{12,396},{24,408},{36,420},{48,432},{60,444},{72,456},{84,... | collective-permute-start | bytes 258056 | tf_op jit(solution)/shard_map/ppermute | solution.py:24
  167.2 8.1 %collective-permute-start.10 = (bf16[2,96,256]{2,1,0:T(8,128)(2,1)S(1)}, bf16[2,96,256]{2,1,0:T(8,128)(2,1)S(1)}, u32[]{:S(2)}, u32[]{:S(2)}) collective-permute-start(bf16[2,96,256]{2,1,0:T(8,128)(2,1)S(1)} %pad_maximum_fusion.6), channel_id=1, source_target_pairs={{0,24},{12,36},{24,0},{36,12},{48,72},{60,84},{72,48},{84,60},{96,... | collective-permute-start | bytes 294920 | tf_op jit(solution)/shard_map/ppermute | solution.py:19
  188.0 8.8 %collective-permute-start.11 = (bf16[432,512]{1,0:T(8,128)(2,1)S(1)}, bf16[432,512]{1,0:T(8,128)(2,1)S(1)}, u32[]{:S(2)}, u32[]{:S(2)}) collective-permute-start(bf16[432,512]{1,0:T(8,128)(2,1)S(1)} %reshape.220), channel_id=1, source_target_pairs={{0,12},{12,0},{24,36},{36,24},{48,60},{60,48},{72,84},{84,72},{96,... | collective-permute-start | bytes 1327112 | tf_op jit(solution)/shard_map/ppermute | solution.py:19
  200.1 14.4 %collective-permute-start.12 = (bf16[448,512]{1,0:T(8,128)(2,1)S(1)}, bf16[448,512]{1,0:T(8,128)(2,1)S(1)}, u32[]{:S(2)}, u32[]{:S(2)}) collective-permute-start(bf16[448,512]{1,0:T(8,128)(2,1)S(1)} %fusion.7), channel_id=1, source_target_pairs={{0,96},{12,108},{24,120},{36,132},{48,144},{60,156},{72,168},{84,1... | collective-permute-start | bytes 1376264 | tf_op jit(solution)/shard_map/ppermute | solution.py:19
  214.9 14.3 %collective-permute-start.13 = (bf16[448,256]{1,0:T(8,128)(2,1)S(1)}, bf16[448,256]{1,0:T(8,128)(2,1)S(1)}, u32[]{:S(2)}, u32[]{:S(2)}) collective-permute-start(bf16[448,256]{1,0:T(8,128)(2,1)S(1)} %pad_maximum_fusion.2), channel_id=1, source_target_pairs={{0,192},{12,204},{24,216},{36,228},{48,240},{60,252},{72,264},{84,... | collective-permute-start | bytes 688136 | tf_op jit(solution)/shard_map/ppermute | solution.py:19
  229.4 21.7 %collective-permute-start.14 = (bf16[448,256]{1,0:T(8,128)(2,1)S(1)}, bf16[448,256]{1,0:T(8,128)(2,1)S(1)}, u32[]{:S(2)}, u32[]{:S(2)}) collective-permute-start(bf16[448,256]{1,0:T(8,128)(2,1)S(1)} %pad_maximum_fusion.3), channel_id=1, source_target_pairs={{0,48},{12,60},{24,72},{36,84},{48,0},{60,12},{72,24},{84,36},{96,... | collective-permute-start | bytes 688136 | tf_op jit(solution)/shard_map/ppermute | solution.py:19
  251.5 6.4 %collective-permute-start.15 = (bf16[432,128]{1,0:T(8,128)(2,1)S(1)}, bf16[432,128]{1,0:T(8,128)(2,1)S(1)}, u32[]{:S(2)}, u32[]{:S(2)}) collective-permute-start(bf16[432,128]{1,0:T(8,128)(2,1)S(1)} %fusion.32), channel_id=1, source_target_pairs={{0,192},{12,204},{24,216},{36,228},{48,240},{60,252},{72,264},{84,... | collective-permute-start | bytes 331784 | tf_op jit(solution)/shard_map/ppermute | solution.py:19
  257.9 10.0 %collective-permute-start.16 = (bf16[432,256]{1,0:T(8,128)(2,1)S(1)}, bf16[432,256]{1,0:T(8,128)(2,1)S(1)}, u32[]{:S(2)}, u32[]{:S(2)}) collective-permute-start(bf16[432,256]{1,0:T(8,128)(2,1)S(1)} %pad_maximum_fusion.5), channel_id=1, source_target_pairs={{0,96},{12,108},{24,120},{36,132},{48,144},{60,156},{72,168},{84,1... | collective-permute-start | bytes 663560 | tf_op jit(solution)/shard_map/ppermute | solution.py:19
  268.6 6.4 %collective-permute-start.17 = (bf16[432,512]{1,0:T(8,128)(2,1)S(1)}, bf16[432,512]{1,0:T(8,128)(2,1)S(1)}, u32[]{:S(2)}, u32[]{:S(2)}) collective-permute-start(bf16[432,512]{1,0:T(8,128)(2,1)S(1)} %slice.378), channel_id=1, source_target_pairs={{0,12},{12,0},{24,36},{36,24},{48,60},{60,48},{72,84},{84,72},{96,... | collective-permute-start | bytes 1327112 | tf_op jit(solution)/shard_map/ppermute | solution.py:19
  290.2 19.9 %collective-permute-start.18 = (bf16[2,96,256]{2,1,0:T(8,128)(2,1)S(1)}, bf16[2,96,256]{2,1,0:T(8,128)(2,1)S(1)}, u32[]{:S(2)}, u32[]{:S(2)}) collective-permute-start(bf16[2,96,256]{2,1,0:T(8,128)(2,1)S(1)} %slice.384), channel_id=1, source_target_pairs={{0,24},{12,36},{24,0},{36,12},{48,72},{60,84},{72,48},{84,60},{96,... | collective-permute-start | bytes 294920 | tf_op jit(solution)/shard_map/ppermute | solution.py:19

commit v2 on v1

--- a/solution.py
+++ b/solution.py
@@ -10,7 +10,9 @@
 EPS = 1e-06
 ROUTE_SCALE = 2.5
 LANES = 256
-SQ_TILE = 16
+SQ_TILE = 8
+LEAD = 2
+TIE = True
 DOT_ROWS = (((1,), (1,)), ((), ()))
 
 
@@ -72,72 +74,114 @@
     return jnp.sum(chosen, axis=2).astype(jnp.bfloat16), mix
 
 
+def tied(x, *others):
+    return lax.optimization_barrier((x, *others))[0]
+
+
 def layer(state, spread, mix, gain, w_in, w_out, expert_count, capacity):
-    lead, rows, cols = state.shape
+    rows, cols = state.shape
+    slots = expert_count * capacity
     values = state.astype(jnp.float32)
-    squares = jnp.sum(values * values, axis=2, keepdims=True)
+    squares = jnp.sum(values * values, axis=1, keepdims=True)
     high = squares.astype(jnp.bfloat16)
     low = (squares - high.astype(jnp.float32)).astype(jnp.bfloat16)
-    tail = jnp.zeros((lead, rows, LANES - cols - 2), jnp.bfloat16)
-    prepared = jnp.concatenate([(values * gain).astype(jnp.bfloat16), high, low, tail], axis=2)
-    both = jnp.concatenate([prepared, exchange(prepared, 1)], axis=2)
-    buffer = jnp.einsum("nrs,nrc->nsc", spread, both, preferred_element_type=jnp.float32)
-    buffer = buffer.astype(jnp.bfloat16).reshape(lead, expert_count, capacity, 2 * LANES)
-    arrived = lax.all_to_all(
-        buffer.transpose(1, 0, 2, 3), "expert", split_axis=0, concat_axis=0, tiled=True
-    )
-    slots = expert_count * lead * capacity
+    tail = jnp.zeros((rows, LANES - cols - 2), jnp.bfloat16)
+    prepared = jnp.concatenate([(values * gain).astype(jnp.bfloat16), high, low, tail], axis=1)
+    prepared = yield "gather", prepared
+    both = jnp.concatenate([prepared, exchange(prepared, 1)], axis=1)
+    buffer = lax.dot_general(
+        spread, both, (((0,), (0,)), ((), ())), preferred_element_type=jnp.float32
+    ).astype(jnp.bfloat16)
+    buffer = yield "dispatch", buffer.reshape(expert_count, capacity, 2 * LANES)
+    arrived = lax.all_to_all(buffer, "expert", split_axis=0, concat_axis=0, tiled=True)
     arrived = arrived.reshape(slots, 2 * LANES)
+    arrived = yield "cores", arrived
     inputs = jnp.concatenate([arrived, exchange(arrived, 0)], axis=1)
     lane = jnp.arange(4 * LANES) % LANES
     marks = ((lane == cols) | (lane == cols + 1)).astype(jnp.bfloat16)
     marks = jnp.broadcast_to(marks[None], (SQ_TILE, 4 * LANES))
-    half = LANES
-    sums = [
-        lax.dot_general(marks, part, DOT_ROWS, preferred_element_type=jnp.float32)
-        for part in (inputs[:half], inputs[half:])
-    ]
-    sums[1] = jnp.pad(sums[1], ((0, 0), (0, 2 * half - slots)))
-    index = jnp.arange(SQ_TILE)[:, None]
-    sums = jnp.where(index == 0, sums[0], jnp.where(index == 1, sums[1], 0.0))
+    sums = lax.dot_general(marks, inputs, DOT_ROWS, preferred_element_type=jnp.float32)
     partial = jnp.dot(inputs, w_in, preferred_element_type=jnp.float32)
     width = partial.shape[1]
-    for bit in (3, 4):
+    for name, bit in (("near", 3), ("far", 4)):
         width //= 2
         message = jnp.concatenate(
             [
                 partial[:, width:].astype(jnp.bfloat16),
-                jnp.pad(sums, ((0, 0), (0, width - half))).astype(jnp.bfloat16),
+                jnp.pad(sums, ((0, 0), (0, width - slots))).astype(jnp.bfloat16),
             ],
             axis=0,
         )
+        message = yield name, message
         got = exchange(message, bit).astype(jnp.float32)
         partial = partial[:, :width] + got[:slots]
-        sums = sums + got[slots:, :half]
-    message = jnp.concatenate([partial, sums], axis=0).astype(jnp.bfloat16)
+        sums = sums + got[slots:, :slots]
+    message = jnp.concatenate([partial, jnp.pad(sums, ((0, 0), (0, width - slots)))], axis=0)
+    message = yield "across", message.astype(jnp.bfloat16)
     got = exchange(message, 2).astype(jnp.float32)
     partial = partial + got[:slots]
-    sums = sums + got[slots:]
-    scaling = lax.rsqrt(jnp.concatenate([sums[0], sums[1, : slots - half]]) / D + EPS)[:, None]
+    sums = sums[0] + got[slots, :slots]
+    scaling = lax.rsqrt(sums / D + EPS)[:, None]
     projected = partial * scaling
     activated = (jax.nn.silu(projected[:, :128]) * projected[:, 128:]).astype(jnp.bfloat16)
-    for bit in (4, 3):
+    for name, bit in (("hidden_far", 4), ("hidden_near", 3)):
+        activated = yield name, activated
         activated = jnp.concatenate([activated, exchange(activated, bit)], axis=1)
     partial = lax.dot_general(activated, w_out, DOT_ROWS, preferred_element_type=jnp.float32)
-    got = exchange(partial[:, 2 * LANES :].astype(jnp.bfloat16), 0)
+    message = yield "out_cores", partial[:, 2 * LANES :].astype(jnp.bfloat16)
+    got = exchange(message, 0)
     expert_out = (partial[:, : 2 * LANES] + got.astype(jnp.float32)).astype(jnp.bfloat16)
-    expert_out = expert_out.reshape(expert_count, lead, capacity, 2 * LANES)
+    expert_out = yield "back", expert_out.reshape(expert_count, capacity, 2 * LANES)
     returned = lax.all_to_all(expert_out, "expert", split_axis=0, concat_axis=0, tiled=True)
-    returned = returned.transpose(1, 0, 2, 3).reshape(lead, expert_count * capacity, 2 * LANES)
+    returned = returned.reshape(slots, 2 * LANES)
     mix_high = mix.astype(jnp.bfloat16)
     mix_low = (mix - mix_high.astype(jnp.float32)).astype(jnp.bfloat16)
     mixed = sum(
-        jnp.einsum("nrs,nsc->nrc", part, returned, preferred_element_type=jnp.float32)
-        for part in (mix_high, mix_low)
+        jnp.dot(part, returned, preferred_element_type=jnp.float32) for part in (mix_high, mix_low)
     )
-    got = exchange(mixed[:, :, LANES:].astype(jnp.bfloat16), 1)
-    mixed = mixed[:, :, :cols] + got[:, :, :cols].astype(jnp.float32)
+    message = yield "out_gather", mixed[:, LANES:].astype(jnp.bfloat16)
+    got = exchange(message, 1)
+    mixed = mixed[:, :cols] + got[:, :cols].astype(jnp.float32)
     return (values + mixed).astype(jnp.bfloat16)
+
+
+def window(state, direction, spreads, mixes, *rest):
+    ticks = len(spreads)
+    for tick in range(ticks):
+        state = yield from layer(state, spreads[tick][direction], mixes[tick][direction], *rest)
+        if tick + 1 < ticks:
+            state = yield "relay", state
+            state = other_section(state)
+    return state
+
+
+def interleaved(first, second, lead, tie):
+    outs, sent, turn, done = [None, None], [None, None], 0, 0
+    streams = [first, second]
+    alive = [True, True]
+    step = [0, 0]
+
+    def advance(which):
+        try:
+            if step[which] == 0:
+                name, message = next(streams[which])
+            else:
+                name, message = streams[which].send(sent[which])
+            other = sent[1 - which]
+            if tie and other is not None:
+                message = tied(message, other)
+            sent[which] = message
+            step[which] += 1
+        except StopIteration as end:
+            outs[which] = end.value
+            alive[which] = False
+
+    while alive[0] or alive[1]:
+        if alive[0]:
+            advance(0)
+        if alive[1] and (step[0] - step[1] >= lead or not alive[0]):
+            advance(1)
+    return outs
 
 
 def body(flowing, norm_gain, gate_up, down_proj, down_step, step_rate, routes, scores):
@@ -152,13 +196,16 @@
     route_here = lax.dynamic_index_in_dim(routes, section, 1, keepdims=False)
     score_here = lax.dynamic_index_in_dim(scores, section, 1, keepdims=False)
     ticks = routes.shape[0]
-    state = flowing
+    spreads, mixes = [], []
     for tick in range(ticks):
         spread, mix = routing(route_here[tick], score_here[tick], expert_count, capacity)
-        state = layer(state, spread, mix, norm_gain, w_in, w_out, expert_count, capacity)
-        if tick + 1 < ticks:
-            state = other_section(state)
-    return state
+        spreads.append(spread)
+        mixes.append(mix)
+    streams = [
+        window(flowing[d], d, spreads, mixes, norm_gain, w_in, w_out, expert_count, capacity)
+        for d in range(2)
+    ]
+    return jnp.stack(interleaved(*streams, LEAD, TIE))
 
 
 def solution(mesh):

time: 312 us -> 377 us (1.21); the launches traced: 311 us -> 370 us
  starting transfers between devices: 138 us -> 214 us
  waiting for transfers between devices: 117 us -> 78.3 us
  blocking collectives: 25.8 us -> 0 us
  other arithmetic: 7.67 us -> 31.4 us
  local copies, waits for them, and re-layouts: 7.78 us -> 24.8 us
  matrix products: 9.07 us -> 14.7 us
    ppermute x18 -> x36, starting transfers between devices: 112 us -> 158 us  [exchange(): return lax.ppermute(x, 'pipe', [(i, i ^ 1 << bit) for i in range(size)])]
    ppermute x18 -> x36, waiting for transfers between devices: 96.1 us -> 57.7 us  [exchange(): return lax.ppermute(x, 'pipe', [(i, i ^ 1 << bit) for i in range(size)])]
    all_to_all x2 -> x0, blocking collectives: 25.8 us -> none  [the longest x1 14.1 us: layer(): lax.all_to_all(expert_out, 'expert', split_axis=0, concat_axis=0, tiled=T...]
    all_to_all x1 -> x4, starting transfers between devices: 9.45 us -> 27.7 us  [layer(): lax.all_to_all(buffer, 'expert', split_axis=0, concat_axis=0, tiled=True)]
    all_to_all x1 -> x4, starting transfers between devices: 10.3 us -> 18.8 us  [layer(): lax.all_to_all(expert_out, 'expert', split_axis=0, concat_axis=0, tiled=T...]
    unnamed x14 -> x56, local copies, waits for them, and re-layouts: 0.34 us -> 7.46 us
    reshape x4 -> x12, local copies, waits for them, and re-layouts: 1.71 us -> 8.6 us  [the longest x4 3.21 us: layer(): buffer.reshape(expert_count, capacity, 2 * LANES)]
    another operation x12 -> x23, other arithmetic: 2.77 us -> 9.19 us
  transfers between devices with their start and end apart: 21 -> 46, of which waited for: 19 -> 22; matrix products, arithmetic and copies ran while one was open for 2% -> 12% of each run, Pallas kernels for 2% -> 1%
where the time goes in v2:
time: 377 us; the launch traced here: 370 us
  starting transfers between devices  214 us (57%)
  waiting for transfers between devices  78.3 us (21%)
  other arithmetic  31.4 us (8%)
  local copies, waits for them, and re-layouts  24.8 us (7%)
  matrix products  14.7 us (4%)
  Pallas kernels  5.1 us (1%)
    ppermute x36, starting transfers between devices, exchange(): return lax.ppermute(x, 'pipe', [(i, i ^ 1 << bit) for i in range(size)])  158 us
    ppermute x36, waiting for transfers between devices, exchange(): return lax.ppermute(x, 'pipe', [(i, i ^ 1 << bit) for i in range(size)])  57.7 us
    all_to_all x4, starting transfers between devices, layer(): lax.all_to_all(buffer, 'expert', split_axis=0, concat_axis=0, tiled=True)  27.7 us
    all_to_all x4, starting transfers between devices, layer(): lax.all_to_all(expert_out, 'expert', split_axis=0, concat_axis=0, tiled=T...  18.8 us
    all_to_all x4, waiting for transfers between devices, layer(): lax.all_to_all(expert_out, 'expert', split_axis=0, concat_axis=0, tiled=T...  10.4 us
    all_to_all x4, waiting for transfers between devices, layer(): lax.all_to_all(buffer, 'expert', split_axis=0, concat_axis=0, tiled=True)  10.2 us
    ppermute x2, starting transfers between devices, other_section(): lax.ppermute(x, 'pipe', [(i, (i + size // 2) % size) for i in range(size)])  9.21 us
    another operation x20, other arithmetic  7.68 us
  transfers between devices with their start and end apart: 46, of which 22 were waited for; matrix products, arithmetic and copies ran while one was open for 12% of the time, Pallas kernels for 1%

profile of v2, /device:TPU:1, one launch (start us, length us, event | category | flops | bytes accessed | tf_op | source)
XLA Modules:
  0.0 369.6 jit_solution(9065335111636369874)
XLA Ops:
  1.6 8.4 %collective-permute-start = (bf16[96,256]{1,0:T(8,128)(2,1)S(1)}, bf16[96,256]{1,0:T(8,128)(2,1)S(1)}, u32[]{:S(2)}, u32[]{:S(2)}) collective-permute-start(bf16[96,256]{1,0:T(8,128)(2,1)S(1)} %get-tuple-element.121), channel_id=1, source_target_pairs={{0,24},{12,36},{24,0},{36,12},{48,72},{60,84},{72,48},{84,60},{96,... | collective-permute-start | bytes 147464 | tf_op jit(solution)/shard_map/ppermute | solution.py:21
  17.1 8.9 %all-to-all-start = ((bf16[12,18,512]{2,1,0:T(8,128)(2,1)}), bf16[12,18,512]{2,1,0:T(8,128)(2,1)S(1)}, u32[]{:S(2)}, u32[]{:S(2)}) async-start(bf16[12,18,512]{2,1,0:T(8,128)(2,1)} %reshape.321), calls=%async_computation | async-start | bytes 589824 | tf_op jit(solution)/shard_map/all_to_all | solution.py:96
  26.0 2.6 collective-permute-start.2
  29.7 5.1 %shard_map.82 = (bf16[1024,1024]{1,0:T(8,128)(2,1)}, bf16[1024,512]{1,0:T(8,128)(2,1)}) custom-call(s32[2]{0:T(128)} %pad_add_fusion.where, bf16[896,1024]{1,0:T(8,128)(2,1)} %bitcast.135, bf16[896,512]{1,0:T(8,128)(2,1)} %bitcast.136, bf16[896,512]{1,0:T(8,128)(2,1)} %bitcast.137, f32[1]{0:T(128)} %bitcast.16.rate), custom_call_target="tpu_custom_call" | custom-call | flops 2000000 | bytes 8000000 | tf_op jit(solution)/shard_map/pallas_call | solution.py:52
  34.9 4.2 %collective-permute-start.1 = (bf16[216,512]{1,0:T(8,128)(2,1)S(1)}, bf16[216,512]{1,0:T(8,128)(2,1)S(1)}, u32[]{:S(2)}, u32[]{:S(2)}) collective-permute-start(bf16[216,512]{1,0:T(8,128)(2,1)S(1)} %reshape.322), channel_id=1, source_target_pairs={{0,12},{12,0},{24,36},{36,24},{48,60},{60,48},{72,84},{84,72},{96,... | collective-permute-start | bytes 663560 | tf_op jit(solution)/shard_map/ppermute | solution.py:21
  41.9 3.2 collective-permute-start.3
  45.1 7.2 %all-to-all-start.1 = ((bf16[12,18,512]{2,1,0:T(8,128)(2,1)}), bf16[12,18,512]{2,1,0:T(8,128)(2,1)S(1)}, u32[]{:S(2)}, u32[]{:S(2)}) async-start(bf16[12,18,512]{2,1,0:T(8,128)(2,1)} %reshape.323), calls=%async_computation.1 | async-start | bytes 589824 | tf_op jit(solution)/shard_map/all_to_all | solution.py:96
  55.2 5.3 %all-to-all-done.1 = bf16[12,18,512]{2,1,0:T(8,128)(2,1)S(1)} async-done(((bf16[12,18,512]{2,1,0:T(8,128)(2,1)}), bf16[12,18,512]{2,1,0:T(8,128)(2,1)S(1)}, u32[]{:S(2)}, u32[]{:S(2)}) %all-to-all-start.1) | async-done | bytes 221216 | tf_op jit(solution)/shard_map/all_to_all | solution.py:96
  60.6 4.2 %collective-permute-start.5 = (bf16[216,512]{1,0:T(8,128)(2,1)S(1)}, bf16[216,512]{1,0:T(8,128)(2,1)S(1)}, u32[]{:S(2)}, u32[]{:S(2)}) collective-permute-start(bf16[216,512]{1,0:T(8,128)(2,1)S(1)} %reshape.324), channel_id=1, source_target_pairs={{0,12},{12,0},{24,36},{36,24},{48,60},{60,48},{72,84},{84,72},{96,... | collective-permute-start | bytes 663560 | tf_op jit(solution)/shard_map/ppermute | solution.py:21
  64.8 4.2 %collective-permute-start.4 = (bf16[224,256]{1,0:T(8,128)(2,1)}, bf16[224,256]{1,0:T(8,128)(2,1)S(1)}, u32[]{:S(2)}, u32[]{:S(2)}) collective-permute-start(bf16[224,256]{1,0:T(8,128)(2,1)} %fusion.40), channel_id=1, source_target_pairs={{0,192},{12,204},{24,216},{36,228},{48,240},{60,252},{72,264},{84,... | collective-permute-start | bytes 344072 | tf_op jit(solution)/shard_map/ppermute | solution.py:21
  69.1 6.2 %collective-permute-done.4 = bf16[224,256]{1,0:T(8,128)(2,1)S(1)} collective-permute-done((bf16[224,256]{1,0:T(8,128)(2,1)}, bf16[224,256]{1,0:T(8,128)(2,1)S(1)}, u32[]{:S(2)}, u32[]{:S(2)}) %collective-permute-start.4) | collective-permute-done | bytes 114720 | tf_op jit(solution)/shard_map/ppermute | solution.py:21
  78.0 10.7 %collective-permute-start.6 = (bf16[224,256]{1,0:T(8,128)(2,1)S(1)}, bf16[224,256]{1,0:T(8,128)(2,1)S(1)}, u32[]{:S(2)}, u32[]{:S(2)}) collective-permute-start(bf16[224,256]{1,0:T(8,128)(2,1)S(1)} %fusion.42), channel_id=1, source_target_pairs={{0,48},{12,60},{24,72},{36,84},{48,0},{60,12},{72,24},{84,36},{96,... | collective-permute-start | bytes 344072 | tf_op jit(solution)/shard_map/ppermute | solution.py:21
  88.7 1.9 collective-permute-start.7
  92.0 5.1 %collective-permute-done.7 = bf16[224,512]{1,0:T(8,128)(2,1)S(1)} collective-permute-done((bf16[224,512]{1,0:T(8,128)(2,1)S(1)}, bf16[224,512]{1,0:T(8,128)(2,1)S(1)}, u32[]{:S(2)}, u32[]{:S(2)}) %collective-permute-start.7) | collective-permute-done | bytes 229408 | tf_op jit(solution)/shard_map/ppermute | solution.py:21
  98.1 2.4 collective-permute-start.8
  101.8 3.7 %collective-permute-start.9 = (bf16[224,256]{1,0:T(8,128)(2,1)S(1)}, bf16[224,256]{1,0:T(8,128)(2,1)S(1)}, u32[]{:S(2)}, u32[]{:S(2)}) collective-permute-start(bf16[224,256]{1,0:T(8,128)(2,1)S(1)} %fusion.41), channel_id=1, source_target_pairs={{0,192},{12,204},{24,216},{36,228},{48,240},{60,252},{72,264},{84,... | collective-permute-start | bytes 344072 | tf_op jit(solution)/shard_map/ppermute | solution.py:21
  105.5 1.5 pad_maximum_fusion
  107.0 2.4 collective-permute-done.9
  111.8 1.9 collective-permute-start.10
  114.0 5.0 %collective-permute-start.11 = (bf16[224,256]{1,0:T(8,128)(2,1)}, bf16[224,256]{1,0:T(8,128)(2,1)S(1)}, u32[]{:S(2)}, u32[]{:S(2)}) collective-permute-start(bf16[224,256]{1,0:T(8,128)(2,1)} %fusion.43), channel_id=1, source_target_pairs={{0,48},{12,60},{24,72},{36,84},{48,0},{60,12},{72,24},{84,36},{96,... | collective-permute-start | bytes 344072 | tf_op jit(solution)/shard_map/ppermute | solution.py:21
  122.1 4.3 %collective-permute-done.11 = bf16[224,256]{1,0:T(8,128)(2,1)S(1)} collective-permute-done((bf16[224,256]{1,0:T(8,128)(2,1)}, bf16[224,256]{1,0:T(8,128)(2,1)S(1)}, u32[]{:S(2)}, u32[]{:S(2)}) %collective-permute-start.11) | collective-permute-done | bytes 114720 | tf_op jit(solution)/shard_map/ppermute | solution.py:21
  126.6 4.5 %collective-permute-start.13 = (bf16[216,128]{1,0:T(8,128)(2,1)S(1)}, bf16[216,128]{1,0:T(8,128)(2,1)S(1)}, u32[]{:S(2)}, u32[]{:S(2)}) collective-permute-start(bf16[216,128]{1,0:T(8,128)(2,1)S(1)} %fusion.50), channel_id=1, source_target_pairs={{0,192},{12,204},{24,216},{36,228},{48,240},{60,252},{72,264},{84,... | collective-permute-start | bytes 165896 | tf_op jit(solution)/shard_map/ppermute | solution.py:21
  131.1 7.8 %collective-permute-start.12 = (bf16[216,512]{1,0:T(8,128)(2,1)}, bf16[216,512]{1,0:T(8,128)(2,1)}, u32[]{:S(2)}, u32[]{:S(2)}) collective-permute-start(bf16[216,512]{1,0:T(8,128)(2,1)} %slice.729), channel_id=1, source_target_pairs={{0,12},{12,0},{24,36},{36,24},{48,60},{60,48},{72,84},{84,72},{96,... | collective-permute-start | bytes 663560 | tf_op jit(solution)/shard_map/ppermute | solution.py:21
  142.3 4.2 %all-to-all-start.2 = ((bf16[12,18,512]{2,1,0:T(8,128)(2,1)}), bf16[12,18,512]{2,1,0:T(8,128)(2,1)}, u32[]{:S(2)}, u32[]{:S(2)}) async-start(bf16[12,18,512]{2,1,0:T(8,128)(2,1)} %reshape.325), calls=%async_computation.2 | async-start | bytes 589824 | tf_op jit(solution)/shard_map/all_to_all | solution.py:135
  146.7 3.2 collective-permute-start.14
  150.0 2.8 collective-permute-done.14
  155.9 4.7 %collective-permute-start.16 = (bf16[216,512]{1,0:T(8,128)(2,1)}, bf16[216,512]{1,0:T(8,128)(2,1)}, u32[]{:S(2)}, u32[]{:S(2)}) collective-permute-start(bf16[216,512]{1,0:T(8,128)(2,1)} %slice.728), channel_id=1, source_target_pairs={{0,12},{12,0},{24,36},{36,24},{48,60},{60,48},{72,84},{84,72},{96,... | collective-permute-start | bytes 663560 | tf_op jit(solution)/shard_map/ppermute | solution.py:21
  163.7 2.1 collective-permute-start.15
  167.7 3.2 collective-permute-done.15
  171.9 6.4 %collective-permute-start.17 = (bf16[96,224]{1,0:T(8,128)(2,1)S(1)}, bf16[96,224]{1,0:T(8,128)(2,1)S(1)}, u32[]{:S(2)}, u32[]{:S(2)}) collective-permute-start(bf16[96,224]{1,0:T(8,128)(2,1)S(1)} %fusion.60), channel_id=1, source_target_pairs={{0,384},{12,396},{24,408},{36,420},{48,432},{60,444},{72,456},{84,... | collective-permute-start | bytes 129032 | tf_op jit(solution)/shard_map/ppermute | solution.py:26
  179.2 7.4 %all-to-all-start.3 = ((bf16[12,18,512]{2,1,0:T(8,128)(2,1)}), bf16[12,18,512]{2,1,0:T(8,128)(2,1)}, u32[]{:S(2)}, u32[]{:S(2)}) async-start(bf16[12,18,512]{2,1,0:T(8,128)(2,1)} %reshape.327), calls=%async_computation.3 | async-start | bytes 589824 | tf_op jit(solution)/shard_map/all_to_all | solution.py:135
  187.3 7.2 %all-to-all-done.3 = bf16[12,18,512]{2,1,0:T(8,128)(2,1)} async-done(((bf16[12,18,512]{2,1,0:T(8,128)(2,1)}), bf16[12,18,512]{2,1,0:T(8,128)(2,1)}, u32[]{:S(2)}, u32[]{:S(2)}) %all-to-all-start.3) | async-done | bytes 221216 | tf_op jit(solution)/shard_map/all_to_all | solution.py:135
  197.7 6.0 %collective-permute-start.19 = (bf16[96,256]{1,0:T(8,128)(2,1)S(1)}, bf16[96,256]{1,0:T(8,128)(2,1)S(1)}, u32[]{:S(2)}, u32[]{:S(2)}) collective-permute-start(bf16[96,256]{1,0:T(8,128)(2,1)S(1)} %slice.738), channel_id=1, source_target_pairs={{0,24},{12,36},{24,0},{36,12},{48,72},{60,84},{72,48},{84,60},{96,... | collective-permute-start | bytes 147464 | tf_op jit(solution)/shard_map/ppermute | solution.py:21
  203.8 1.9 collective-permute-start.18
  206.6 2.8 collective-permute-start.20
  212.3 4.2 %all-to-all-start.4 = ((bf16[12,18,512]{2,1,0:T(8,128)(2,1)}), bf16[12,18,512]{2,1,0:T(8,128)(2,1)S(1)}, u32[]{:S(2)}, u32[]{:S(2)}) async-start(bf16[12,18,512]{2,1,0:T(8,128)(2,1)} %reshape.331), calls=%async_computation.4 | async-start | bytes 589824 | tf_op jit(solution)/shard_map/all_to_all | solution.py:96
  218.2 1.4 pad_maximum_fusion.4
  219.7 4.5 %collective-permute-start.22 = (bf16[96,256]{1,0:T(8,128)(2,1)}, bf16[96,256]{1,0:T(8,128)(2,1)S(1)}, u32[]{:S(2)}, u32[]{:S(2)}) collective-permute-start(bf16[96,256]{1,0:T(8,128)(2,1)} %pad_maximum_fusion.4), channel_id=1, source_target_pairs={{0,24},{12,36},{24,0},{36,12},{48,72},{60,84},{72,48},{84,60},{96,... | collective-permute-start | bytes 147464 | tf_op jit(solution)/shard_map/ppermute | solution.py:21
  224.9 6.7 %collective-permute-start.21 = (bf16[216,512]{1,0:T(8,128)(2,1)}, bf16[216,512]{1,0:T(8,128)(2,1)}, u32[]{:S(2)}, u32[]{:S(2)}) collective-permute-start(bf16[216,512]{1,0:T(8,128)(2,1)} %reshape.332), channel_id=1, source_target_pairs={{0,12},{12,0},{24,36},{36,24},{48,60},{60,48},{72,84},{84,72},{96,... | collective-permute-start | bytes 663560 | tf_op jit(solution)/shard_map/ppermute | solution.py:21
  237.8 2.2 collective-permute-start.23
  240.0 7.4 %all-to-all-start.5 = ((bf16[12,18,512]{2,1,0:T(8,128)(2,1)}), bf16[12,18,512]{2,1,0:T(8,128)(2,1)S(1)}, u32[]{:S(2)}, u32[]{:S(2)}) async-start(bf16[12,18,512]{2,1,0:T(8,128)(2,1)} %reshape.333), calls=%async_computation.5 | async-start | bytes 589824 | tf_op jit(solution)/shard_map/all_to_all | solution.py:96
  251.1 4.9 %all-to-all-done.5 = bf16[12,18,512]{2,1,0:T(8,128)(2,1)S(1)} async-done(((bf16[12,18,512]{2,1,0:T(8,128)(2,1)}), bf16[12,18,512]{2,1,0:T(8,128)(2,1)S(1)}, u32[]{:S(2)}, u32[]{:S(2)}) %all-to-all-start.5) | async-done | bytes 221216 | tf_op jit(solution)/shard_map/all_to_all | solution.py:96
  256.8 3.8 %collective-permute-start.25 = (bf16[216,512]{1,0:T(8,128)(2,1)}, bf16[216,512]{1,0:T(8,128)(2,1)S(1)}, u32[]{:S(2)}, u32[]{:S(2)}) collective-permute-start(bf16[216,512]{1,0:T(8,128)(2,1)} %reshape.334), channel_id=1, source_target_pairs={{0,12},{12,0},{24,36},{36,24},{48,60},{60,48},{72,84},{84,72},{96,... | collective-permute-start | bytes 663560 | tf_op jit(solution)/shard_map/ppermute | solution.py:21
  260.6 4.0 %collective-permute-start.24 = (bf16[224,256]{1,0:T(8,128)(2,1)}, bf16[224,256]{1,0:T(8,128)(2,1)S(1)}, u32[]{:S(2)}, u32[]{:S(2)}) collective-permute-start(bf16[224,256]{1,0:T(8,128)(2,1)} %fusion.44), channel_id=1, source_target_pairs={{0,192},{12,204},{24,216},{36,228},{48,240},{60,252},{72,264},{84,... | collective-permute-start | bytes 344072 | tf_op jit(solution)/shard_map/ppermute | solution.py:21
  265.6 5.2 %collective-permute-done.24 = bf16[224,256]{1,0:T(8,128)(2,1)S(1)} collective-permute-done((bf16[224,256]{1,0:T(8,128)(2,1)}, bf16[224,256]{1,0:T(8,128)(2,1)S(1)}, u32[]{:S(2)}, u32[]{:S(2)}) %collective-permute-start.24) | collective-permute-done | bytes 114720 | tf_op jit(solution)/shard_map/ppermute | solution.py:21
  273.5 7.1 %collective-permute-start.26 = (bf16[224,256]{1,0:T(8,128)(2,1)S(1)}, bf16[224,256]{1,0:T(8,128)(2,1)S(1)}, u32[]{:S(2)}, u32[]{:S(2)}) collective-permute-start(bf16[224,256]{1,0:T(8,128)(2,1)S(1)} %fusion.46), channel_id=1, source_target_pairs={{0,48},{12,60},{24,72},{36,84},{48,0},{60,12},{72,24},{84,36},{96,... | collective-permute-start | bytes 344072 | tf_op jit(solution)/shard_map/ppermute | solution.py:21
  280.6 1.9 collective-permute-start.27
  282.5 9.0 %collective-permute-done.26 = bf16[224,256]{1,0:T(8,128)(2,1)S(1)} collective-permute-done((bf16[224,256]{1,0:T(8,128)(2,1)S(1)}, bf16[224,256]{1,0:T(8,128)(2,1)S(1)}, u32[]{:S(2)}, u32[]{:S(2)}) %collective-permute-start.26) | collective-permute-done | bytes 114720 | tf_op jit(solution)/shard_map/ppermute | solution.py:21
  291.9 1.9 collective-permute-start.28
  293.8 4.3 %collective-permute-start.29 = (bf16[224,256]{1,0:T(8,128)(2,1)S(1)}, bf16[224,256]{1,0:T(8,128)(2,1)S(1)}, u32[]{:S(2)}, u32[]{:S(2)}) collective-permute-start(bf16[224,256]{1,0:T(8,128)(2,1)S(1)} %fusion.45), channel_id=1, source_target_pairs={{0,192},{12,204},{24,216},{36,228},{48,240},{60,252},{72,264},{84,... | collective-permute-start | bytes 344072 | tf_op jit(solution)/shard_map/ppermute | solution.py:21
  298.7 2.0 collective-permute-done.29
  300.8 3.6 collective-permute-start.30
  304.4 6.9 %collective-permute-start.31 = (bf16[224,256]{1,0:T(8,128)(2,1)S(1)}, bf16[224,256]{1,0:T(8,128)(2,1)S(1)}, u32[]{:S(2)}, u32[]{:S(2)}) collective-permute-start(bf16[224,256]{1,0:T(8,128)(2,1)S(1)} %fusion.47), channel_id=1, source_target_pairs={{0,48},{12,60},{24,72},{36,84},{48,0},{60,12},{72,24},{84,36},{96,... | collective-permute-start | bytes 344072 | tf_op jit(solution)/shard_map/ppermute | solution.py:21
  311.8 9.1 %collective-permute-done.31 = bf16[224,256]{1,0:T(8,128)(2,1)S(1)} collective-permute-done((bf16[224,256]{1,0:T(8,128)(2,1)S(1)}, bf16[224,256]{1,0:T(8,128)(2,1)S(1)}, u32[]{:S(2)}, u32[]{:S(2)}) %collective-permute-start.31) | collective-permute-done | bytes 114720 | tf_op jit(solution)/shard_map/ppermute | solution.py:21
  321.1 2.8 collective-permute-start.32
  324.0 3.8 %collective-permute-start.33 = (bf16[216,128]{1,0:T(8,128)(2,1)S(1)}, bf16[216,128]{1,0:T(8,128)(2,1)S(1)}, u32[]{:S(2)}, u32[]{:S(2)}) collective-permute-start(bf16[216,128]{1,0:T(8,128)(2,1)S(1)} %fusion.48), channel_id=1, source_target_pairs={{0,192},{12,204},{24,216},{36,228},{48,240},{60,252},{72,264},{84,... | collective-permute-start | bytes 165896 | tf_op jit(solution)/shard_map/ppermute | solution.py:21
  327.7 2.4 collective-permute-done.33
  330.2 3.4 collective-permute-start.34
  334.4 3.5 all-to-all-start.6
  338.6 2.9 collective-permute-start.36
  343.4 2.6 all-to-all-done.6
  346.5 3.6 all-to-all-start.7
  350.1 7.1 %collective-permute-start.35 = (bf16[96,256]{1,0:T(8,128)(2,1)S(1)}, bf16[96,256]{1,0:T(8,128)(2,1)S(1)}, u32[]{:S(2)}, u32[]{:S(2)}) collective-permute-start(bf16[96,256]{1,0:T(8,128)(2,1)S(1)} %slice.737), channel_id=1, source_target_pairs={{0,24},{12,36},{24,0},{36,12},{48,72},{60,84},{72,48},{84,60},{96,... | collective-permute-start | bytes 147464 | tf_op jit(solution)/shard_map/ppermute | solution.py:21
  358.3 8.3 %collective-permute-start.37 = (bf16[96,256]{1,0:T(8,128)(2,1)S(1)}, bf16[96,256]{1,0:T(8,128)(2,1)S(1)}, u32[]{:S(2)}, u32[]{:S(2)}) collective-permute-start(bf16[96,256]{1,0:T(8,128)(2,1)S(1)} %slice.736), channel_id=1, source_target_pairs={{0,24},{12,36},{24,0},{36,12},{48,72},{60,84},{72,48},{84,60},{96,... | collective-permute-start | bytes 147464 | tf_op jit(solution)/shard_map/ppermute | solution.py:21
  (272 shorter events, 74.5 us)
Async XLA Ops:
  0.0 29.2 %copy-start = (f32[1,2]{1,0:T(1,128)S(1)}, f32[1,2]{1,0:T(1,128)}, u32[]{:S(2)}) copy-start(f32[1,2]{1,0:T(1,128)} %param.13) | copy-start | bytes 28
  1.5 14.5 %copy-start.16 = (bf16[96,30]{1,0:T(8,128)(2,1)}, bf16[96,30]{1,0:T(8,128)(2,1)S(1)}, u32[]{:S(2)}) copy-start(bf16[96,30]{1,0:T(8,128)(2,1)S(1)} %broadcast.191) | copy-start | bytes 17284
  1.6 14.3 %collective-permute-start = (bf16[96,256]{1,0:T(8,128)(2,1)S(1)}, bf16[96,256]{1,0:T(8,128)(2,1)S(1)}, u32[]{:S(2)}, u32[]{:S(2)}) collective-permute-start(bf16[96,256]{1,0:T(8,128)(2,1)S(1)} %get-tuple-element.121), channel_id=1, source_target_pairs={{0,24},{12,36},{24,0},{36,12},{48,72},{60,84},{72,48},{84,60},{96,... | collective-permute-start | bytes 147464 | tf_op jit(solution)/shard_map/ppermute | solution.py:21
  17.1 17.8 %all-to-all-start = ((bf16[12,18,512]{2,1,0:T(8,128)(2,1)}), bf16[12,18,512]{2,1,0:T(8,128)(2,1)S(1)}, u32[]{:S(2)}, u32[]{:S(2)}) async-start(bf16[12,18,512]{2,1,0:T(8,128)(2,1)} %reshape.321), calls=%async_computation | async-start | bytes 589824 | tf_op jit(solution)/shard_map/all_to_all | solution.py:96
  26.0 13.2 %collective-permute-start.2 = (bf16[96,256]{1,0:T(8,128)(2,1)S(1)}, bf16[96,256]{1,0:T(8,128)(2,1)S(1)}, u32[]{:S(2)}, u32[]{:S(2)}) collective-permute-start(bf16[96,256]{1,0:T(8,128)(2,1)S(1)} %get-tuple-element.51), channel_id=1, source_target_pairs={{0,24},{12,36},{24,0},{36,12},{48,72},{60,84},{72,48},{84,60},{96,... | collective-permute-start | bytes 147464 | tf_op jit(solution)/shard_map/ppermute | solution.py:21
  34.9 5.4 %copy-start.1 = (bf16[1024,1024]{1,0:T(8,128)(2,1)S(1)}, bf16[1024,1024]{1,0:T(8,128)(2,1)}, u32[]{:S(2)}) copy-start(bf16[1024,1024]{1,0:T(8,128)(2,1)} %get-tuple-element.53) | copy-start | bytes 6291460
  34.9 5.3 %collective-permute-start.1 = (bf16[216,512]{1,0:T(8,128)(2,1)S(1)}, bf16[216,512]{1,0:T(8,128)(2,1)S(1)}, u32[]{:S(2)}, u32[]{:S(2)}) collective-permute-start(bf16[216,512]{1,0:T(8,128)(2,1)S(1)} %reshape.322), channel_id=1, source_target_pairs={{0,12},{12,0},{24,36},{36,24},{48,60},{60,48},{72,84},{84,72},{96,... | collective-permute-start | bytes 663560 | tf_op jit(solution)/shard_map/ppermute | solution.py:21
  41.9 10.7 %collective-permute-start.3 = (bf16[224,512]{1,0:T(8,128)(2,1)}, bf16[224,512]{1,0:T(8,128)(2,1)}, u32[]{:S(2)}, u32[]{:S(2)}) collective-permute-start(bf16[224,512]{1,0:T(8,128)(2,1)} %fusion.8), channel_id=1, source_target_pairs={{0,96},{12,108},{24,120},{36,132},{48,144},{60,156},{72,168},{84,1... | collective-permute-start | bytes 688136 | tf_op jit(solution)/shard_map/ppermute | solution.py:21
  45.1 15.4 %all-to-all-start.1 = ((bf16[12,18,512]{2,1,0:T(8,128)(2,1)}), bf16[12,18,512]{2,1,0:T(8,128)(2,1)S(1)}, u32[]{:S(2)}, u32[]{:S(2)}) async-start(bf16[12,18,512]{2,1,0:T(8,128)(2,1)} %reshape.323), calls=%async_computation.1 | async-start | bytes 589824 | tf_op jit(solution)/shard_map/all_to_all | solution.py:96
  52.6 36.1 %copy-start.21 = (s32[2,192]{1,0:T(2,128)}, s32[2,192]{1,0:T(2,128)S(1)}, u32[]{:S(2)}) copy-start(s32[2,192]{1,0:T(2,128)S(1)} %eq.119) | copy-start | bytes 4612
  53.6 1.0 copy-start.13
  60.6 16.4 %collective-permute-start.5 = (bf16[216,512]{1,0:T(8,128)(2,1)S(1)}, bf16[216,512]{1,0:T(8,128)(2,1)S(1)}, u32[]{:S(2)}, u32[]{:S(2)}) collective-permute-start(bf16[216,512]{1,0:T(8,128)(2,1)S(1)} %reshape.324), channel_id=1, source_target_pairs={{0,12},{12,0},{24,36},{36,24},{48,60},{60,48},{72,84},{84,72},{96,... | collective-permute-start | bytes 663560 | tf_op jit(solution)/shard_map/ppermute | solution.py:21
  64.8 10.5 %collective-permute-start.4 = (bf16[224,256]{1,0:T(8,128)(2,1)}, bf16[224,256]{1,0:T(8,128)(2,1)S(1)}, u32[]{:S(2)}, u32[]{:S(2)}) collective-permute-start(bf16[224,256]{1,0:T(8,128)(2,1)} %fusion.40), channel_id=1, source_target_pairs={{0,192},{12,204},{24,216},{36,228},{48,240},{60,252},{72,264},{84,... | collective-permute-start | bytes 344072 | tf_op jit(solution)/shard_map/ppermute | solution.py:21
  77.1 14.7 %copy-start.11 = (f32[216,512]{1,0:T(8,128)S(1)}, f32[216,512]{1,0:T(8,128)}, u32[]{:S(2)}) copy-start(f32[216,512]{1,0:T(8,128)} %copy-done.10) | copy-start | bytes 1327108
  78.0 13.7 %collective-permute-start.6 = (bf16[224,256]{1,0:T(8,128)(2,1)S(1)}, bf16[224,256]{1,0:T(8,128)(2,1)S(1)}, u32[]{:S(2)}, u32[]{:S(2)}) collective-permute-start(bf16[224,256]{1,0:T(8,128)(2,1)S(1)} %fusion.42), channel_id=1, source_target_pairs={{0,48},{12,60},{24,72},{36,84},{48,0},{60,12},{72,24},{84,36},{96,... | collective-permute-start | bytes 344072 | tf_op jit(solution)/shard_map/ppermute | solution.py:21
  88.7 8.3 %collective-permute-start.7 = (bf16[224,512]{1,0:T(8,128)(2,1)S(1)}, bf16[224,512]{1,0:T(8,128)(2,1)S(1)}, u32[]{:S(2)}, u32[]{:S(2)}) collective-permute-start(bf16[224,512]{1,0:T(8,128)(2,1)S(1)} %fusion.9), channel_id=1, source_target_pairs={{0,96},{12,108},{24,120},{36,132},{48,144},{60,156},{72,168},{84,1... | collective-permute-start | bytes 688136 | tf_op jit(solution)/shard_map/ppermute | solution.py:21
  91.9 27.1 %copy-start.2 = (bf16[1024,512]{1,0:T(8,128)(2,1)S(1)}, bf16[1024,512]{1,0:T(8,128)(2,1)}, u32[]{:S(2)}) copy-start(bf16[1024,512]{1,0:T(8,128)(2,1)} %get-tuple-element.64) | copy-start | bytes 3145732
  97.1 1.0 copy-start.12
  98.1 7.4 %collective-permute-start.8 = (bf16[216,128]{1,0:T(8,128)(2,1)S(1)}, bf16[216,128]{1,0:T(8,128)(2,1)}, u32[]{:S(2)}, u32[]{:S(2)}) collective-permute-start(bf16[216,128]{1,0:T(8,128)(2,1)S(1)} %fusion.51), channel_id=1, source_target_pairs={{0,192},{12,204},{24,216},{36,228},{48,240},{60,252},{72,264},{84,... | collective-permute-start | bytes 165896 | tf_op jit(solution)/shard_map/ppermute | solution.py:21
  101.8 7.7 %collective-permute-start.9 = (bf16[224,256]{1,0:T(8,128)(2,1)S(1)}, bf16[224,256]{1,0:T(8,128)(2,1)S(1)}, u32[]{:S(2)}, u32[]{:S(2)}) collective-permute-start(bf16[224,256]{1,0:T(8,128)(2,1)S(1)} %fusion.41), channel_id=1, source_target_pairs={{0,192},{12,204},{24,216},{36,228},{48,240},{60,252},{72,264},{84,... | collective-permute-start | bytes 344072 | tf_op jit(solution)/shard_map/ppermute | solution.py:21
  111.8 7.2 %collective-permute-start.10 = (bf16[216,256]{1,0:T(8,128)(2,1)}, bf16[216,256]{1,0:T(8,128)(2,1)}, u32[]{:S(2)}, u32[]{:S(2)}) collective-permute-start(bf16[216,256]{1,0:T(8,128)(2,1)} %pad_maximum_fusion), channel_id=1, source_target_pairs={{0,96},{12,108},{24,120},{36,132},{48,144},{60,156},{72,168},{84,1... | collective-permute-start | bytes 331784 | tf_op jit(solution)/shard_map/ppermute | solution.py:21
  114.0 12.4 %copy-start.7 = (f32[216,512]{1,0:T(8,128)S(1)}, f32[216,512]{1,0:T(8,128)}, u32[]{:S(2)}) copy-start(f32[216,512]{1,0:T(8,128)} %copy-done.6) | copy-start | bytes 1327108
  114.0 12.4 %collective-permute-start.11 = (bf16[224,256]{1,0:T(8,128)(2,1)}, bf16[224,256]{1,0:T(8,128)(2,1)S(1)}, u32[]{:S(2)}, u32[]{:S(2)}) collective-permute-start(bf16[224,256]{1,0:T(8,128)(2,1)} %fusion.43), channel_id=1, source_target_pairs={{0,48},{12,60},{24,72},{36,84},{48,0},{60,12},{72,24},{84,36},{96,... | collective-permute-start | bytes 344072 | tf_op jit(solution)/shard_map/ppermute | solution.py:21
  121.4 25.1 %copy-start.22 = (s32[2,192]{1,0:T(2,128)S(1)}, s32[2,192]{1,0:T(2,128)}, u32[]{:S(2)}) copy-start(s32[2,192]{1,0:T(2,128)} %copy-done.21) | copy-start | bytes 4612
  126.6 12.5 %collective-permute-start.13 = (bf16[216,128]{1,0:T(8,128)(2,1)S(1)}, bf16[216,128]{1,0:T(8,128)(2,1)S(1)}, u32[]{:S(2)}, u32[]{:S(2)}) collective-permute-start(bf16[216,128]{1,0:T(8,128)(2,1)S(1)} %fusion.50), channel_id=1, source_target_pairs={{0,192},{12,204},{24,216},{36,228},{48,240},{60,252},{72,264},{84,... | collective-permute-start | bytes 165896 | tf_op jit(solution)/shard_map/ppermute | solution.py:21
  131.1 9.3 %collective-permute-start.12 = (bf16[216,512]{1,0:T(8,128)(2,1)}, bf16[216,512]{1,0:T(8,128)(2,1)}, u32[]{:S(2)}, u32[]{:S(2)}) collective-permute-start(bf16[216,512]{1,0:T(8,128)(2,1)} %slice.729), channel_id=1, source_target_pairs={{0,12},{12,0},{24,36},{36,24},{48,60},{60,48},{72,84},{84,72},{96,... | collective-permute-start | bytes 663560 | tf_op jit(solution)/shard_map/ppermute | solution.py:21
  142.3 18.2 %all-to-all-start.2 = ((bf16[12,18,512]{2,1,0:T(8,128)(2,1)}), bf16[12,18,512]{2,1,0:T(8,128)(2,1)}, u32[]{:S(2)}, u32[]{:S(2)}) async-start(bf16[12,18,512]{2,1,0:T(8,128)(2,1)} %reshape.325), calls=%async_computation.2 | async-start | bytes 589824 | tf_op jit(solution)/shard_map/all_to_all | solution.py:135
  146.7 6.1 %collective-permute-start.14 = (bf16[216,256]{1,0:T(8,128)(2,1)}, bf16[216,256]{1,0:T(8,128)(2,1)}, u32[]{:S(2)}, u32[]{:S(2)}) collective-permute-start(bf16[216,256]{1,0:T(8,128)(2,1)} %pad_maximum_fusion.1), channel_id=1, source_target_pairs={{0,96},{12,108},{24,120},{36,132},{48,144},{60,156},{72,168},{84,1... | collective-permute-start | bytes 331784 | tf_op jit(solution)/shard_map/ppermute | solution.py:21
  155.1 23.2 %copy-start.24 = (f32[2,96,2]{1,2,0:T(2,128)S(1)}, f32[2,96,2]{1,2,0:T(2,128)}, u32[]{:S(2)}) copy-start(f32[2,96,2]{1,2,0:T(2,128)} %get-tuple-element.125) | copy-start | bytes 4612
  155.9 30.8 %copy-start.23 = (f32[224]{0:T(256)S(1)}, f32[224]{0:T(256)}, u32[]{:S(2)}) copy-start(f32[224]{0:T(256)} %param.9) | copy-start | bytes 2692
  155.9 10.0 %collective-permute-start.16 = (bf16[216,512]{1,0:T(8,128)(2,1)}, bf16[216,512]{1,0:T(8,128)(2,1)}, u32[]{:S(2)}, u32[]{:S(2)}) collective-permute-start(bf16[216,512]{1,0:T(8,128)(2,1)} %slice.728), channel_id=1, source_target_pairs={{0,12},{12,0},{24,36},{36,24},{48,60},{60,48},{72,84},{84,72},{96,... | collective-permute-start | bytes 663560 | tf_op jit(solution)/shard_map/ppermute | solution.py:21
  163.7 2.1 copy-start.18
  163.7 40.0 %copy-start.17 = (bf16[96,30]{1,0:T(8,128)(2,1)S(1)}, bf16[96,30]{1,0:T(8,128)(2,1)}, u32[]{:S(2)}) copy-start(bf16[96,30]{1,0:T(8,128)(2,1)} %copy-done.16) | copy-start | bytes 17284
  163.7 7.2 %collective-permute-start.15 = (bf16[96,256]{1,0:T(8,128)(2,1)S(1)}, bf16[96,256]{1,0:T(8,128)(2,1)}, u32[]{:S(2)}, u32[]{:S(2)}) collective-permute-start(bf16[96,256]{1,0:T(8,128)(2,1)S(1)} %slice.739), channel_id=1, source_target_pairs={{0,24},{12,36},{24,0},{36,12},{48,72},{60,84},{72,48},{84,60},{96,... | collective-permute-start | bytes 147464 | tf_op jit(solution)/shard_map/ppermute | solution.py:21
  171.9 14.7 %collective-permute-start.17 = (bf16[96,224]{1,0:T(8,128)(2,1)S(1)}, bf16[96,224]{1,0:T(8,128)(2,1)S(1)}, u32[]{:S(2)}, u32[]{:S(2)}) collective-permute-start(bf16[96,224]{1,0:T(8,128)(2,1)S(1)} %fusion.60), channel_id=1, source_target_pairs={{0,384},{12,396},{24,408},{36,420},{48,432},{60,444},{72,456},{84,... | collective-permute-start | bytes 129032 | tf_op jit(solution)/shard_map/ppermute | solution.py:26
  179.2 15.2 %all-to-all-start.3 = ((bf16[12,18,512]{2,1,0:T(8,128)(2,1)}), bf16[12,18,512]{2,1,0:T(8,128)(2,1)}, u32[]{:S(2)}, u32[]{:S(2)}) async-start(bf16[12,18,512]{2,1,0:T(8,128)(2,1)} %reshape.327), calls=%async_computation.3 | async-start | bytes 589824 | tf_op jit(solution)/shard_map/all_to_all | solution.py:135
  197.7 8.1 %collective-permute-start.19 = (bf16[96,256]{1,0:T(8,128)(2,1)S(1)}, bf16[96,256]{1,0:T(8,128)(2,1)S(1)}, u32[]{:S(2)}, u32[]{:S(2)}) collective-permute-start(bf16[96,256]{1,0:T(8,128)(2,1)S(1)} %slice.738), channel_id=1, source_target_pairs={{0,24},{12,36},{24,0},{36,12},{48,72},{60,84},{72,48},{84,60},{96,... | collective-permute-start | bytes 147464 | tf_op jit(solution)/shard_map/ppermute | solution.py:21
  203.8 6.6 %collective-permute-start.18 = (bf16[96,256]{1,0:T(8,128)(2,1)S(1)}, bf16[96,256]{1,0:T(8,128)(2,1)S(1)}, u32[]{:S(2)}, u32[]{:S(2)}) collective-permute-start(bf16[96,256]{1,0:T(8,128)(2,1)S(1)} %pad_maximum_fusion.5), channel_id=1, source_target_pairs={{0,24},{12,36},{24,0},{36,12},{48,72},{60,84},{72,48},{84,60},{96,... | collective-permute-start | bytes 147464 | tf_op jit(solution)/shard_map/ppermute | solution.py:21
  206.6 9.9 %collective-permute-start.20 = (bf16[96,224]{1,0:T(8,128)(2,1)S(1)}, bf16[96,224]{1,0:T(8,128)(2,1)}, u32[]{:S(2)}, u32[]{:S(2)}) collective-permute-start(bf16[96,224]{1,0:T(8,128)(2,1)S(1)} %fusion.63), channel_id=1, source_target_pairs={{0,384},{12,396},{24,408},{36,420},{48,432},{60,444},{72,456},{84,... | collective-permute-start | bytes 129032 | tf_op jit(solution)/shard_map/ppermute | solution.py:26
  212.3 11.9 %all-to-all-start.4 = ((bf16[12,18,512]{2,1,0:T(8,128)(2,1)}), bf16[12,18,512]{2,1,0:T(8,128)(2,1)S(1)}, u32[]{:S(2)}, u32[]{:S(2)}) async-start(bf16[12,18,512]{2,1,0:T(8,128)(2,1)} %reshape.331), calls=%async_computation.4 | async-start | bytes 589824 | tf_op jit(solution)/shard_map/all_to_all | solution.py:96
  219.7 12.0 %collective-permute-start.22 = (bf16[96,256]{1,0:T(8,128)(2,1)}, bf16[96,256]{1,0:T(8,128)(2,1)S(1)}, u32[]{:S(2)}, u32[]{:S(2)}) collective-permute-start(bf16[96,256]{1,0:T(8,128)(2,1)} %pad_maximum_fusion.4), channel_id=1, source_target_pairs={{0,24},{12,36},{24,0},{36,12},{48,72},{60,84},{72,48},{84,60},{96,... | collective-permute-start | bytes 147464 | tf_op jit(solution)/shard_map/ppermute | solution.py:21
  224.9 9.6 %collective-permute-start.21 = (bf16[216,512]{1,0:T(8,128)(2,1)}, bf16[216,512]{1,0:T(8,128)(2,1)}, u32[]{:S(2)}, u32[]{:S(2)}) collective-permute-start(bf16[216,512]{1,0:T(8,128)(2,1)} %reshape.332), channel_id=1, source_target_pairs={{0,12},{12,0},{24,36},{36,24},{48,60},{60,48},{72,84},{84,72},{96,... | collective-permute-start | bytes 663560 | tf_op jit(solution)/shard_map/ppermute | solution.py:21
  237.8 9.6 %collective-permute-start.23 = (bf16[224,512]{1,0:T(8,128)(2,1)}, bf16[224,512]{1,0:T(8,128)(2,1)}, u32[]{:S(2)}, u32[]{:S(2)}) collective-permute-start(bf16[224,512]{1,0:T(8,128)(2,1)} %fusion.10), channel_id=1, source_target_pairs={{0,96},{12,108},{24,120},{36,132},{48,144},{60,156},{72,168},{84,1... | collective-permute-start | bytes 688136 | tf_op jit(solution)/shard_map/ppermute | solution.py:21
  240.0 16.0 %all-to-all-start.5 = ((bf16[12,18,512]{2,1,0:T(8,128)(2,1)}), bf16[12,18,512]{2,1,0:T(8,128)(2,1)S(1)}, u32[]{:S(2)}, u32[]{:S(2)}) async-start(bf16[12,18,512]{2,1,0:T(8,128)(2,1)} %reshape.333), calls=%async_computation.5 | async-start | bytes 589824 | tf_op jit(solution)/shard_map/all_to_all | solution.py:96
  248.4 2.0 copy-start.14
  256.8 15.7 %collective-permute-start.25 = (bf16[216,512]{1,0:T(8,128)(2,1)}, bf16[216,512]{1,0:T(8,128)(2,1)S(1)}, u32[]{:S(2)}, u32[]{:S(2)}) collective-permute-start(bf16[216,512]{1,0:T(8,128)(2,1)} %reshape.334), channel_id=1, source_target_pairs={{0,12},{12,0},{24,36},{36,24},{48,60},{60,48},{72,84},{84,72},{96,... | collective-permute-start | bytes 663560 | tf_op jit(solution)/shard_map/ppermute | solution.py:21
  260.6 10.1 %collective-permute-start.24 = (bf16[224,256]{1,0:T(8,128)(2,1)}, bf16[224,256]{1,0:T(8,128)(2,1)S(1)}, u32[]{:S(2)}, u32[]{:S(2)}) collective-permute-start(bf16[224,256]{1,0:T(8,128)(2,1)} %fusion.44), channel_id=1, source_target_pairs={{0,192},{12,204},{24,216},{36,228},{48,240},{60,252},{72,264},{84,... | collective-permute-start | bytes 344072 | tf_op jit(solution)/shard_map/ppermute | solution.py:21
  272.5 19.0 %copy-start.9 = (f32[216,512]{1,0:T(8,128)S(1)}, f32[216,512]{1,0:T(8,128)}, u32[]{:S(2)}) copy-start(f32[216,512]{1,0:T(8,128)} %copy-done.8) | copy-start | bytes 1327108
  273.5 18.1 %collective-permute-start.26 = (bf16[224,256]{1,0:T(8,128)(2,1)S(1)}, bf16[224,256]{1,0:T(8,128)(2,1)S(1)}, u32[]{:S(2)}, u32[]{:S(2)}) collective-permute-start(bf16[224,256]{1,0:T(8,128)(2,1)S(1)} %fusion.46), channel_id=1, source_target_pairs={{0,48},{12,60},{24,72},{36,84},{48,0},{60,12},{72,24},{84,36},{96,... | collective-permute-start | bytes 344072 | tf_op jit(solution)/shard_map/ppermute | solution.py:21
  280.6 11.2 %collective-permute-start.27 = (bf16[224,512]{1,0:T(8,128)(2,1)S(1)}, bf16[224,512]{1,0:T(8,128)(2,1)S(1)}, u32[]{:S(2)}, u32[]{:S(2)}) collective-permute-start(bf16[224,512]{1,0:T(8,128)(2,1)S(1)} %fusion.11), channel_id=1, source_target_pairs={{0,96},{12,108},{24,120},{36,132},{48,144},{60,156},{72,168},{84,1... | collective-permute-start | bytes 688136 | tf_op jit(solution)/shard_map/ppermute | solution.py:21
  291.9 6.8 %collective-permute-start.28 = (bf16[216,128]{1,0:T(8,128)(2,1)S(1)}, bf16[216,128]{1,0:T(8,128)(2,1)S(1)}, u32[]{:S(2)}, u32[]{:S(2)}) collective-permute-start(bf16[216,128]{1,0:T(8,128)(2,1)S(1)} %fusion.49), channel_id=1, source_target_pairs={{0,192},{12,204},{24,216},{36,228},{48,240},{60,252},{72,264},{84,... | collective-permute-start | bytes 165896 | tf_op jit(solution)/shard_map/ppermute | solution.py:21
  293.8 6.9 %collective-permute-start.29 = (bf16[224,256]{1,0:T(8,128)(2,1)S(1)}, bf16[224,256]{1,0:T(8,128)(2,1)S(1)}, u32[]{:S(2)}, u32[]{:S(2)}) collective-permute-start(bf16[224,256]{1,0:T(8,128)(2,1)S(1)} %fusion.45), channel_id=1, source_target_pairs={{0,192},{12,204},{24,216},{36,228},{48,240},{60,252},{72,264},{84,... | collective-permute-start | bytes 344072 | tf_op jit(solution)/shard_map/ppermute | solution.py:21
  300.8 10.5 %collective-permute-start.30 = (bf16[216,256]{1,0:T(8,128)(2,1)S(1)}, bf16[216,256]{1,0:T(8,128)(2,1)S(1)}, u32[]{:S(2)}, u32[]{:S(2)}) collective-permute-start(bf16[216,256]{1,0:T(8,128)(2,1)S(1)} %pad_maximum_fusion.2), channel_id=1, source_target_pairs={{0,96},{12,108},{24,120},{36,132},{48,144},{60,156},{72,168},{84,1... | collective-permute-start | bytes 331784 | tf_op jit(solution)/shard_map/ppermute | solution.py:21
  304.4 16.5 %collective-permute-start.31 = (bf16[224,256]{1,0:T(8,128)(2,1)S(1)}, bf16[224,256]{1,0:T(8,128)(2,1)S(1)}, u32[]{:S(2)}, u32[]{:S(2)}) collective-permute-start(bf16[224,256]{1,0:T(8,128)(2,1)S(1)} %fusion.47), channel_id=1, source_target_pairs={{0,48},{12,60},{24,72},{36,84},{48,0},{60,12},{72,24},{84,36},{96,... | collective-permute-start | bytes 344072 | tf_op jit(solution)/shard_map/ppermute | solution.py:21
  321.1 12.5 %collective-permute-start.32 = (bf16[216,512]{1,0:T(8,128)(2,1)S(1)}, bf16[216,512]{1,0:T(8,128)(2,1)S(1)}, u32[]{:S(2)}, u32[]{:S(2)}) collective-permute-start(bf16[216,512]{1,0:T(8,128)(2,1)S(1)} %slice.725), channel_id=1, source_target_pairs={{0,12},{12,0},{24,36},{36,24},{48,60},{60,48},{72,84},{84,72},{96,... | collective-permute-start | bytes 663560 | tf_op jit(solution)/shard_map/ppermute | solution.py:21
  324.0 6.2 %collective-permute-start.33 = (bf16[216,128]{1,0:T(8,128)(2,1)S(1)}, bf16[216,128]{1,0:T(8,128)(2,1)S(1)}, u32[]{:S(2)}, u32[]{:S(2)}) collective-permute-start(bf16[216,128]{1,0:T(8,128)(2,1)S(1)} %fusion.48), channel_id=1, source_target_pairs={{0,192},{12,204},{24,216},{36,228},{48,240},{60,252},{72,264},{84,... | collective-permute-start | bytes 165896 | tf_op jit(solution)/shard_map/ppermute | solution.py:21
  330.2 7.8 %collective-permute-start.34 = (bf16[216,256]{1,0:T(8,128)(2,1)S(1)}, bf16[216,256]{1,0:T(8,128)(2,1)S(1)}, u32[]{:S(2)}, u32[]{:S(2)}) collective-permute-start(bf16[216,256]{1,0:T(8,128)(2,1)S(1)} %pad_maximum_fusion.3), channel_id=1, source_target_pairs={{0,96},{12,108},{24,120},{36,132},{48,144},{60,156},{72,168},{84,1... | collective-permute-start | bytes 331784 | tf_op jit(solution)/shard_map/ppermute | solution.py:21
  334.4 11.6 %all-to-all-start.6 = ((bf16[12,18,512]{2,1,0:T(8,128)(2,1)}), bf16[12,18,512]{2,1,0:T(8,128)(2,1)S(1)}, u32[]{:S(2)}, u32[]{:S(2)}) async-start(bf16[12,18,512]{2,1,0:T(8,128)(2,1)} %reshape.335), calls=%async_computation.6 | async-start | bytes 589824 | tf_op jit(solution)/shard_map/all_to_all | solution.py:135
  338.0 8.1 %copy-start.15 = (f32[2,96,216]{2,1,0:T(8,128)S(1)}, f32[2,96,216]{2,1,0:T(8,128)}, u32[]{:S(2)}) copy-start(f32[2,96,216]{2,1,0:T(8,128)} %get-tuple-element.101) | copy-start | bytes 497668
  338.6 4.0 %collective-permute-start.36 = (bf16[216,512]{1,0:T(8,128)(2,1)S(1)}, bf16[216,512]{1,0:T(8,128)(2,1)S(1)}, u32[]{:S(2)}, u32[]{:S(2)}) collective-permute-start(bf16[216,512]{1,0:T(8,128)(2,1)S(1)} %slice.724), channel_id=1, source_target_pairs={{0,12},{12,0},{24,36},{36,24},{48,60},{60,48},{72,84},{84,72},{96,... | collective-permute-start | bytes 663560 | tf_op jit(solution)/shard_map/ppermute | solution.py:21
  343.4 23.2 %copy-start.20 = (bf16[96,224]{1,0:T(8,128)(2,1)S(1)}, bf16[96,224]{1,0:T(8,128)(2,1)}, u32[]{:S(2)}) copy-start(bf16[96,224]{1,0:T(8,128)(2,1)} %copy-done.19) | copy-start | bytes 129028
  346.5 11.4 %all-to-all-start.7 = ((bf16[12,18,512]{2,1,0:T(8,128)(2,1)}), bf16[12,18,512]{2,1,0:T(8,128)(2,1)S(1)}, u32[]{:S(2)}, u32[]{:S(2)}) async-start(bf16[12,18,512]{2,1,0:T(8,128)(2,1)} %reshape.337), calls=%async_computation.7 | async-start | bytes 589824 | tf_op jit(solution)/shard_map/all_to_all | solution.py:135
  350.1 16.5 %collective-permute-start.35 = (bf16[96,256]{1,0:T(8,128)(2,1)S(1)}, bf16[96,256]{1,0:T(8,128)(2,1)S(1)}, u32[]{:S(2)}, u32[]{:S(2)}) collective-permute-start(bf16[96,256]{1,0:T(8,128)(2,1)S(1)} %slice.737), channel_id=1, source_target_pairs={{0,24},{12,36},{24,0},{36,12},{48,72},{60,84},{72,48},{84,60},{96,... | collective-permute-start | bytes 147464 | tf_op jit(solution)/shard_map/ppermute | solution.py:21
  358.3 9.7 %collective-permute-start.37 = (bf16[96,256]{1,0:T(8,128)(2,1)S(1)}, bf16[96,256]{1,0:T(8,128)(2,1)S(1)}, u32[]{:S(2)}, u32[]{:S(2)}) collective-permute-start(bf16[96,256]{1,0:T(8,128)(2,1)S(1)} %slice.736), channel_id=1, source_target_pairs={{0,24},{12,36},{24,0},{36,12},{48,72},{60,84},{72,48},{84,60},{96,... | collective-permute-start | bytes 147464 | tf_op jit(solution)/shard_map/ppermute | solution.py:21
  (7 other events, 5.9 us)

commit v3 on v1

--- a/solution.py
+++ b/solution.py
@@ -19,6 +19,11 @@
     return lax.ppermute(x, "pipe", [(i, i ^ (1 << bit)) for i in range(size)])
 
 
+def along_y(x, apart):
+    size = lax.axis_size("pipe")
+    return lax.ppermute(x, "pipe", [(i, i ^ (apart << 3)) for i in range(size)])
+
+
 def other_section(x):
     size = lax.axis_size("pipe")
     return lax.ppermute(x, "pipe", [(i, (i + size // 2) % size) for i in range(size)])
@@ -31,7 +36,7 @@
     w_out[...] = jnp.zeros_like(w_out)
     for block in range(4):
         rows = pl.ds(pl.multiple_of((h ^ ((block & 1) * 2 + (block >> 1))) * cols, 32), cols)
-        for place, rel in enumerate((0, 2, 1, 3)):
+        for place, rel in enumerate(range(4)):
             at = pl.multiple_of((y ^ rel) * 128, 128)
             to = slice(block * LANES, block * LANES + cols)
             w_in[to, place * 256 : place * 256 + 128] = gate_up[rows, pl.ds(at, 128)]
@@ -80,7 +85,8 @@
     low = (squares - high.astype(jnp.float32)).astype(jnp.bfloat16)
     tail = jnp.zeros((lead, rows, LANES - cols - 2), jnp.bfloat16)
     prepared = jnp.concatenate([(values * gain).astype(jnp.bfloat16), high, low, tail], axis=2)
-    both = jnp.concatenate([prepared, exchange(prepared, 1)], axis=2)
+    got, w_in, w_out = lax.optimization_barrier((exchange(prepared, 1), w_in, w_out))
+    both = jnp.concatenate([prepared, got], axis=2)
     buffer = jnp.einsum("nrs,nrc->nsc", spread, both, preferred_element_type=jnp.float32)
     buffer = buffer.astype(jnp.bfloat16).reshape(lead, expert_count, capacity, 2 * LANES)
     arrived = lax.all_to_all(
@@ -101,19 +107,18 @@
     index = jnp.arange(SQ_TILE)[:, None]
     sums = jnp.where(index == 0, sums[0], jnp.where(index == 1, sums[1], 0.0))
     partial = jnp.dot(inputs, w_in, preferred_element_type=jnp.float32)
-    width = partial.shape[1]
-    for bit in (3, 4):
-        width //= 2
-        message = jnp.concatenate(
-            [
-                partial[:, width:].astype(jnp.bfloat16),
-                jnp.pad(sums, ((0, 0), (0, width - half))).astype(jnp.bfloat16),
-            ],
-            axis=0,
+    got = [
+        along_y(
+            jnp.concatenate(
+                [partial[:, apart * 256 : apart * 256 + 256].astype(jnp.bfloat16), sums.astype(jnp.bfloat16)]
+            ),
+            apart,
         )
-        got = exchange(message, bit).astype(jnp.float32)
-        partial = partial[:, :width] + got[:slots]
-        sums = sums + got[slots:, :half]
+        for apart in (3, 2, 1)
+    ]
+    got = sum(part.astype(jnp.float32) for part in got)
+    partial = partial[:, :256] + got[:slots]
+    sums = sums + got[slots:]
     message = jnp.concatenate([partial, sums], axis=0).astype(jnp.bfloat16)
     got = exchange(message, 2).astype(jnp.float32)
     partial = partial + got[:slots]
@@ -121,8 +126,8 @@
     scaling = lax.rsqrt(jnp.concatenate([sums[0], sums[1, : slots - half]]) / D + EPS)[:, None]
     projected = partial * scaling
     activated = (jax.nn.silu(projected[:, :128]) * projected[:, 128:]).astype(jnp.bfloat16)
-    for bit in (4, 3):
-        activated = jnp.concatenate([activated, exchange(activated, bit)], axis=1)
+    got = [along_y(activated, apart) for apart in (3, 2, 1)]
+    activated = jnp.concatenate([activated, *got[::-1]], axis=1)
     partial = lax.dot_general(activated, w_out, DOT_ROWS, preferred_element_type=jnp.float32)
     got = exchange(partial[:, 2 * LANES :].astype(jnp.bfloat16), 0)
     expert_out = (partial[:, : 2 * LANES] + got.astype(jnp.float32)).astype(jnp.bfloat16)

time: 312 us -> 290 us (0.929)
  waiting for transfers between devices: 117 us -> 92.9 us
  blocking collectives: 25.8 us -> 49.6 us
  starting transfers between devices: 138 us -> 120 us
  matrix products: 9.07 us -> 5.93 us
    ppermute x18 -> x10, waiting for transfers between devices: 96.1 us -> 48.4 us  [exchange(): return lax.ppermute(x, 'pipe', [(i, i ^ 1 << bit) for i in range(size)])]
    ppermute x18 -> x10, starting transfers between devices: 112 us -> 66 us  [exchange(): return lax.ppermute(x, 'pipe', [(i, i ^ 1 << bit) for i in range(size)])]
    ppermute x0 -> x12, starting transfers between devices: none -> 43.6 us  [along_y(): return lax.ppermute(x, 'pipe', [(i, i ^ apart << 3) for i in range(size)])]
    ppermute x0 -> x12, waiting for transfers between devices: none -> 33.3 us  [along_y(): return lax.ppermute(x, 'pipe', [(i, i ^ apart << 3) for i in range(size)])]
    all_to_all x1 -> x2, blocking collectives: 11.7 us -> 35.5 us  [layer(): lax.all_to_all(buffer.transpose(1, 0, 2, 3), 'expert', split_axis=0, conc...]
    all_to_all x1 -> x0, starting transfers between devices: 9.45 us -> none  [layer(): lax.all_to_all(buffer.transpose(1, 0, 2, 3), 'expert', split_axis=0, conc...]
    all_to_all x1 -> x0, waiting for transfers between devices: 9.35 us -> none  [layer(): lax.all_to_all(buffer.transpose(1, 0, 2, 3), 'expert', split_axis=0, conc...]
    all_to_all x1, starting transfers between devices: 10.3 us -> 3.58 us  [layer(): lax.all_to_all(expert_out, 'expert', split_axis=0, concat_axis=0, tiled=T...]
  transfers between devices with their start and end apart: 21 -> 24, of which waited for: 19 -> 18; matrix products, arithmetic and copies ran while one was open for 2% -> 3% of each run, Pallas kernels for 2% -> 2%
where the time goes in v3:
time: 290 us; the launch traced here: 289 us
  starting transfers between devices  120 us (41%)
  waiting for transfers between devices  92.9 us (32%)
  blocking collectives  49.6 us (17%)
  other arithmetic  7.84 us (3%)
  local copies, waits for them, and re-layouts  7.03 us (2%)
  matrix products  5.93 us (2%)
  Pallas kernels  5.22 us (2%)
    ppermute x10, starting transfers between devices, exchange(): return lax.ppermute(x, 'pipe', [(i, i ^ 1 << bit) for i in range(size)])  66 us
    ppermute x10, waiting for transfers between devices, exchange(): return lax.ppermute(x, 'pipe', [(i, i ^ 1 << bit) for i in range(size)])  48.4 us
    ppermute x12, starting transfers between devices, along_y(): return lax.ppermute(x, 'pipe', [(i, i ^ apart << 3) for i in range(size)])  43.6 us
    all_to_all x2, blocking collectives, layer(): lax.all_to_all(buffer.transpose(1, 0, 2, 3), 'expert', split_axis=0, conc...  35.5 us
    ppermute x12, waiting for transfers between devices, along_y(): return lax.ppermute(x, 'pipe', [(i, i ^ apart << 3) for i in range(size)])  33.3 us
    all_to_all x1, blocking collectives, layer(): lax.all_to_all(expert_out, 'expert', split_axis=0, concat_axis=0, tiled=T...  14.1 us
    all_to_all x1, waiting for transfers between devices, layer(): lax.all_to_all(expert_out, 'expert', split_axis=0, concat_axis=0, tiled=T...  8.69 us
    ppermute x1, starting transfers between devices, other_section(): lax.ppermute(x, 'pipe', [(i, (i + size // 2) % size) for i in range(size)])  6.57 us
  transfers between devices with their start and end apart: 24, of which 18 were waited for; matrix products, arithmetic and copies ran while one was open for 3% of the time, Pallas kernels for 2%

profile of v3, /device:TPU:1, one launch (start us, length us, event | category | flops | bytes accessed | tf_op | source)
XLA Modules:
  0.0 289.2 jit_solution(15158631445129075781)
XLA Ops:
  0.0 1.0 fusion.34
  1.5 8.4 %collective-permute-start = (bf16[2,96,256]{2,1,0:T(8,128)(2,1)S(1)}, bf16[2,96,256]{2,1,0:T(8,128)(2,1)S(1)}, u32[]{:S(2)}, u32[]{:S(2)}) collective-permute-start(bf16[2,96,256]{2,1,0:T(8,128)(2,1)S(1)} %pad_maximum_fusion.9), channel_id=1, source_target_pairs={{0,24},{12,36},{24,0},{36,12},{48,72},{60,84},{72,48},{84,60},{96,... | collective-permute-start | bytes 294920 | tf_op jit(solution)/shard_map/ppermute | solution.py:19
  9.9 0.6 constant_dynamic-slice_fusion.1
  10.6 0.7 fusion.69
  11.3 0.7 constant_dynamic-slice_fusion.3
  12.4 1.2 reduce-window.14
  14.2 0.6 pad_add_fusion.where
  14.8 5.2 %shard_map.82 = (bf16[1024,1024]{1,0:T(8,128)(2,1)}, bf16[1024,512]{1,0:T(8,128)(2,1)}) custom-call(s32[2]{0:T(128)} %pad_add_fusion.where, bf16[896,1024]{1,0:T(8,128)(2,1)} %bitcast.70, bf16[896,512]{1,0:T(8,128)(2,1)} %bitcast.73, bf16[896,512]{1,0:T(8,128)(2,1)} %bitcast.74, f32[1]{0:T(128)} %bitcast.9.rate), custom_call_target="tpu_custom_call" | custom-call | flops 2000000 | bytes 8000000 | tf_op jit(solution)/shard_map/pallas_call | solution.py:55
  20.3 0.3 convolution_convert_fusion.1
  20.7 0.3 copy.86
  21.0 19.2 %all_to_all.20 = bf16[12,2,18,512]{3,1,2,0:T(2,128)(2,1)S(1)} all-to-all(bf16[12,2,18,512]{3,1,2,0:T(2,128)(2,1)S(1)} %bitcast.71), channel_id=1, replica_groups=mesh['pipe'=64,'expert'=12] {'expert'}, dimensions={0} | all-to-all | bytes 884736 | tf_op jit(solution)/shard_map/all_to_all | solution.py:92
  40.5 4.4 %collective-permute-start.1 = (bf16[432,512]{1,0:T(8,128)(2,1)S(1)}, bf16[432,512]{1,0:T(8,128)(2,1)S(1)}, u32[]{:S(2)}, u32[]{:S(2)}) collective-permute-start(bf16[432,512]{1,0:T(8,128)(2,1)S(1)} %reshape.214), channel_id=1, source_target_pairs={{0,12},{12,0},{24,36},{36,24},{48,60},{60,48},{72,84},{84,72},{96,... | collective-permute-start | bytes 1327112 | tf_op jit(solution)/shard_map/ppermute | solution.py:19
  44.9 1.3 collective-permute-done.1
  46.5 1.1 fusion.76
  48.0 3.2 %collective-permute-start.4 = (bf16[448,256]{1,0:T(8,128)(2,1)S(1)}, bf16[448,256]{1,0:T(8,128)(2,1)S(1)}, u32[]{:S(2)}, u32[]{:S(2)}) collective-permute-start(bf16[448,256]{1,0:T(8,128)(2,1)S(1)} %get-tuple-element.50), channel_id=1, source_target_pairs={{0,96},{12,108},{24,120},{36,132},{48,144},{60,156},{72,168},{84,1... | collective-permute-start | bytes 688136 | tf_op jit(solution)/shard_map/ppermute | solution.py:24
  51.2 4.2 %collective-permute-start.3 = (bf16[448,256]{1,0:T(8,128)(2,1)S(1)}, bf16[448,256]{1,0:T(8,128)(2,1)S(1)}, u32[]{:S(2)}, u32[]{:S(2)}) collective-permute-start(bf16[448,256]{1,0:T(8,128)(2,1)S(1)} %get-tuple-element.49), channel_id=1, source_target_pairs={{0,192},{12,204},{24,216},{36,228},{48,240},{60,252},{72,264},{84,... | collective-permute-start | bytes 688136 | tf_op jit(solution)/shard_map/ppermute | solution.py:24
  55.4 1.9 collective-permute-start.2
  57.4 13.1 %collective-permute-done.3 = bf16[448,256]{1,0:T(8,128)(2,1)S(1)} collective-permute-done((bf16[448,256]{1,0:T(8,128)(2,1)S(1)}, bf16[448,256]{1,0:T(8,128)(2,1)S(1)}, u32[]{:S(2)}, u32[]{:S(2)}) %collective-permute-start.3) | collective-permute-done | bytes 229408 | tf_op jit(solution)/shard_map/ppermute | solution.py:24
  70.6 11.1 %collective-permute-start.5 = (bf16[448,256]{1,0:T(8,128)(2,1)S(1)}, bf16[448,256]{1,0:T(8,128)(2,1)S(1)}, u32[]{:S(2)}, u32[]{:S(2)}) collective-permute-start(bf16[448,256]{1,0:T(8,128)(2,1)S(1)} %pad_maximum_fusion.6), channel_id=1, source_target_pairs={{0,48},{12,60},{24,72},{36,84},{48,0},{60,12},{72,24},{84,36},{96,... | collective-permute-start | bytes 688136 | tf_op jit(solution)/shard_map/ppermute | solution.py:19
  81.8 9.9 %collective-permute-done.5 = bf16[448,256]{1,0:T(8,128)(2,1)S(1)} collective-permute-done((bf16[448,256]{1,0:T(8,128)(2,1)S(1)}, bf16[448,256]{1,0:T(8,128)(2,1)S(1)}, u32[]{:S(2)}, u32[]{:S(2)}) %collective-permute-start.5) | collective-permute-done | bytes 229408 | tf_op jit(solution)/shard_map/ppermute | solution.py:19
  92.0 4.3 %collective-permute-start.8 = (bf16[432,128]{1,0:T(8,128)(2,1)S(1)}, bf16[432,128]{1,0:T(8,128)(2,1)S(1)}, u32[]{:S(2)}, u32[]{:S(2)}) collective-permute-start(bf16[432,128]{1,0:T(8,128)(2,1)S(1)} %fusion.33), channel_id=1, source_target_pairs={{0,288},{12,300},{24,312},{36,324},{48,336},{60,348},{72,360},{84,... | collective-permute-start | bytes 331784 | tf_op jit(solution)/shard_map/ppermute | solution.py:24
  96.3 6.4 %collective-permute-start.7 = (bf16[432,128]{1,0:T(8,128)(2,1)S(1)}, bf16[432,128]{1,0:T(8,128)(2,1)S(1)}, u32[]{:S(2)}, u32[]{:S(2)}) collective-permute-start(bf16[432,128]{1,0:T(8,128)(2,1)S(1)} %fusion.33), channel_id=1, source_target_pairs={{0,192},{12,204},{24,216},{36,228},{48,240},{60,252},{72,264},{84,... | collective-permute-start | bytes 331784 | tf_op jit(solution)/shard_map/ppermute | solution.py:24
  102.7 2.1 collective-permute-start.6
  104.9 0.4 collective-permute-done.7
  105.2 3.0 %collective-permute-done.6 = bf16[432,128]{1,0:T(8,128)(2,1)S(1)} collective-permute-done((bf16[432,128]{1,0:T(8,128)(2,1)S(1)}, bf16[432,128]{1,0:T(8,128)(2,1)S(1)}, u32[]{:S(2)}, u32[]{:S(2)}) %collective-permute-start.6) | collective-permute-done | bytes 110624 | tf_op jit(solution)/shard_map/ppermute | solution.py:24
  108.2 0.7 fusion.6
  108.9 9.6 %collective-permute-start.9 = (bf16[432,512]{1,0:T(8,128)(2,1)S(1)}, bf16[432,512]{1,0:T(8,128)(2,1)S(1)}, u32[]{:S(2)}, u32[]{:S(2)}) collective-permute-start(bf16[432,512]{1,0:T(8,128)(2,1)S(1)} %slice.335), channel_id=1, source_target_pairs={{0,12},{12,0},{24,36},{36,24},{48,60},{60,48},{72,84},{84,72},{96,... | collective-permute-start | bytes 1327112 | tf_op jit(solution)/shard_map/ppermute | solution.py:19
  118.6 1.4 collective-permute-done.9
  120.3 1.1 copy.88
  121.4 3.6 %all-to-all-start.1 = ((bf16[12,2,18,512]{3,1,2,0:T(2,128)(2,1)}), bf16[12,2,18,512]{3,1,2,0:T(2,128)(2,1)S(1)}, u32[]{:S(2)}, u32[]{:S(2)}) async-start(bf16[12,2,18,512]{3,1,2,0:T(2,128)(2,1)} %copy.88), calls=%async_computation.1 | async-start | bytes 884736 | tf_op jit(solution)/shard_map/all_to_all | solution.py:135
  125.3 1.2 reduce-window.16
  126.9 8.7 %all-to-all-done.1 = bf16[12,2,18,512]{3,1,2,0:T(2,128)(2,1)S(1)} async-done(((bf16[12,2,18,512]{3,1,2,0:T(2,128)(2,1)}), bf16[12,2,18,512]{3,1,2,0:T(2,128)(2,1)S(1)}, u32[]{:S(2)}, u32[]{:S(2)}) %all-to-all-start.1) | async-done | bytes 442400 | tf_op jit(solution)/shard_map/all_to_all | solution.py:135
  136.1 1.9 collective-permute-start.10
  138.2 5.1 %collective-permute-done.10 = bf16[2,96,256]{2,1,0:T(8,128)(2,1)S(1)} collective-permute-done((bf16[2,96,256]{2,1,0:T(8,128)(2,1)S(1)}, bf16[2,96,256]{2,1,0:T(8,128)(2,1)S(1)}, u32[]{:S(2)}, u32[]{:S(2)}) %collective-permute-start.10) | collective-permute-done | bytes 98336 | tf_op jit(solution)/shard_map/ppermute | solution.py:19
  143.3 6.6 %collective-permute-start.11 = (bf16[2,96,224]{2,1,0:T(8,128)(2,1)S(1)}, bf16[2,96,224]{2,1,0:T(8,128)(2,1)S(1)}, u32[]{:S(2)}, u32[]{:S(2)}) collective-permute-start(bf16[2,96,224]{2,1,0:T(8,128)(2,1)S(1)} %fusion.36), channel_id=1, source_target_pairs={{0,384},{12,396},{24,408},{36,420},{48,432},{60,444},{72,456},{84,... | collective-permute-start | bytes 258056 | tf_op jit(solution)/shard_map/ppermute | solution.py:29
  150.0 2.6 collective-permute-done.11
  153.1 2.1 collective-permute-start.12
  155.4 4.9 %collective-permute-done.12 = bf16[2,96,256]{2,1,0:T(8,128)(2,1)S(1)} collective-permute-done((bf16[2,96,256]{2,1,0:T(8,128)(2,1)S(1)}, bf16[2,96,256]{2,1,0:T(8,128)(2,1)S(1)}, u32[]{:S(2)}, u32[]{:S(2)}) %collective-permute-start.12) | collective-permute-done | bytes 98336 | tf_op jit(solution)/shard_map/ppermute | solution.py:19
  160.4 0.3 convolution_convert_fusion
  160.7 0.3 copy.98
  161.0 16.3 %all_to_all.21 = bf16[12,2,18,512]{3,1,2,0:T(2,128)(2,1)S(1)} all-to-all(bf16[12,2,18,512]{3,1,2,0:T(2,128)(2,1)S(1)} %bitcast.72), channel_id=1, replica_groups=mesh['pipe'=64,'expert'=12] {'expert'}, dimensions={0} | all-to-all | bytes 884736 | tf_op jit(solution)/shard_map/all_to_all | solution.py:92
  177.6 8.1 %collective-permute-start.13 = (bf16[432,512]{1,0:T(8,128)(2,1)S(1)}, bf16[432,512]{1,0:T(8,128)(2,1)S(1)}, u32[]{:S(2)}, u32[]{:S(2)}) collective-permute-start(bf16[432,512]{1,0:T(8,128)(2,1)S(1)} %reshape.220), channel_id=1, source_target_pairs={{0,12},{12,0},{24,36},{36,24},{48,60},{60,48},{72,84},{84,72},{96,... | collective-permute-start | bytes 1327112 | tf_op jit(solution)/shard_map/ppermute | solution.py:19
  185.7 1.3 collective-permute-done.13
  187.6 1.1 fusion.78
  188.8 2.0 collective-permute-start.16
  190.8 4.3 %collective-permute-start.15 = (bf16[448,256]{1,0:T(8,128)(2,1)S(1)}, bf16[448,256]{1,0:T(8,128)(2,1)S(1)}, u32[]{:S(2)}, u32[]{:S(2)}) collective-permute-start(bf16[448,256]{1,0:T(8,128)(2,1)S(1)} %get-tuple-element.42), channel_id=1, source_target_pairs={{0,192},{12,204},{24,216},{36,228},{48,240},{60,252},{72,264},{84,... | collective-permute-start | bytes 688136 | tf_op jit(solution)/shard_map/ppermute | solution.py:24
  195.2 2.9 %collective-permute-start.14 = (bf16[448,256]{1,0:T(8,128)(2,1)S(1)}, bf16[448,256]{1,0:T(8,128)(2,1)S(1)}, u32[]{:S(2)}, u32[]{:S(2)}) collective-permute-start(bf16[448,256]{1,0:T(8,128)(2,1)S(1)} %get-tuple-element.41), channel_id=1, source_target_pairs={{0,288},{12,300},{24,312},{36,324},{48,336},{60,348},{72,360},{84,... | collective-permute-start | bytes 688136 | tf_op jit(solution)/shard_map/ppermute | solution.py:24
  198.1 2.2 collective-permute-done.16
  200.2 10.0 %collective-permute-done.15 = bf16[448,256]{1,0:T(8,128)(2,1)S(1)} collective-permute-done((bf16[448,256]{1,0:T(8,128)(2,1)S(1)}, bf16[448,256]{1,0:T(8,128)(2,1)S(1)}, u32[]{:S(2)}, u32[]{:S(2)}) %collective-permute-start.15) | collective-permute-done | bytes 229408 | tf_op jit(solution)/shard_map/ppermute | solution.py:24
  210.4 12.8 %collective-permute-start.17 = (bf16[448,256]{1,0:T(8,128)(2,1)S(1)}, bf16[448,256]{1,0:T(8,128)(2,1)S(1)}, u32[]{:S(2)}, u32[]{:S(2)}) collective-permute-start(bf16[448,256]{1,0:T(8,128)(2,1)S(1)} %pad_maximum_fusion.7), channel_id=1, source_target_pairs={{0,48},{12,60},{24,72},{36,84},{48,0},{60,12},{72,24},{84,36},{96,... | collective-permute-start | bytes 688136 | tf_op jit(solution)/shard_map/ppermute | solution.py:19
  223.3 13.2 %collective-permute-done.17 = bf16[448,256]{1,0:T(8,128)(2,1)S(1)} collective-permute-done((bf16[448,256]{1,0:T(8,128)(2,1)S(1)}, bf16[448,256]{1,0:T(8,128)(2,1)S(1)}, u32[]{:S(2)}, u32[]{:S(2)}) %collective-permute-start.17) | collective-permute-done | bytes 229408 | tf_op jit(solution)/shard_map/ppermute | solution.py:19
  236.8 3.2 %collective-permute-start.20 = (bf16[432,128]{1,0:T(8,128)(2,1)S(1)}, bf16[432,128]{1,0:T(8,128)(2,1)S(1)}, u32[]{:S(2)}, u32[]{:S(2)}) collective-permute-start(bf16[432,128]{1,0:T(8,128)(2,1)S(1)} %fusion.32), channel_id=1, source_target_pairs={{0,288},{12,300},{24,312},{36,324},{48,336},{60,348},{72,360},{84,... | collective-permute-start | bytes 331784 | tf_op jit(solution)/shard_map/ppermute | solution.py:24
  240.0 7.1 %collective-permute-start.19 = (bf16[432,128]{1,0:T(8,128)(2,1)S(1)}, bf16[432,128]{1,0:T(8,128)(2,1)S(1)}, u32[]{:S(2)}, u32[]{:S(2)}) collective-permute-start(bf16[432,128]{1,0:T(8,128)(2,1)S(1)} %fusion.32), channel_id=1, source_target_pairs={{0,192},{12,204},{24,216},{36,228},{48,240},{60,252},{72,264},{84,... | collective-permute-start | bytes 331784 | tf_op jit(solution)/shard_map/ppermute | solution.py:24
  247.1 1.9 collective-permute-start.18
  249.0 0.6 collective-permute-done.19
  249.6 4.1 %collective-permute-done.18 = bf16[432,128]{1,0:T(8,128)(2,1)S(1)} collective-permute-done((bf16[432,128]{1,0:T(8,128)(2,1)S(1)}, bf16[432,128]{1,0:T(8,128)(2,1)S(1)}, u32[]{:S(2)}, u32[]{:S(2)}) %collective-permute-start.18) | collective-permute-done | bytes 110624 | tf_op jit(solution)/shard_map/ppermute | solution.py:24
  253.7 0.7 fusion.14
  254.5 5.6 %collective-permute-start.21 = (bf16[432,512]{1,0:T(8,128)(2,1)S(1)}, bf16[432,512]{1,0:T(8,128)(2,1)S(1)}, u32[]{:S(2)}, u32[]{:S(2)}) collective-permute-start(bf16[432,512]{1,0:T(8,128)(2,1)S(1)} %slice.334), channel_id=1, source_target_pairs={{0,12},{12,0},{24,36},{36,24},{48,60},{60,48},{72,84},{84,72},{96,... | collective-permute-start | bytes 1327112 | tf_op jit(solution)/shard_map/ppermute | solution.py:19
  260.1 1.4 collective-permute-done.21
  261.8 0.3 copy.100
  262.1 14.1 %all_to_all.22 = bf16[12,2,18,512]{3,1,2,0:T(2,128)(2,1)S(1)} all-to-all(bf16[12,2,18,512]{3,1,2,0:T(2,128)(2,1)S(1)} %copy.100), channel_id=1, replica_groups=mesh['pipe'=64,'expert'=12] {'expert'}, dimensions={0} | all-to-all | bytes 884736 | tf_op jit(solution)/shard_map/all_to_all | solution.py:135
  276.7 1.9 collective-permute-start.22
  278.6 9.9 %collective-permute-done.22 = bf16[2,96,256]{2,1,0:T(8,128)(2,1)S(1)} collective-permute-done((bf16[2,96,256]{2,1,0:T(8,128)(2,1)S(1)}, bf16[2,96,256]{2,1,0:T(8,128)(2,1)S(1)}, u32[]{:S(2)}, u32[]{:S(2)}) %collective-permute-start.22) | collective-permute-done | bytes 98336 | tf_op jit(solution)/shard_map/ppermute | solution.py:19
  288.6 0.7 fusion.39
  (120 shorter events, 7.9 us)
Async XLA Ops:
  0.0 9.9 %copy-start = (f32[1,2]{1,0:T(1,128)S(1)}, f32[1,2]{1,0:T(1,128)}, u32[]{:S(2)}) copy-start(f32[1,2]{1,0:T(1,128)} %param.13) | copy-start | bytes 28
  0.0 14.8 %copy-start.2 = (f32[2,2,2,96,2]{3,4,2,1,0:T(2,128)S(1)}, f32[2,2,2,96,2]{3,4,2,1,0:T(2,128)}, u32[]{:S(2)}) copy-start(f32[2,2,2,96,2]{3,4,2,1,0:T(2,128)} %param.15) | copy-start | bytes 18436
  1.5 18.7 %collective-permute-start = (bf16[2,96,256]{2,1,0:T(8,128)(2,1)S(1)}, bf16[2,96,256]{2,1,0:T(8,128)(2,1)S(1)}, u32[]{:S(2)}, u32[]{:S(2)}) collective-permute-start(bf16[2,96,256]{2,1,0:T(8,128)(2,1)S(1)} %pad_maximum_fusion.9), channel_id=1, source_target_pairs={{0,24},{12,36},{24,0},{36,12},{48,72},{60,84},{72,48},{84,60},{96,... | collective-permute-start | bytes 294920 | tf_op jit(solution)/shard_map/ppermute | solution.py:19
  40.5 6.0 %copy-start.4 = (bf16[1024,1024]{1,0:T(8,128)(2,1)S(1)}, bf16[1024,1024]{1,0:T(8,128)(2,1)}, u32[]{:S(2)}) copy-start(bf16[1024,1024]{1,0:T(8,128)(2,1)} %get-tuple-element.19) | copy-start | bytes 6291460
  40.5 5.8 %collective-permute-start.1 = (bf16[432,512]{1,0:T(8,128)(2,1)S(1)}, bf16[432,512]{1,0:T(8,128)(2,1)S(1)}, u32[]{:S(2)}, u32[]{:S(2)}) collective-permute-start(bf16[432,512]{1,0:T(8,128)(2,1)S(1)} %reshape.214), channel_id=1, source_target_pairs={{0,12},{12,0},{24,36},{36,24},{48,60},{60,48},{72,84},{84,72},{96,... | collective-permute-start | bytes 1327112 | tf_op jit(solution)/shard_map/ppermute | solution.py:19
  48.0 9.4 %collective-permute-start.4 = (bf16[448,256]{1,0:T(8,128)(2,1)S(1)}, bf16[448,256]{1,0:T(8,128)(2,1)S(1)}, u32[]{:S(2)}, u32[]{:S(2)}) collective-permute-start(bf16[448,256]{1,0:T(8,128)(2,1)S(1)} %get-tuple-element.50), channel_id=1, source_target_pairs={{0,96},{12,108},{24,120},{36,132},{48,144},{60,156},{72,168},{84,1... | collective-permute-start | bytes 688136 | tf_op jit(solution)/shard_map/ppermute | solution.py:24
  51.2 19.2 %collective-permute-start.3 = (bf16[448,256]{1,0:T(8,128)(2,1)S(1)}, bf16[448,256]{1,0:T(8,128)(2,1)S(1)}, u32[]{:S(2)}, u32[]{:S(2)}) collective-permute-start(bf16[448,256]{1,0:T(8,128)(2,1)S(1)} %get-tuple-element.49), channel_id=1, source_target_pairs={{0,192},{12,204},{24,216},{36,228},{48,240},{60,252},{72,264},{84,... | collective-permute-start | bytes 688136 | tf_op jit(solution)/shard_map/ppermute | solution.py:24
  55.4 15.0 %collective-permute-start.2 = (bf16[448,256]{1,0:T(8,128)(2,1)S(1)}, bf16[448,256]{1,0:T(8,128)(2,1)S(1)}, u32[]{:S(2)}, u32[]{:S(2)}) collective-permute-start(bf16[448,256]{1,0:T(8,128)(2,1)S(1)} %get-tuple-element.48), channel_id=1, source_target_pairs={{0,288},{12,300},{24,312},{36,324},{48,336},{60,348},{72,360},{84,... | collective-permute-start | bytes 688136 | tf_op jit(solution)/shard_map/ppermute | solution.py:24
  70.6 37.6 %copy-start.6 = (bf16[1024,512]{1,0:T(8,128)(2,1)S(1)}, bf16[1024,512]{1,0:T(8,128)(2,1)}, u32[]{:S(2)}) copy-start(bf16[1024,512]{1,0:T(8,128)(2,1)} %get-tuple-element.20) | copy-start | bytes 3145732
  70.6 21.0 %collective-permute-start.5 = (bf16[448,256]{1,0:T(8,128)(2,1)S(1)}, bf16[448,256]{1,0:T(8,128)(2,1)S(1)}, u32[]{:S(2)}, u32[]{:S(2)}) collective-permute-start(bf16[448,256]{1,0:T(8,128)(2,1)S(1)} %pad_maximum_fusion.6), channel_id=1, source_target_pairs={{0,48},{12,60},{24,72},{36,84},{48,0},{60,12},{72,24},{84,36},{96,... | collective-permute-start | bytes 688136 | tf_op jit(solution)/shard_map/ppermute | solution.py:19
  92.0 12.9 %collective-permute-start.8 = (bf16[432,128]{1,0:T(8,128)(2,1)S(1)}, bf16[432,128]{1,0:T(8,128)(2,1)S(1)}, u32[]{:S(2)}, u32[]{:S(2)}) collective-permute-start(bf16[432,128]{1,0:T(8,128)(2,1)S(1)} %fusion.33), channel_id=1, source_target_pairs={{0,288},{12,300},{24,312},{36,324},{48,336},{60,348},{72,360},{84,... | collective-permute-start | bytes 331784 | tf_op jit(solution)/shard_map/ppermute | solution.py:24
  96.3 9.0 %collective-permute-start.7 = (bf16[432,128]{1,0:T(8,128)(2,1)S(1)}, bf16[432,128]{1,0:T(8,128)(2,1)S(1)}, u32[]{:S(2)}, u32[]{:S(2)}) collective-permute-start(bf16[432,128]{1,0:T(8,128)(2,1)S(1)} %fusion.33), channel_id=1, source_target_pairs={{0,192},{12,204},{24,216},{36,228},{48,240},{60,252},{72,264},{84,... | collective-permute-start | bytes 331784 | tf_op jit(solution)/shard_map/ppermute | solution.py:24
  102.7 5.5 %collective-permute-start.6 = (bf16[432,128]{1,0:T(8,128)(2,1)S(1)}, bf16[432,128]{1,0:T(8,128)(2,1)S(1)}, u32[]{:S(2)}, u32[]{:S(2)}) collective-permute-start(bf16[432,128]{1,0:T(8,128)(2,1)S(1)} %fusion.33), channel_id=1, source_target_pairs={{0,96},{12,108},{24,120},{36,132},{48,144},{60,156},{72,168},{84,1... | collective-permute-start | bytes 331784 | tf_op jit(solution)/shard_map/ppermute | solution.py:24
  108.9 11.0 %collective-permute-start.9 = (bf16[432,512]{1,0:T(8,128)(2,1)S(1)}, bf16[432,512]{1,0:T(8,128)(2,1)S(1)}, u32[]{:S(2)}, u32[]{:S(2)}) collective-permute-start(bf16[432,512]{1,0:T(8,128)(2,1)S(1)} %slice.335), channel_id=1, source_target_pairs={{0,12},{12,0},{24,36},{36,24},{48,60},{60,48},{72,84},{84,72},{96,... | collective-permute-start | bytes 1327112 | tf_op jit(solution)/shard_map/ppermute | solution.py:19
  121.4 14.2 %all-to-all-start.1 = ((bf16[12,2,18,512]{3,1,2,0:T(2,128)(2,1)}), bf16[12,2,18,512]{3,1,2,0:T(2,128)(2,1)S(1)}, u32[]{:S(2)}, u32[]{:S(2)}) async-start(bf16[12,2,18,512]{3,1,2,0:T(2,128)(2,1)} %copy.88), calls=%async_computation.1 | async-start | bytes 884736 | tf_op jit(solution)/shard_map/all_to_all | solution.py:135
  124.9 18.3 %copy-start.1 = (bf16[2,96,224]{2,1,0:T(8,128)(2,1)S(1)}, bf16[2,96,224]{2,1,0:T(8,128)(2,1)}, u32[]{:S(2)}) copy-start(bf16[2,96,224]{2,1,0:T(8,128)(2,1)} %param.8) | copy-start | bytes 258052
  135.6 17.0 %copy-start.3 = (f32[224]{0:T(256)S(1)}, f32[224]{0:T(256)}, u32[]{:S(2)}) copy-start(f32[224]{0:T(256)} %param.9) | copy-start | bytes 2692
  136.1 7.2 %collective-permute-start.10 = (bf16[2,96,256]{2,1,0:T(8,128)(2,1)S(1)}, bf16[2,96,256]{2,1,0:T(8,128)(2,1)S(1)}, u32[]{:S(2)}, u32[]{:S(2)}) collective-permute-start(bf16[2,96,256]{2,1,0:T(8,128)(2,1)S(1)} %slice.337), channel_id=1, source_target_pairs={{0,24},{12,36},{24,0},{36,12},{48,72},{60,84},{72,48},{84,60},{96,... | collective-permute-start | bytes 294920 | tf_op jit(solution)/shard_map/ppermute | solution.py:19
  143.3 9.3 %collective-permute-start.11 = (bf16[2,96,224]{2,1,0:T(8,128)(2,1)S(1)}, bf16[2,96,224]{2,1,0:T(8,128)(2,1)S(1)}, u32[]{:S(2)}, u32[]{:S(2)}) collective-permute-start(bf16[2,96,224]{2,1,0:T(8,128)(2,1)S(1)} %fusion.36), channel_id=1, source_target_pairs={{0,384},{12,396},{24,408},{36,420},{48,432},{60,444},{72,456},{84,... | collective-permute-start | bytes 258056 | tf_op jit(solution)/shard_map/ppermute | solution.py:29
  153.1 7.2 %collective-permute-start.12 = (bf16[2,96,256]{2,1,0:T(8,128)(2,1)S(1)}, bf16[2,96,256]{2,1,0:T(8,128)(2,1)S(1)}, u32[]{:S(2)}, u32[]{:S(2)}) collective-permute-start(bf16[2,96,256]{2,1,0:T(8,128)(2,1)S(1)} %pad_maximum_fusion.8), channel_id=1, source_target_pairs={{0,24},{12,36},{24,0},{36,12},{48,72},{60,84},{72,48},{84,60},{96,... | collective-permute-start | bytes 294920 | tf_op jit(solution)/shard_map/ppermute | solution.py:19
  177.6 10.0 %copy-start.5 = (bf16[1024,1024]{1,0:T(8,128)(2,1)S(1)}, bf16[1024,1024]{1,0:T(8,128)(2,1)}, u32[]{:S(2)}) copy-start(bf16[1024,1024]{1,0:T(8,128)(2,1)} %get-tuple-element.19) | copy-start | bytes 6291460
  177.6 9.5 %collective-permute-start.13 = (bf16[432,512]{1,0:T(8,128)(2,1)S(1)}, bf16[432,512]{1,0:T(8,128)(2,1)S(1)}, u32[]{:S(2)}, u32[]{:S(2)}) collective-permute-start(bf16[432,512]{1,0:T(8,128)(2,1)S(1)} %reshape.220), channel_id=1, source_target_pairs={{0,12},{12,0},{24,36},{36,24},{48,60},{60,48},{72,84},{84,72},{96,... | collective-permute-start | bytes 1327112 | tf_op jit(solution)/shard_map/ppermute | solution.py:19
  188.8 11.5 %collective-permute-start.16 = (bf16[448,256]{1,0:T(8,128)(2,1)S(1)}, bf16[448,256]{1,0:T(8,128)(2,1)S(1)}, u32[]{:S(2)}, u32[]{:S(2)}) collective-permute-start(bf16[448,256]{1,0:T(8,128)(2,1)S(1)} %get-tuple-element.43), channel_id=1, source_target_pairs={{0,96},{12,108},{24,120},{36,132},{48,144},{60,156},{72,168},{84,1... | collective-permute-start | bytes 688136 | tf_op jit(solution)/shard_map/ppermute | solution.py:24
  190.8 19.4 %collective-permute-start.15 = (bf16[448,256]{1,0:T(8,128)(2,1)S(1)}, bf16[448,256]{1,0:T(8,128)(2,1)S(1)}, u32[]{:S(2)}, u32[]{:S(2)}) collective-permute-start(bf16[448,256]{1,0:T(8,128)(2,1)S(1)} %get-tuple-element.42), channel_id=1, source_target_pairs={{0,192},{12,204},{24,216},{36,228},{48,240},{60,252},{72,264},{84,... | collective-permute-start | bytes 688136 | tf_op jit(solution)/shard_map/ppermute | solution.py:24
  195.2 15.0 %collective-permute-start.14 = (bf16[448,256]{1,0:T(8,128)(2,1)S(1)}, bf16[448,256]{1,0:T(8,128)(2,1)S(1)}, u32[]{:S(2)}, u32[]{:S(2)}) collective-permute-start(bf16[448,256]{1,0:T(8,128)(2,1)S(1)} %get-tuple-element.41), channel_id=1, source_target_pairs={{0,288},{12,300},{24,312},{36,324},{48,336},{60,348},{72,360},{84,... | collective-permute-start | bytes 688136 | tf_op jit(solution)/shard_map/ppermute | solution.py:24
  210.4 26.0 %collective-permute-start.17 = (bf16[448,256]{1,0:T(8,128)(2,1)S(1)}, bf16[448,256]{1,0:T(8,128)(2,1)S(1)}, u32[]{:S(2)}, u32[]{:S(2)}) collective-permute-start(bf16[448,256]{1,0:T(8,128)(2,1)S(1)} %pad_maximum_fusion.7), channel_id=1, source_target_pairs={{0,48},{12,60},{24,72},{36,84},{48,0},{60,12},{72,24},{84,36},{96,... | collective-permute-start | bytes 688136 | tf_op jit(solution)/shard_map/ppermute | solution.py:19
  236.8 12.2 %collective-permute-start.20 = (bf16[432,128]{1,0:T(8,128)(2,1)S(1)}, bf16[432,128]{1,0:T(8,128)(2,1)S(1)}, u32[]{:S(2)}, u32[]{:S(2)}) collective-permute-start(bf16[432,128]{1,0:T(8,128)(2,1)S(1)} %fusion.32), channel_id=1, source_target_pairs={{0,288},{12,300},{24,312},{36,324},{48,336},{60,348},{72,360},{84,... | collective-permute-start | bytes 331784 | tf_op jit(solution)/shard_map/ppermute | solution.py:24
  240.0 9.6 %collective-permute-start.19 = (bf16[432,128]{1,0:T(8,128)(2,1)S(1)}, bf16[432,128]{1,0:T(8,128)(2,1)S(1)}, u32[]{:S(2)}, u32[]{:S(2)}) collective-permute-start(bf16[432,128]{1,0:T(8,128)(2,1)S(1)} %fusion.32), channel_id=1, source_target_pairs={{0,192},{12,204},{24,216},{36,228},{48,240},{60,252},{72,264},{84,... | collective-permute-start | bytes 331784 | tf_op jit(solution)/shard_map/ppermute | solution.py:24
  247.1 6.7 %collective-permute-start.18 = (bf16[432,128]{1,0:T(8,128)(2,1)S(1)}, bf16[432,128]{1,0:T(8,128)(2,1)S(1)}, u32[]{:S(2)}, u32[]{:S(2)}) collective-permute-start(bf16[432,128]{1,0:T(8,128)(2,1)S(1)} %fusion.32), channel_id=1, source_target_pairs={{0,96},{12,108},{24,120},{36,132},{48,144},{60,156},{72,168},{84,1... | collective-permute-start | bytes 331784 | tf_op jit(solution)/shard_map/ppermute | solution.py:24
  254.5 7.0 %collective-permute-start.21 = (bf16[432,512]{1,0:T(8,128)(2,1)S(1)}, bf16[432,512]{1,0:T(8,128)(2,1)S(1)}, u32[]{:S(2)}, u32[]{:S(2)}) collective-permute-start(bf16[432,512]{1,0:T(8,128)(2,1)S(1)} %slice.334), channel_id=1, source_target_pairs={{0,12},{12,0},{24,36},{36,24},{48,60},{60,48},{72,84},{84,72},{96,... | collective-permute-start | bytes 1327112 | tf_op jit(solution)/shard_map/ppermute | solution.py:19
  276.7 11.9 %collective-permute-start.22 = (bf16[2,96,256]{2,1,0:T(8,128)(2,1)S(1)}, bf16[2,96,256]{2,1,0:T(8,128)(2,1)S(1)}, u32[]{:S(2)}, u32[]{:S(2)}) collective-permute-start(bf16[2,96,256]{2,1,0:T(8,128)(2,1)S(1)} %slice.336), channel_id=1, source_target_pairs={{0,24},{12,36},{24,0},{36,12},{48,72},{60,84},{72,48},{84,60},{96,... | collective-permute-start | bytes 294920 | tf_op jit(solution)/shard_map/ppermute | solution.py:19

commit v4 on v3

--- a/solution.py
+++ b/solution.py
@@ -10,7 +10,7 @@
 EPS = 1e-06
 ROUTE_SCALE = 2.5
 LANES = 256
-SQ_TILE = 16
+SQ_TILE = 8
 DOT_ROWS = (((1,), (1,)), ((), ()))
 
 
@@ -98,37 +98,42 @@
     lane = jnp.arange(4 * LANES) % LANES
     marks = ((lane == cols) | (lane == cols + 1)).astype(jnp.bfloat16)
     marks = jnp.broadcast_to(marks[None], (SQ_TILE, 4 * LANES))
-    half = LANES
+    half = slots // 2
+    parts = [inputs[:half], inputs[half:]]
+    blocks = [jnp.dot(part, w_in, preferred_element_type=jnp.float32) for part in parts]
     sums = [
         lax.dot_general(marks, part, DOT_ROWS, preferred_element_type=jnp.float32)
-        for part in (inputs[:half], inputs[half:])
+        for part in parts
     ]
-    sums[1] = jnp.pad(sums[1], ((0, 0), (0, 2 * half - slots)))
-    index = jnp.arange(SQ_TILE)[:, None]
-    sums = jnp.where(index == 0, sums[0], jnp.where(index == 1, sums[1], 0.0))
-    partial = jnp.dot(inputs, w_in, preferred_element_type=jnp.float32)
-    got = [
-        along_y(
-            jnp.concatenate(
-                [partial[:, apart * 256 : apart * 256 + 256].astype(jnp.bfloat16), sums.astype(jnp.bfloat16)]
-            ),
-            apart,
+    sums = [jnp.pad(row, ((0, 0), (0, LANES - half))) for row in sums]
+    summed = []
+    for partial, row in zip(blocks, sums):
+        packed = [
+            jnp.concatenate([partial[:, k * 256 : k * 256 + 256], row]).astype(jnp.bfloat16)
+            for k in (3, 2, 1)
+        ]
+        if summed:
+            packed, _ = lax.optimization_barrier((packed, first))
+        first = packed
+        got = [along_y(message, k) for message, k in zip(packed, (3, 2, 1))]
+        got = sum(message.astype(jnp.float32) for message in got)
+        summed.append(jnp.concatenate([partial[:, :256], row]) + got)
+    crossed = [total + exchange(total.astype(jnp.bfloat16), 2).astype(jnp.float32) for total in summed]
+    hidden = []
+    for total in crossed:
+        scaling = lax.rsqrt(total[half, :half] / D + EPS)[:, None]
+        projected = total[:half] * scaling
+        hidden.append(
+            (jax.nn.silu(projected[:, :128]) * projected[:, 128:]).astype(jnp.bfloat16)
         )
-        for apart in (3, 2, 1)
-    ]
-    got = sum(part.astype(jnp.float32) for part in got)
-    partial = partial[:, :256] + got[:slots]
-    sums = sums + got[slots:]
-    message = jnp.concatenate([partial, sums], axis=0).astype(jnp.bfloat16)
-    got = exchange(message, 2).astype(jnp.float32)
-    partial = partial + got[:slots]
-    sums = sums + got[slots:]
-    scaling = lax.rsqrt(jnp.concatenate([sums[0], sums[1, : slots - half]]) / D + EPS)[:, None]
-    projected = partial * scaling
-    activated = (jax.nn.silu(projected[:, :128]) * projected[:, 128:]).astype(jnp.bfloat16)
-    got = [along_y(activated, apart) for apart in (3, 2, 1)]
-    activated = jnp.concatenate([activated, *got[::-1]], axis=1)
-    partial = lax.dot_general(activated, w_out, DOT_ROWS, preferred_element_type=jnp.float32)
+    outs = []
+    for piece in hidden:
+        got = [along_y(piece, k) for k in (3, 2, 1)]
+        piece = jnp.concatenate([piece, *got[::-1]], axis=1)
+        outs.append(
+            lax.dot_general(piece, w_out, DOT_ROWS, preferred_element_type=jnp.float32)
+        )
+    partial = jnp.concatenate(outs)
     got = exchange(partial[:, 2 * LANES :].astype(jnp.bfloat16), 0)
     expert_out = (partial[:, : 2 * LANES] + got.astype(jnp.float32)).astype(jnp.bfloat16)
     expert_out = expert_out.reshape(expert_count, lead, capacity, 2 * LANES)

time: 290 us -> 303 us (1.045)
  waiting for transfers between devices: 92.9 us -> 35.3 us
  starting transfers between devices: 120 us -> 166 us
  local copies, waits for them, and re-layouts: 7.03 us -> 18.3 us
  other arithmetic: 7.84 us -> 14.8 us
  matrix products: 5.93 us -> 9.87 us
    ppermute x12 -> x24, starting transfers between devices: 43.6 us -> 79.5 us  [along_y(): return lax.ppermute(x, 'pipe', [(i, i ^ apart << 3) for i in range(size)])]
    ppermute x12 -> x24, waiting for transfers between devices: 33.3 us -> 4.04 us  [along_y(): return lax.ppermute(x, 'pipe', [(i, i ^ apart << 3) for i in range(size)])]
    ppermute x10 -> x12, waiting for transfers between devices: 48.4 us -> 21.2 us  [exchange(): return lax.ppermute(x, 'pipe', [(i, i ^ 1 << bit) for i in range(size)])]
    ppermute x10 -> x12, starting transfers between devices: 66 us -> 75.8 us  [exchange(): return lax.ppermute(x, 'pipe', [(i, i ^ 1 << bit) for i in range(size)])]
  transfers between devices with their start and end apart: 24 -> 38, of which waited for: 18 -> 13; matrix products, arithmetic and copies ran while one was open for 3% -> 5% of each run, Pallas kernels for 2% -> 2%
where the time goes in v4:
time: 303 us; the launch traced here: 301 us
  starting transfers between devices  166 us (55%)
  blocking collectives  50.4 us (17%)
  waiting for transfers between devices  35.3 us (12%)
  local copies, waits for them, and re-layouts  18.3 us (6%)
  other arithmetic  14.8 us (5%)
  matrix products  9.87 us (3%)
  Pallas kernels  5.11 us (2%)
    ppermute x24, starting transfers between devices, along_y(): return lax.ppermute(x, 'pipe', [(i, i ^ apart << 3) for i in range(size)])  79.5 us
    ppermute x12, starting transfers between devices, exchange(): return lax.ppermute(x, 'pipe', [(i, i ^ 1 << bit) for i in range(size)])  75.8 us
    all_to_all x2, blocking collectives, layer(): lax.all_to_all(buffer.transpose(1, 0, 2, 3), 'expert', split_axis=0, conc...  36.3 us
    ppermute x12, waiting for transfers between devices, exchange(): return lax.ppermute(x, 'pipe', [(i, i ^ 1 << bit) for i in range(size)])  21.2 us
    all_to_all x1, blocking collectives, layer(): lax.all_to_all(expert_out, 'expert', split_axis=0, concat_axis=0, tiled=T...  14.1 us
    all_to_all x1, waiting for transfers between devices, layer(): lax.all_to_all(expert_out, 'expert', split_axis=0, concat_axis=0, tiled=T...  7.09 us
    ppermute x1, starting transfers between devices, other_section(): lax.ppermute(x, 'pipe', [(i, (i + size // 2) % size) for i in range(size)])  6.59 us
  transfers between devices with their start and end apart: 38, of which 13 were waited for; matrix products, arithmetic and copies ran while one was open for 5% of the time, Pallas kernels for 2%

profile of v4, /device:TPU:1, one launch (start us, length us, event | category | flops | bytes accessed | tf_op | source)
XLA Modules:
  0.0 301.1 jit_solution(5222007049809320028)
XLA Ops:
  1.4 8.4 %collective-permute-start = (bf16[2,96,256]{2,1,0:T(8,128)(2,1)S(1)}, bf16[2,96,256]{2,1,0:T(8,128)(2,1)S(1)}, u32[]{:S(2)}, u32[]{:S(2)}) collective-permute-start(bf16[2,96,256]{2,1,0:T(8,128)(2,1)S(1)} %pad_maximum_fusion.15), channel_id=1, source_target_pairs={{0,24},{12,36},{24,0},{36,12},{48,72},{60,84},{72,48},{84,60},{96,... | collective-permute-start | bytes 294920 | tf_op jit(solution)/shard_map/ppermute | solution.py:19
  12.3 1.2 reduce-window.14
  15.5 5.1 %shard_map.82 = (bf16[1024,1024]{1,0:T(8,128)(2,1)}, bf16[1024,512]{1,0:T(8,128)(2,1)}) custom-call(s32[2]{0:T(128)} %pad_add_fusion.where, bf16[896,1024]{1,0:T(8,128)(2,1)} %bitcast.70, bf16[896,512]{1,0:T(8,128)(2,1)} %bitcast.73, bf16[896,512]{1,0:T(8,128)(2,1)} %bitcast.74, f32[1]{0:T(128)} %bitcast.9.rate), custom_call_target="tpu_custom_call" | custom-call | flops 2000000 | bytes 8000000 | tf_op jit(solution)/shard_map/pallas_call | solution.py:55
  21.6 19.2 %all_to_all.20 = bf16[12,2,18,512]{3,1,2,0:T(2,128)(2,1)S(1)} all-to-all(bf16[12,2,18,512]{3,1,2,0:T(2,128)(2,1)S(1)} %bitcast.71), channel_id=1, replica_groups=mesh['pipe'=64,'expert'=12] {'expert'}, dimensions={0} | all-to-all | bytes 884736 | tf_op jit(solution)/shard_map/all_to_all | solution.py:92
  41.8 4.2 %collective-permute-start.1 = (bf16[432,512]{1,0:T(8,128)(2,1)}, bf16[432,512]{1,0:T(8,128)(2,1)S(1)}, u32[]{:S(2)}, u32[]{:S(2)}) collective-permute-start(bf16[432,512]{1,0:T(8,128)(2,1)} %reshape.214), channel_id=1, source_target_pairs={{0,12},{12,0},{24,36},{36,24},{48,60},{60,48},{72,84},{84,72},{96,... | collective-permute-start | bytes 1327112 | tf_op jit(solution)/shard_map/ppermute | solution.py:19
  46.1 1.1 constant_dynamic-update-slice_fusion.1
  49.6 3.2 %collective-permute-start.4 = (bf16[224,256]{1,0:T(8,128)(2,1)S(1)}, bf16[224,256]{1,0:T(8,128)(2,1)S(1)}, u32[]{:S(2)}, u32[]{:S(2)}) collective-permute-start(bf16[224,256]{1,0:T(8,128)(2,1)S(1)} %get-tuple-element.74), channel_id=1, source_target_pairs={{0,96},{12,108},{24,120},{36,132},{48,144},{60,156},{72,168},{84,1... | collective-permute-start | bytes 344072 | tf_op jit(solution)/shard_map/ppermute | solution.py:24
  52.8 4.2 %collective-permute-start.3 = (bf16[224,256]{1,0:T(8,128)(2,1)S(1)}, bf16[224,256]{1,0:T(8,128)(2,1)S(1)}, u32[]{:S(2)}, u32[]{:S(2)}) collective-permute-start(bf16[224,256]{1,0:T(8,128)(2,1)S(1)} %get-tuple-element.73), channel_id=1, source_target_pairs={{0,192},{12,204},{24,216},{36,228},{48,240},{60,252},{72,264},{84,... | collective-permute-start | bytes 344072 | tf_op jit(solution)/shard_map/ppermute | solution.py:24
  57.0 1.9 collective-permute-start.2
  59.1 2.2 collective-permute-start.11
  61.3 5.1 %collective-permute-start.10 = (bf16[224,256]{1,0:T(8,128)(2,1)S(1)}, bf16[224,256]{1,0:T(8,128)(2,1)S(1)}, u32[]{:S(2)}, u32[]{:S(2)}) collective-permute-start(bf16[224,256]{1,0:T(8,128)(2,1)S(1)} %get-tuple-element.25), channel_id=1, source_target_pairs={{0,192},{12,204},{24,216},{36,228},{48,240},{60,252},{72,264},{84,... | collective-permute-start | bytes 344072 | tf_op jit(solution)/shard_map/ppermute | solution.py:24
  66.5 1.9 collective-permute-start.9
  68.5 11.1 %collective-permute-start.5 = (bf16[224,256]{1,0:T(8,128)(2,1)S(1)}, bf16[224,256]{1,0:T(8,128)(2,1)S(1)}, u32[]{:S(2)}, u32[]{:S(2)}) collective-permute-start(bf16[224,256]{1,0:T(8,128)(2,1)S(1)} %fusion.111), channel_id=1, source_target_pairs={{0,48},{12,60},{24,72},{36,84},{48,0},{60,12},{72,24},{84,36},{96,... | collective-permute-start | bytes 344072 | tf_op jit(solution)/shard_map/ppermute | solution.py:19
  79.7 5.2 %collective-permute-start.12 = (bf16[224,256]{1,0:T(8,128)(2,1)S(1)}, bf16[224,256]{1,0:T(8,128)(2,1)S(1)}, u32[]{:S(2)}, u32[]{:S(2)}) collective-permute-start(bf16[224,256]{1,0:T(8,128)(2,1)S(1)} %fusion.110), channel_id=1, source_target_pairs={{0,48},{12,60},{24,72},{36,84},{48,0},{60,12},{72,24},{84,36},{96,... | collective-permute-start | bytes 344072 | tf_op jit(solution)/shard_map/ppermute | solution.py:19
  85.2 5.1 %collective-permute-start.8 = (bf16[216,128]{1,0:T(8,128)(2,1)S(1)}, bf16[216,128]{1,0:T(8,128)(2,1)S(1)}, u32[]{:S(2)}, u32[]{:S(2)}) collective-permute-start(bf16[216,128]{1,0:T(8,128)(2,1)S(1)} %fusion.71), channel_id=1, source_target_pairs={{0,288},{12,300},{24,312},{36,324},{48,336},{60,348},{72,360},{84,... | collective-permute-start | bytes 165896 | tf_op jit(solution)/shard_map/ppermute | solution.py:24
  90.3 3.8 %collective-permute-start.7 = (bf16[216,128]{1,0:T(8,128)(2,1)S(1)}, bf16[216,128]{1,0:T(8,128)(2,1)S(1)}, u32[]{:S(2)}, u32[]{:S(2)}) collective-permute-start(bf16[216,128]{1,0:T(8,128)(2,1)S(1)} %fusion.71), channel_id=1, source_target_pairs={{0,192},{12,204},{24,216},{36,228},{48,240},{60,252},{72,264},{84,... | collective-permute-start | bytes 165896 | tf_op jit(solution)/shard_map/ppermute | solution.py:24
  94.1 1.9 collective-permute-start.6
  96.3 3.9 %collective-permute-start.15 = (bf16[216,128]{1,0:T(8,128)(2,1)S(1)}, bf16[216,128]{1,0:T(8,128)(2,1)S(1)}, u32[]{:S(2)}, u32[]{:S(2)}) collective-permute-start(bf16[216,128]{1,0:T(8,128)(2,1)S(1)} %fusion.70), channel_id=1, source_target_pairs={{0,288},{12,300},{24,312},{36,324},{48,336},{60,348},{72,360},{84,... | collective-permute-start | bytes 165896 | tf_op jit(solution)/shard_map/ppermute | solution.py:24
  100.2 2.5 collective-permute-start.14
  102.7 2.8 collective-permute-start.13
  108.3 5.5 %collective-permute-start.16 = (bf16[432,512]{1,0:T(8,128)(2,1)S(1)}, bf16[432,512]{1,0:T(8,128)(2,1)S(1)}, u32[]{:S(2)}, u32[]{:S(2)}) collective-permute-start(bf16[432,512]{1,0:T(8,128)(2,1)S(1)} %fusion.7), channel_id=1, source_target_pairs={{0,12},{12,0},{24,36},{36,24},{48,60},{60,48},{72,84},{84,72},{96,... | collective-permute-start | bytes 1327112 | tf_op jit(solution)/shard_map/ppermute | solution.py:19
  113.8 1.4 collective-permute-done.16
  116.1 2.0 reshape.215
  118.1 2.2 copy.88
  120.3 4.2 %all-to-all-start.1 = ((bf16[12,2,18,512]{3,1,2,0:T(2,128)(2,1)}), bf16[12,2,18,512]{3,1,2,0:T(2,128)(2,1)}, u32[]{:S(2)}, u32[]{:S(2)}) async-start(bf16[12,2,18,512]{3,1,2,0:T(2,128)(2,1)} %copy.88), calls=%async_computation.1 | async-start | bytes 884736 | tf_op jit(solution)/shard_map/all_to_all | solution.py:140
  125.5 2.2 reduce-window.16
  128.1 7.1 %all-to-all-done.1 = bf16[12,2,18,512]{3,1,2,0:T(2,128)(2,1)} async-done(((bf16[12,2,18,512]{3,1,2,0:T(2,128)(2,1)}), bf16[12,2,18,512]{3,1,2,0:T(2,128)(2,1)}, u32[]{:S(2)}, u32[]{:S(2)}) %all-to-all-start.1) | async-done | bytes 442400 | tf_op jit(solution)/shard_map/all_to_all | solution.py:140
  135.2 1.2 fusion.28
  136.5 1.2 convolution_add_fusion.1
  138.5 2.9 collective-permute-start.17
  141.6 4.1 %collective-permute-done.17 = bf16[2,96,256]{2,1,0:T(8,128)(2,1)} collective-permute-done((bf16[2,96,256]{2,1,0:T(8,128)(2,1)S(1)}, bf16[2,96,256]{2,1,0:T(8,128)(2,1)}, u32[]{:S(2)}, u32[]{:S(2)}) %collective-permute-start.17) | collective-permute-done | bytes 98336 | tf_op jit(solution)/shard_map/ppermute | solution.py:19
  145.7 1.7 fusion.64
  147.5 6.6 %collective-permute-start.18 = (bf16[2,96,224]{2,1,0:T(8,128)(2,1)}, bf16[2,96,224]{2,1,0:T(8,128)(2,1)}, u32[]{:S(2)}, u32[]{:S(2)}) collective-permute-start(bf16[2,96,224]{2,1,0:T(8,128)(2,1)} %fusion.64), channel_id=1, source_target_pairs={{0,384},{12,396},{24,408},{36,420},{48,432},{60,444},{72,456},{84,... | collective-permute-start | bytes 258056 | tf_op jit(solution)/shard_map/ppermute | solution.py:29
  154.2 3.0 collective-permute-done.18
  158.5 3.0 %collective-permute-start.19 = (bf16[2,96,256]{2,1,0:T(8,128)(2,1)S(1)}, bf16[2,96,256]{2,1,0:T(8,128)(2,1)}, u32[]{:S(2)}, u32[]{:S(2)}) collective-permute-start(bf16[2,96,256]{2,1,0:T(8,128)(2,1)S(1)} %pad_maximum_fusion.14), channel_id=1, source_target_pairs={{0,24},{12,36},{24,0},{36,12},{48,72},{60,84},{72,48},{84,60},{96,... | collective-permute-start | bytes 294920 | tf_op jit(solution)/shard_map/ppermute | solution.py:19
  162.4 3.4 %collective-permute-done.19 = bf16[2,96,256]{2,1,0:T(8,128)(2,1)} collective-permute-done((bf16[2,96,256]{2,1,0:T(8,128)(2,1)S(1)}, bf16[2,96,256]{2,1,0:T(8,128)(2,1)}, u32[]{:S(2)}, u32[]{:S(2)}) %collective-permute-start.19) | collective-permute-done | bytes 98336 | tf_op jit(solution)/shard_map/ppermute | solution.py:19
  165.8 1.7 concatenate.113
  167.5 1.3 convolution_convert_fusion
  169.2 17.1 %all_to_all.21 = bf16[12,2,18,512]{3,1,2,0:T(2,128)(2,1)S(1)} all-to-all(bf16[12,2,18,512]{3,1,2,0:T(2,128)(2,1)S(1)} %bitcast.72), channel_id=1, replica_groups=mesh['pipe'=64,'expert'=12] {'expert'}, dimensions={0} | all-to-all | bytes 884736 | tf_op jit(solution)/shard_map/all_to_all | solution.py:92
  187.1 2.0 reshape.220
  189.1 8.6 %collective-permute-start.20 = (bf16[432,512]{1,0:T(8,128)(2,1)}, bf16[432,512]{1,0:T(8,128)(2,1)S(1)}, u32[]{:S(2)}, u32[]{:S(2)}) collective-permute-start(bf16[432,512]{1,0:T(8,128)(2,1)} %reshape.220), channel_id=1, source_target_pairs={{0,12},{12,0},{24,36},{36,24},{48,60},{60,48},{72,84},{84,72},{96,... | collective-permute-start | bytes 1327112 | tf_op jit(solution)/shard_map/ppermute | solution.py:19
  197.8 1.1 constant_dynamic-update-slice_fusion.3
  201.1 3.4 %collective-permute-start.23 = (bf16[224,256]{1,0:T(8,128)(2,1)S(1)}, bf16[224,256]{1,0:T(8,128)(2,1)S(1)}, u32[]{:S(2)}, u32[]{:S(2)}) collective-permute-start(bf16[224,256]{1,0:T(8,128)(2,1)S(1)} %get-tuple-element.68), channel_id=1, source_target_pairs={{0,96},{12,108},{24,120},{36,132},{48,144},{60,156},{72,168},{84,1... | collective-permute-start | bytes 344072 | tf_op jit(solution)/shard_map/ppermute | solution.py:24
  204.5 3.4 %collective-permute-start.22 = (bf16[224,256]{1,0:T(8,128)(2,1)S(1)}, bf16[224,256]{1,0:T(8,128)(2,1)S(1)}, u32[]{:S(2)}, u32[]{:S(2)}) collective-permute-start(bf16[224,256]{1,0:T(8,128)(2,1)S(1)} %get-tuple-element.67), channel_id=1, source_target_pairs={{0,192},{12,204},{24,216},{36,228},{48,240},{60,252},{72,264},{84,... | collective-permute-start | bytes 344072 | tf_op jit(solution)/shard_map/ppermute | solution.py:24
  207.9 3.1 %collective-permute-start.21 = (bf16[224,256]{1,0:T(8,128)(2,1)S(1)}, bf16[224,256]{1,0:T(8,128)(2,1)S(1)}, u32[]{:S(2)}, u32[]{:S(2)}) collective-permute-start(bf16[224,256]{1,0:T(8,128)(2,1)S(1)} %get-tuple-element.66), channel_id=1, source_target_pairs={{0,288},{12,300},{24,312},{36,324},{48,336},{60,348},{72,360},{84,... | collective-permute-start | bytes 344072 | tf_op jit(solution)/shard_map/ppermute | solution.py:24
  211.1 2.2 collective-permute-start.30
  213.3 4.0 %collective-permute-start.29 = (bf16[224,256]{1,0:T(8,128)(2,1)S(1)}, bf16[224,256]{1,0:T(8,128)(2,1)S(1)}, u32[]{:S(2)}, u32[]{:S(2)}) collective-permute-start(bf16[224,256]{1,0:T(8,128)(2,1)S(1)} %get-tuple-element.31), channel_id=1, source_target_pairs={{0,192},{12,204},{24,216},{36,228},{48,240},{60,252},{72,264},{84,... | collective-permute-start | bytes 344072 | tf_op jit(solution)/shard_map/ppermute | solution.py:24
  217.4 3.1 %collective-permute-start.28 = (bf16[224,256]{1,0:T(8,128)(2,1)S(1)}, bf16[224,256]{1,0:T(8,128)(2,1)S(1)}, u32[]{:S(2)}, u32[]{:S(2)}) collective-permute-start(bf16[224,256]{1,0:T(8,128)(2,1)S(1)} %get-tuple-element.30), channel_id=1, source_target_pairs={{0,288},{12,300},{24,312},{36,324},{48,336},{60,348},{72,360},{84,... | collective-permute-start | bytes 344072 | tf_op jit(solution)/shard_map/ppermute | solution.py:24
  220.5 15.3 %collective-permute-start.24 = (bf16[224,256]{1,0:T(8,128)(2,1)S(1)}, bf16[224,256]{1,0:T(8,128)(2,1)S(1)}, u32[]{:S(2)}, u32[]{:S(2)}) collective-permute-start(bf16[224,256]{1,0:T(8,128)(2,1)S(1)} %fusion.109), channel_id=1, source_target_pairs={{0,48},{12,60},{24,72},{36,84},{48,0},{60,12},{72,24},{84,36},{96,... | collective-permute-start | bytes 344072 | tf_op jit(solution)/shard_map/ppermute | solution.py:19
  236.0 4.2 %collective-permute-start.31 = (bf16[224,256]{1,0:T(8,128)(2,1)S(1)}, bf16[224,256]{1,0:T(8,128)(2,1)S(1)}, u32[]{:S(2)}, u32[]{:S(2)}) collective-permute-start(bf16[224,256]{1,0:T(8,128)(2,1)S(1)} %fusion.108), channel_id=1, source_target_pairs={{0,48},{12,60},{24,72},{36,84},{48,0},{60,12},{72,24},{84,36},{96,... | collective-permute-start | bytes 344072 | tf_op jit(solution)/shard_map/ppermute | solution.py:19
  240.4 6.7 %collective-permute-start.27 = (bf16[216,128]{1,0:T(8,128)(2,1)S(1)}, bf16[216,128]{1,0:T(8,128)(2,1)S(1)}, u32[]{:S(2)}, u32[]{:S(2)}) collective-permute-start(bf16[216,128]{1,0:T(8,128)(2,1)S(1)} %fusion.69), channel_id=1, source_target_pairs={{0,288},{12,300},{24,312},{36,324},{48,336},{60,348},{72,360},{84,... | collective-permute-start | bytes 165896 | tf_op jit(solution)/shard_map/ppermute | solution.py:24
  247.1 3.5 %collective-permute-start.26 = (bf16[216,128]{1,0:T(8,128)(2,1)S(1)}, bf16[216,128]{1,0:T(8,128)(2,1)S(1)}, u32[]{:S(2)}, u32[]{:S(2)}) collective-permute-start(bf16[216,128]{1,0:T(8,128)(2,1)S(1)} %fusion.69), channel_id=1, source_target_pairs={{0,192},{12,204},{24,216},{36,228},{48,240},{60,252},{72,264},{84,... | collective-permute-start | bytes 165896 | tf_op jit(solution)/shard_map/ppermute | solution.py:24
  250.6 2.2 collective-permute-start.25
  253.1 4.0 %collective-permute-start.34 = (bf16[216,128]{1,0:T(8,128)(2,1)S(1)}, bf16[216,128]{1,0:T(8,128)(2,1)S(1)}, u32[]{:S(2)}, u32[]{:S(2)}) collective-permute-start(bf16[216,128]{1,0:T(8,128)(2,1)S(1)} %fusion.68), channel_id=1, source_target_pairs={{0,288},{12,300},{24,312},{36,324},{48,336},{60,348},{72,360},{84,... | collective-permute-start | bytes 165896 | tf_op jit(solution)/shard_map/ppermute | solution.py:24
  257.1 2.2 collective-permute-start.33
  259.3 3.1 %collective-permute-start.32 = (bf16[216,128]{1,0:T(8,128)(2,1)S(1)}, bf16[216,128]{1,0:T(8,128)(2,1)S(1)}, u32[]{:S(2)}, u32[]{:S(2)}) collective-permute-start(bf16[216,128]{1,0:T(8,128)(2,1)S(1)} %fusion.68), channel_id=1, source_target_pairs={{0,96},{12,108},{24,120},{36,132},{48,144},{60,156},{72,168},{84,1... | collective-permute-start | bytes 165896 | tf_op jit(solution)/shard_map/ppermute | solution.py:24
  262.9 1.2 collective-permute-done.33
  264.1 1.1 collective-permute-done.32
  265.8 5.2 %collective-permute-start.35 = (bf16[432,512]{1,0:T(8,128)(2,1)S(1)}, bf16[432,512]{1,0:T(8,128)(2,1)S(1)}, u32[]{:S(2)}, u32[]{:S(2)}) collective-permute-start(bf16[432,512]{1,0:T(8,128)(2,1)S(1)} %fusion.6), channel_id=1, source_target_pairs={{0,12},{12,0},{24,36},{36,24},{48,60},{60,48},{72,84},{84,72},{96,... | collective-permute-start | bytes 1327112 | tf_op jit(solution)/shard_map/ppermute | solution.py:19
  271.1 1.4 collective-permute-done.35
  273.1 14.1 %all_to_all.22 = bf16[12,2,18,512]{3,1,2,0:T(2,128)(2,1)S(1)} all-to-all(bf16[12,2,18,512]{3,1,2,0:T(2,128)(2,1)S(1)} %copy.100), channel_id=1, replica_groups=mesh['pipe'=64,'expert'=12] {'expert'}, dimensions={0} | all-to-all | bytes 884736 | tf_op jit(solution)/shard_map/all_to_all | solution.py:140
  287.7 1.9 collective-permute-start.36
  289.6 9.9 %collective-permute-done.36 = bf16[2,96,256]{2,1,0:T(8,128)(2,1)S(1)} collective-permute-done((bf16[2,96,256]{2,1,0:T(8,128)(2,1)S(1)}, bf16[2,96,256]{2,1,0:T(8,128)(2,1)S(1)}, u32[]{:S(2)}, u32[]{:S(2)}) %collective-permute-start.36) | collective-permute-done | bytes 98336 | tf_op jit(solution)/shard_map/ppermute | solution.py:19
  299.5 1.6 fusion.67
  (161 shorter events, 25.2 us)
Async XLA Ops:
  0.0 9.9 %copy-start = (f32[1,2]{1,0:T(1,128)S(1)}, f32[1,2]{1,0:T(1,128)}, u32[]{:S(2)}) copy-start(f32[1,2]{1,0:T(1,128)} %param.13) | copy-start | bytes 28
  1.4 19.4 %collective-permute-start = (bf16[2,96,256]{2,1,0:T(8,128)(2,1)S(1)}, bf16[2,96,256]{2,1,0:T(8,128)(2,1)S(1)}, u32[]{:S(2)}, u32[]{:S(2)}) collective-permute-start(bf16[2,96,256]{2,1,0:T(8,128)(2,1)S(1)} %pad_maximum_fusion.15), channel_id=1, source_target_pairs={{0,24},{12,36},{24,0},{36,12},{48,72},{60,84},{72,48},{84,60},{96,... | collective-permute-start | bytes 294920 | tf_op jit(solution)/shard_map/ppermute | solution.py:19
  40.9 7.3 %copy-start.1 = (bf16[1024,1024]{1,0:T(8,128)(2,1)S(1)}, bf16[1024,1024]{1,0:T(8,128)(2,1)}, u32[]{:S(2)}) copy-start(bf16[1024,1024]{1,0:T(8,128)(2,1)} %get-tuple-element.28) | copy-start | bytes 6291460
  41.8 5.8 %collective-permute-start.1 = (bf16[432,512]{1,0:T(8,128)(2,1)}, bf16[432,512]{1,0:T(8,128)(2,1)S(1)}, u32[]{:S(2)}, u32[]{:S(2)}) collective-permute-start(bf16[432,512]{1,0:T(8,128)(2,1)} %reshape.214), channel_id=1, source_target_pairs={{0,12},{12,0},{24,36},{36,24},{48,60},{60,48},{72,84},{84,72},{96,... | collective-permute-start | bytes 1327112 | tf_op jit(solution)/shard_map/ppermute | solution.py:19
  49.6 16.9 %collective-permute-start.4 = (bf16[224,256]{1,0:T(8,128)(2,1)S(1)}, bf16[224,256]{1,0:T(8,128)(2,1)S(1)}, u32[]{:S(2)}, u32[]{:S(2)}) collective-permute-start(bf16[224,256]{1,0:T(8,128)(2,1)S(1)} %get-tuple-element.74), channel_id=1, source_target_pairs={{0,96},{12,108},{24,120},{36,132},{48,144},{60,156},{72,168},{84,1... | collective-permute-start | bytes 344072 | tf_op jit(solution)/shard_map/ppermute | solution.py:24
  52.8 15.6 %collective-permute-start.3 = (bf16[224,256]{1,0:T(8,128)(2,1)S(1)}, bf16[224,256]{1,0:T(8,128)(2,1)S(1)}, u32[]{:S(2)}, u32[]{:S(2)}) collective-permute-start(bf16[224,256]{1,0:T(8,128)(2,1)S(1)} %get-tuple-element.73), channel_id=1, source_target_pairs={{0,192},{12,204},{24,216},{36,228},{48,240},{60,252},{72,264},{84,... | collective-permute-start | bytes 344072 | tf_op jit(solution)/shard_map/ppermute | solution.py:24
  57.0 11.4 %collective-permute-start.2 = (bf16[224,256]{1,0:T(8,128)(2,1)S(1)}, bf16[224,256]{1,0:T(8,128)(2,1)S(1)}, u32[]{:S(2)}, u32[]{:S(2)}) collective-permute-start(bf16[224,256]{1,0:T(8,128)(2,1)S(1)} %get-tuple-element.72), channel_id=1, source_target_pairs={{0,288},{12,300},{24,312},{36,324},{48,336},{60,348},{72,360},{84,... | collective-permute-start | bytes 344072 | tf_op jit(solution)/shard_map/ppermute | solution.py:24
  59.1 20.5 %collective-permute-start.11 = (bf16[224,256]{1,0:T(8,128)(2,1)S(1)}, bf16[224,256]{1,0:T(8,128)(2,1)S(1)}, u32[]{:S(2)}, u32[]{:S(2)}) collective-permute-start(bf16[224,256]{1,0:T(8,128)(2,1)S(1)} %get-tuple-element.26), channel_id=1, source_target_pairs={{0,96},{12,108},{24,120},{36,132},{48,144},{60,156},{72,168},{84,1... | collective-permute-start | bytes 344072 | tf_op jit(solution)/shard_map/ppermute | solution.py:24
  61.3 18.3 %collective-permute-start.10 = (bf16[224,256]{1,0:T(8,128)(2,1)S(1)}, bf16[224,256]{1,0:T(8,128)(2,1)S(1)}, u32[]{:S(2)}, u32[]{:S(2)}) collective-permute-start(bf16[224,256]{1,0:T(8,128)(2,1)S(1)} %get-tuple-element.25), channel_id=1, source_target_pairs={{0,192},{12,204},{24,216},{36,228},{48,240},{60,252},{72,264},{84,... | collective-permute-start | bytes 344072 | tf_op jit(solution)/shard_map/ppermute | solution.py:24
  66.5 13.2 %collective-permute-start.9 = (bf16[224,256]{1,0:T(8,128)(2,1)S(1)}, bf16[224,256]{1,0:T(8,128)(2,1)S(1)}, u32[]{:S(2)}, u32[]{:S(2)}) collective-permute-start(bf16[224,256]{1,0:T(8,128)(2,1)S(1)} %get-tuple-element.24), channel_id=1, source_target_pairs={{0,288},{12,300},{24,312},{36,324},{48,336},{60,348},{72,360},{84,... | collective-permute-start | bytes 344072 | tf_op jit(solution)/shard_map/ppermute | solution.py:24
  68.5 37.1 %copy-start.2 = (bf16[1024,512]{1,0:T(8,128)(2,1)S(1)}, bf16[1024,512]{1,0:T(8,128)(2,1)}, u32[]{:S(2)}) copy-start(bf16[1024,512]{1,0:T(8,128)(2,1)} %get-tuple-element.29) | copy-start | bytes 3145732
  68.5 16.5 %collective-permute-start.5 = (bf16[224,256]{1,0:T(8,128)(2,1)S(1)}, bf16[224,256]{1,0:T(8,128)(2,1)S(1)}, u32[]{:S(2)}, u32[]{:S(2)}) collective-permute-start(bf16[224,256]{1,0:T(8,128)(2,1)S(1)} %fusion.111), channel_id=1, source_target_pairs={{0,48},{12,60},{24,72},{36,84},{48,0},{60,12},{72,24},{84,36},{96,... | collective-permute-start | bytes 344072 | tf_op jit(solution)/shard_map/ppermute | solution.py:19
  79.7 16.3 %collective-permute-start.12 = (bf16[224,256]{1,0:T(8,128)(2,1)S(1)}, bf16[224,256]{1,0:T(8,128)(2,1)S(1)}, u32[]{:S(2)}, u32[]{:S(2)}) collective-permute-start(bf16[224,256]{1,0:T(8,128)(2,1)S(1)} %fusion.110), channel_id=1, source_target_pairs={{0,48},{12,60},{24,72},{36,84},{48,0},{60,12},{72,24},{84,36},{96,... | collective-permute-start | bytes 344072 | tf_op jit(solution)/shard_map/ppermute | solution.py:19
  85.2 17.5 %collective-permute-start.8 = (bf16[216,128]{1,0:T(8,128)(2,1)S(1)}, bf16[216,128]{1,0:T(8,128)(2,1)S(1)}, u32[]{:S(2)}, u32[]{:S(2)}) collective-permute-start(bf16[216,128]{1,0:T(8,128)(2,1)S(1)} %fusion.71), channel_id=1, source_target_pairs={{0,288},{12,300},{24,312},{36,324},{48,336},{60,348},{72,360},{84,... | collective-permute-start | bytes 165896 | tf_op jit(solution)/shard_map/ppermute | solution.py:24
  90.3 15.3 %collective-permute-start.7 = (bf16[216,128]{1,0:T(8,128)(2,1)S(1)}, bf16[216,128]{1,0:T(8,128)(2,1)S(1)}, u32[]{:S(2)}, u32[]{:S(2)}) collective-permute-start(bf16[216,128]{1,0:T(8,128)(2,1)S(1)} %fusion.71), channel_id=1, source_target_pairs={{0,192},{12,204},{24,216},{36,228},{48,240},{60,252},{72,264},{84,... | collective-permute-start | bytes 165896 | tf_op jit(solution)/shard_map/ppermute | solution.py:24
  94.1 11.5 %collective-permute-start.6 = (bf16[216,128]{1,0:T(8,128)(2,1)S(1)}, bf16[216,128]{1,0:T(8,128)(2,1)S(1)}, u32[]{:S(2)}, u32[]{:S(2)}) collective-permute-start(bf16[216,128]{1,0:T(8,128)(2,1)S(1)} %fusion.71), channel_id=1, source_target_pairs={{0,96},{12,108},{24,120},{36,132},{48,144},{60,156},{72,168},{84,1... | collective-permute-start | bytes 165896 | tf_op jit(solution)/shard_map/ppermute | solution.py:24
  96.3 9.8 %collective-permute-start.15 = (bf16[216,128]{1,0:T(8,128)(2,1)S(1)}, bf16[216,128]{1,0:T(8,128)(2,1)S(1)}, u32[]{:S(2)}, u32[]{:S(2)}) collective-permute-start(bf16[216,128]{1,0:T(8,128)(2,1)S(1)} %fusion.70), channel_id=1, source_target_pairs={{0,288},{12,300},{24,312},{36,324},{48,336},{60,348},{72,360},{84,... | collective-permute-start | bytes 165896 | tf_op jit(solution)/shard_map/ppermute | solution.py:24
  100.2 6.9 %collective-permute-start.14 = (bf16[216,128]{1,0:T(8,128)(2,1)S(1)}, bf16[216,128]{1,0:T(8,128)(2,1)S(1)}, u32[]{:S(2)}, u32[]{:S(2)}) collective-permute-start(bf16[216,128]{1,0:T(8,128)(2,1)S(1)} %fusion.70), channel_id=1, source_target_pairs={{0,192},{12,204},{24,216},{36,228},{48,240},{60,252},{72,264},{84,... | collective-permute-start | bytes 165896 | tf_op jit(solution)/shard_map/ppermute | solution.py:24
  102.7 5.0 %collective-permute-start.13 = (bf16[216,128]{1,0:T(8,128)(2,1)S(1)}, bf16[216,128]{1,0:T(8,128)(2,1)S(1)}, u32[]{:S(2)}, u32[]{:S(2)}) collective-permute-start(bf16[216,128]{1,0:T(8,128)(2,1)S(1)} %fusion.70), channel_id=1, source_target_pairs={{0,96},{12,108},{24,120},{36,132},{48,144},{60,156},{72,168},{84,1... | collective-permute-start | bytes 165896 | tf_op jit(solution)/shard_map/ppermute | solution.py:24
  108.3 6.9 %collective-permute-start.16 = (bf16[432,512]{1,0:T(8,128)(2,1)S(1)}, bf16[432,512]{1,0:T(8,128)(2,1)S(1)}, u32[]{:S(2)}, u32[]{:S(2)}) collective-permute-start(bf16[432,512]{1,0:T(8,128)(2,1)S(1)} %fusion.7), channel_id=1, source_target_pairs={{0,12},{12,0},{24,36},{36,24},{48,60},{60,48},{72,84},{84,72},{96,... | collective-permute-start | bytes 1327112 | tf_op jit(solution)/shard_map/ppermute | solution.py:19
  120.3 15.0 %all-to-all-start.1 = ((bf16[12,2,18,512]{3,1,2,0:T(2,128)(2,1)}), bf16[12,2,18,512]{3,1,2,0:T(2,128)(2,1)}, u32[]{:S(2)}, u32[]{:S(2)}) async-start(bf16[12,2,18,512]{3,1,2,0:T(2,128)(2,1)} %copy.88), calls=%async_computation.1 | async-start | bytes 884736 | tf_op jit(solution)/shard_map/all_to_all | solution.py:140
  137.7 0.8 copy-start.3
  138.5 7.3 %collective-permute-start.17 = (bf16[2,96,256]{2,1,0:T(8,128)(2,1)S(1)}, bf16[2,96,256]{2,1,0:T(8,128)(2,1)}, u32[]{:S(2)}, u32[]{:S(2)}) collective-permute-start(bf16[2,96,256]{2,1,0:T(8,128)(2,1)S(1)} %slice.395), channel_id=1, source_target_pairs={{0,24},{12,36},{24,0},{36,12},{48,72},{60,84},{72,48},{84,60},{96,... | collective-permute-start | bytes 294920 | tf_op jit(solution)/shard_map/ppermute | solution.py:19
  147.5 9.7 %collective-permute-start.18 = (bf16[2,96,224]{2,1,0:T(8,128)(2,1)}, bf16[2,96,224]{2,1,0:T(8,128)(2,1)}, u32[]{:S(2)}, u32[]{:S(2)}) collective-permute-start(bf16[2,96,224]{2,1,0:T(8,128)(2,1)} %fusion.64), channel_id=1, source_target_pairs={{0,384},{12,396},{24,408},{36,420},{48,432},{60,444},{72,456},{84,... | collective-permute-start | bytes 258056 | tf_op jit(solution)/shard_map/ppermute | solution.py:29
  158.4 3.2 %copy-start.4 = (bf16[2,96,1]{2,1,0:T(8,128)(2,1)}, bf16[2,96,1]{2,1,0:T(8,128)(2,1)S(1)}, u32[]{:S(2)}) copy-start(bf16[2,96,1]{2,1,0:T(8,128)(2,1)S(1)} %copy.96) | copy-start | bytes 1156
  158.5 7.3 %collective-permute-start.19 = (bf16[2,96,256]{2,1,0:T(8,128)(2,1)S(1)}, bf16[2,96,256]{2,1,0:T(8,128)(2,1)}, u32[]{:S(2)}, u32[]{:S(2)}) collective-permute-start(bf16[2,96,256]{2,1,0:T(8,128)(2,1)S(1)} %pad_maximum_fusion.14), channel_id=1, source_target_pairs={{0,24},{12,36},{24,0},{36,12},{48,72},{60,84},{72,48},{84,60},{96,... | collective-permute-start | bytes 294920 | tf_op jit(solution)/shard_map/ppermute | solution.py:19
  189.1 10.1 %collective-permute-start.20 = (bf16[432,512]{1,0:T(8,128)(2,1)}, bf16[432,512]{1,0:T(8,128)(2,1)S(1)}, u32[]{:S(2)}, u32[]{:S(2)}) collective-permute-start(bf16[432,512]{1,0:T(8,128)(2,1)} %reshape.220), channel_id=1, source_target_pairs={{0,12},{12,0},{24,36},{36,24},{48,60},{60,48},{72,84},{84,72},{96,... | collective-permute-start | bytes 1327112 | tf_op jit(solution)/shard_map/ppermute | solution.py:19
  201.1 16.2 %collective-permute-start.23 = (bf16[224,256]{1,0:T(8,128)(2,1)S(1)}, bf16[224,256]{1,0:T(8,128)(2,1)S(1)}, u32[]{:S(2)}, u32[]{:S(2)}) collective-permute-start(bf16[224,256]{1,0:T(8,128)(2,1)S(1)} %get-tuple-element.68), channel_id=1, source_target_pairs={{0,96},{12,108},{24,120},{36,132},{48,144},{60,156},{72,168},{84,1... | collective-permute-start | bytes 344072 | tf_op jit(solution)/shard_map/ppermute | solution.py:24
  204.5 15.9 %collective-permute-start.22 = (bf16[224,256]{1,0:T(8,128)(2,1)S(1)}, bf16[224,256]{1,0:T(8,128)(2,1)S(1)}, u32[]{:S(2)}, u32[]{:S(2)}) collective-permute-start(bf16[224,256]{1,0:T(8,128)(2,1)S(1)} %get-tuple-element.67), channel_id=1, source_target_pairs={{0,192},{12,204},{24,216},{36,228},{48,240},{60,252},{72,264},{84,... | collective-permute-start | bytes 344072 | tf_op jit(solution)/shard_map/ppermute | solution.py:24
  207.9 12.5 %collective-permute-start.21 = (bf16[224,256]{1,0:T(8,128)(2,1)S(1)}, bf16[224,256]{1,0:T(8,128)(2,1)S(1)}, u32[]{:S(2)}, u32[]{:S(2)}) collective-permute-start(bf16[224,256]{1,0:T(8,128)(2,1)S(1)} %get-tuple-element.66), channel_id=1, source_target_pairs={{0,288},{12,300},{24,312},{36,324},{48,336},{60,348},{72,360},{84,... | collective-permute-start | bytes 344072 | tf_op jit(solution)/shard_map/ppermute | solution.py:24
  211.1 24.7 %collective-permute-start.30 = (bf16[224,256]{1,0:T(8,128)(2,1)S(1)}, bf16[224,256]{1,0:T(8,128)(2,1)S(1)}, u32[]{:S(2)}, u32[]{:S(2)}) collective-permute-start(bf16[224,256]{1,0:T(8,128)(2,1)S(1)} %get-tuple-element.32), channel_id=1, source_target_pairs={{0,96},{12,108},{24,120},{36,132},{48,144},{60,156},{72,168},{84,1... | collective-permute-start | bytes 344072 | tf_op jit(solution)/shard_map/ppermute | solution.py:24
  213.3 22.6 %collective-permute-start.29 = (bf16[224,256]{1,0:T(8,128)(2,1)S(1)}, bf16[224,256]{1,0:T(8,128)(2,1)S(1)}, u32[]{:S(2)}, u32[]{:S(2)}) collective-permute-start(bf16[224,256]{1,0:T(8,128)(2,1)S(1)} %get-tuple-element.31), channel_id=1, source_target_pairs={{0,192},{12,204},{24,216},{36,228},{48,240},{60,252},{72,264},{84,... | collective-permute-start | bytes 344072 | tf_op jit(solution)/shard_map/ppermute | solution.py:24
  217.4 18.5 %collective-permute-start.28 = (bf16[224,256]{1,0:T(8,128)(2,1)S(1)}, bf16[224,256]{1,0:T(8,128)(2,1)S(1)}, u32[]{:S(2)}, u32[]{:S(2)}) collective-permute-start(bf16[224,256]{1,0:T(8,128)(2,1)S(1)} %get-tuple-element.30), channel_id=1, source_target_pairs={{0,288},{12,300},{24,312},{36,324},{48,336},{60,348},{72,360},{84,... | collective-permute-start | bytes 344072 | tf_op jit(solution)/shard_map/ppermute | solution.py:24
  220.5 19.7 %collective-permute-start.24 = (bf16[224,256]{1,0:T(8,128)(2,1)S(1)}, bf16[224,256]{1,0:T(8,128)(2,1)S(1)}, u32[]{:S(2)}, u32[]{:S(2)}) collective-permute-start(bf16[224,256]{1,0:T(8,128)(2,1)S(1)} %fusion.109), channel_id=1, source_target_pairs={{0,48},{12,60},{24,72},{36,84},{48,0},{60,12},{72,24},{84,36},{96,... | collective-permute-start | bytes 344072 | tf_op jit(solution)/shard_map/ppermute | solution.py:19
  236.0 16.9 %collective-permute-start.31 = (bf16[224,256]{1,0:T(8,128)(2,1)S(1)}, bf16[224,256]{1,0:T(8,128)(2,1)S(1)}, u32[]{:S(2)}, u32[]{:S(2)}) collective-permute-start(bf16[224,256]{1,0:T(8,128)(2,1)S(1)} %fusion.108), channel_id=1, source_target_pairs={{0,48},{12,60},{24,72},{36,84},{48,0},{60,12},{72,24},{84,36},{96,... | collective-permute-start | bytes 344072 | tf_op jit(solution)/shard_map/ppermute | solution.py:19
  240.4 18.8 %collective-permute-start.27 = (bf16[216,128]{1,0:T(8,128)(2,1)S(1)}, bf16[216,128]{1,0:T(8,128)(2,1)S(1)}, u32[]{:S(2)}, u32[]{:S(2)}) collective-permute-start(bf16[216,128]{1,0:T(8,128)(2,1)S(1)} %fusion.69), channel_id=1, source_target_pairs={{0,288},{12,300},{24,312},{36,324},{48,336},{60,348},{72,360},{84,... | collective-permute-start | bytes 165896 | tf_op jit(solution)/shard_map/ppermute | solution.py:24
  247.1 15.3 %collective-permute-start.26 = (bf16[216,128]{1,0:T(8,128)(2,1)S(1)}, bf16[216,128]{1,0:T(8,128)(2,1)S(1)}, u32[]{:S(2)}, u32[]{:S(2)}) collective-permute-start(bf16[216,128]{1,0:T(8,128)(2,1)S(1)} %fusion.69), channel_id=1, source_target_pairs={{0,192},{12,204},{24,216},{36,228},{48,240},{60,252},{72,264},{84,... | collective-permute-start | bytes 165896 | tf_op jit(solution)/shard_map/ppermute | solution.py:24
  250.6 11.8 %collective-permute-start.25 = (bf16[216,128]{1,0:T(8,128)(2,1)S(1)}, bf16[216,128]{1,0:T(8,128)(2,1)S(1)}, u32[]{:S(2)}, u32[]{:S(2)}) collective-permute-start(bf16[216,128]{1,0:T(8,128)(2,1)S(1)} %fusion.69), channel_id=1, source_target_pairs={{0,96},{12,108},{24,120},{36,132},{48,144},{60,156},{72,168},{84,1... | collective-permute-start | bytes 165896 | tf_op jit(solution)/shard_map/ppermute | solution.py:24
  253.1 9.8 %collective-permute-start.34 = (bf16[216,128]{1,0:T(8,128)(2,1)S(1)}, bf16[216,128]{1,0:T(8,128)(2,1)S(1)}, u32[]{:S(2)}, u32[]{:S(2)}) collective-permute-start(bf16[216,128]{1,0:T(8,128)(2,1)S(1)} %fusion.68), channel_id=1, source_target_pairs={{0,288},{12,300},{24,312},{36,324},{48,336},{60,348},{72,360},{84,... | collective-permute-start | bytes 165896 | tf_op jit(solution)/shard_map/ppermute | solution.py:24
  257.1 7.0 %collective-permute-start.33 = (bf16[216,128]{1,0:T(8,128)(2,1)S(1)}, bf16[216,128]{1,0:T(8,128)(2,1)S(1)}, u32[]{:S(2)}, u32[]{:S(2)}) collective-permute-start(bf16[216,128]{1,0:T(8,128)(2,1)S(1)} %fusion.68), channel_id=1, source_target_pairs={{0,192},{12,204},{24,216},{36,228},{48,240},{60,252},{72,264},{84,... | collective-permute-start | bytes 165896 | tf_op jit(solution)/shard_map/ppermute | solution.py:24
  259.3 6.0 %collective-permute-start.32 = (bf16[216,128]{1,0:T(8,128)(2,1)S(1)}, bf16[216,128]{1,0:T(8,128)(2,1)S(1)}, u32[]{:S(2)}, u32[]{:S(2)}) collective-permute-start(bf16[216,128]{1,0:T(8,128)(2,1)S(1)} %fusion.68), channel_id=1, source_target_pairs={{0,96},{12,108},{24,120},{36,132},{48,144},{60,156},{72,168},{84,1... | collective-permute-start | bytes 165896 | tf_op jit(solution)/shard_map/ppermute | solution.py:24
  265.8 6.6 %collective-permute-start.35 = (bf16[432,512]{1,0:T(8,128)(2,1)S(1)}, bf16[432,512]{1,0:T(8,128)(2,1)S(1)}, u32[]{:S(2)}, u32[]{:S(2)}) collective-permute-start(bf16[432,512]{1,0:T(8,128)(2,1)S(1)} %fusion.6), channel_id=1, source_target_pairs={{0,12},{12,0},{24,36},{36,24},{48,60},{60,48},{72,84},{84,72},{96,... | collective-permute-start | bytes 1327112 | tf_op jit(solution)/shard_map/ppermute | solution.py:19
  287.7 11.9 %collective-permute-start.36 = (bf16[2,96,256]{2,1,0:T(8,128)(2,1)S(1)}, bf16[2,96,256]{2,1,0:T(8,128)(2,1)S(1)}, u32[]{:S(2)}, u32[]{:S(2)}) collective-permute-start(bf16[2,96,256]{2,1,0:T(8,128)(2,1)S(1)} %slice.394), channel_id=1, source_target_pairs={{0,24},{12,36},{24,0},{36,12},{48,72},{60,84},{72,48},{84,60},{96,... | collective-permute-start | bytes 294920 | tf_op jit(solution)/shard_map/ppermute | solution.py:19

commit v5 on v4

--- a/solution.py
+++ b/solution.py
@@ -100,16 +100,20 @@
     marks = jnp.broadcast_to(marks[None], (SQ_TILE, 4 * LANES))
     half = slots // 2
     parts = [inputs[:half], inputs[half:]]
-    blocks = [jnp.dot(part, w_in, preferred_element_type=jnp.float32) for part in parts]
+    kept = [jnp.dot(part, w_in[:, :256], preferred_element_type=jnp.float32) for part in parts]
+    sent = [
+        jnp.dot(part, w_in[:, 256:], preferred_element_type=jnp.float32).astype(jnp.bfloat16)
+        for part in parts
+    ]
     sums = [
         lax.dot_general(marks, part, DOT_ROWS, preferred_element_type=jnp.float32)
         for part in parts
     ]
     sums = [jnp.pad(row, ((0, 0), (0, LANES - half))) for row in sums]
     summed = []
-    for partial, row in zip(blocks, sums):
+    for partial, blocks, row in zip(kept, sent, sums):
         packed = [
-            jnp.concatenate([partial[:, k * 256 : k * 256 + 256], row]).astype(jnp.bfloat16)
+            jnp.concatenate([blocks[:, k * 256 - 256 : k * 256], row.astype(jnp.bfloat16)])
             for k in (3, 2, 1)
         ]
         if summed:
@@ -117,7 +121,7 @@
         first = packed
         got = [along_y(message, k) for message, k in zip(packed, (3, 2, 1))]
         got = sum(message.astype(jnp.float32) for message in got)
-        summed.append(jnp.concatenate([partial[:, :256], row]) + got)
+        summed.append(jnp.concatenate([partial, row]) + got)
     crossed = [total + exchange(total.astype(jnp.bfloat16), 2).astype(jnp.float32) for total in summed]
     hidden = []
     for total in crossed:

time: 303 us -> 293 us (0.967)
  local copies, waits for them, and re-layouts: 18.3 us -> 6.94 us
  other arithmetic: 14.8 us -> 8.88 us
  starting transfers between devices: 166 us -> 170 us
    ppermute x12, starting transfers between devices: 75.8 us -> 84.9 us  [exchange(): return lax.ppermute(x, 'pipe', [(i, i ^ 1 << bit) for i in range(size)])]
    ppermute x24, starting transfers between devices: 79.5 us -> 74.2 us  [along_y(): return lax.ppermute(x, 'pipe', [(i, i ^ apart << 3) for i in range(size)])]
    dot_general x4 -> x8, matrix products: 2.59 us -> 5.88 us  [the longest x4 3.57 us: layer(): jnp.dot(part, w_in[:, 256:], preferred_element_type=jnp.float32)]
  transfers between devices with their start and end apart: 38 -> 38, of which waited for: 13 -> 11; matrix products, arithmetic and copies ran while one was open for 5% -> 4% of each run, Pallas kernels for 2% -> 2%
where the time goes in v5:
time: 293 us; the launch traced here: 291 us
  starting transfers between devices  170 us (58%)
  blocking collectives  51.9 us (18%)
  waiting for transfers between devices  36.5 us (12%)
  matrix products  10.1 us (3%)
  other arithmetic  8.88 us (3%)
  local copies, waits for them, and re-layouts  6.94 us (2%)
  Pallas kernels  5.24 us (2%)
    ppermute x12, starting transfers between devices, exchange(): return lax.ppermute(x, 'pipe', [(i, i ^ 1 << bit) for i in range(size)])  84.9 us
    ppermute x24, starting transfers between devices, along_y(): return lax.ppermute(x, 'pipe', [(i, i ^ apart << 3) for i in range(size)])  74.2 us
    all_to_all x2, blocking collectives, layer(): lax.all_to_all(buffer.transpose(1, 0, 2, 3), 'expert', split_axis=0, conc...  37.8 us
    ppermute x12, waiting for transfers between devices, exchange(): return lax.ppermute(x, 'pipe', [(i, i ^ 1 << bit) for i in range(size)])  19.9 us
    all_to_all x1, blocking collectives, layer(): lax.all_to_all(expert_out, 'expert', split_axis=0, concat_axis=0, tiled=T...  14.1 us
    all_to_all x1, waiting for transfers between devices, layer(): lax.all_to_all(expert_out, 'expert', split_axis=0, concat_axis=0, tiled=T...  8.46 us
    ppermute x1, starting transfers between devices, other_section(): lax.ppermute(x, 'pipe', [(i, (i + size // 2) % size) for i in range(size)])  7.28 us
    ppermute x24, waiting for transfers between devices, along_y(): return lax.ppermute(x, 'pipe', [(i, i ^ apart << 3) for i in range(size)])  6.21 us
  transfers between devices with their start and end apart: 38, of which 11 were waited for; matrix products, arithmetic and copies ran while one was open for 4% of the time, Pallas kernels for 2%

profile of v5, /device:TPU:1, one launch (start us, length us, event | category | flops | bytes accessed | tf_op | source)
XLA Modules:
  0.0 291.3 jit_solution(9448644930240827113)
XLA Ops:
  0.0 1.0 fusion.90
  1.4 8.4 %collective-permute-start = (bf16[2,96,256]{2,1,0:T(8,128)(2,1)S(1)}, bf16[2,96,256]{2,1,0:T(8,128)(2,1)S(1)}, u32[]{:S(2)}, u32[]{:S(2)}) collective-permute-start(bf16[2,96,256]{2,1,0:T(8,128)(2,1)S(1)} %pad_maximum_fusion.15), channel_id=1, source_target_pairs={{0,24},{12,36},{24,0},{36,12},{48,72},{60,84},{72,48},{84,60},{96,... | collective-permute-start | bytes 294920 | tf_op jit(solution)/shard_map/ppermute | solution.py:19
  9.9 0.7 constant_dynamic-slice_fusion.1
  10.6 0.7 constant_dynamic-slice_fusion.3
  11.7 1.2 reduce-window.14
  13.5 0.7 fusion.121
  14.8 0.7 bitcast_divide_fusion
  15.5 5.2 %shard_map.82 = (bf16[1024,1024]{1,0:T(8,128)(2,1)}, bf16[1024,512]{1,0:T(8,128)(2,1)}) custom-call(s32[2]{0:T(128)} %pad_add_fusion.where, bf16[896,1024]{1,0:T(8,128)(2,1)} %bitcast.68, bf16[896,512]{1,0:T(8,128)(2,1)} %bitcast.71, bf16[896,512]{1,0:T(8,128)(2,1)} %bitcast.72, f32[1]{0:T(128)} %bitcast.9.rate), custom_call_target="tpu_custom_call" | custom-call | flops 2000000 | bytes 8000000 | tf_op jit(solution)/shard_map/pallas_call | solution.py:55
  21.8 19.2 %all_to_all.20 = bf16[12,2,18,512]{3,1,2,0:T(2,128)(2,1)S(1)} all-to-all(bf16[12,2,18,512]{3,1,2,0:T(2,128)(2,1)S(1)} %bitcast.69), channel_id=1, replica_groups=mesh['pipe'=64,'expert'=12] {'expert'}, dimensions={0} | all-to-all | bytes 884736 | tf_op jit(solution)/shard_map/all_to_all | solution.py:92
  41.2 4.2 %collective-permute-start.1 = (bf16[432,512]{1,0:T(8,128)(2,1)S(1)}, bf16[432,512]{1,0:T(8,128)(2,1)S(1)}, u32[]{:S(2)}, u32[]{:S(2)}) collective-permute-start(bf16[432,512]{1,0:T(8,128)(2,1)S(1)} %reshape.214), channel_id=1, source_target_pairs={{0,12},{12,0},{24,36},{36,24},{48,60},{60,48},{72,84},{84,72},{96,... | collective-permute-start | bytes 1327112 | tf_op jit(solution)/shard_map/ppermute | solution.py:19
  45.5 1.3 collective-permute-done.1
  46.9 1.9 fusion.11
  50.3 4.2 %collective-permute-start.10 = (bf16[224,256]{1,0:T(8,128)(2,1)S(1)}, bf16[224,256]{1,0:T(8,128)(2,1)S(1)}, u32[]{:S(2)}, u32[]{:S(2)}) collective-permute-start(bf16[224,256]{1,0:T(8,128)(2,1)S(1)} %get-tuple-element.25), channel_id=1, source_target_pairs={{0,192},{12,204},{24,216},{36,228},{48,240},{60,252},{72,264},{84,... | collective-permute-start | bytes 344072 | tf_op jit(solution)/shard_map/ppermute | solution.py:24
  54.6 3.2 %collective-permute-start.11 = (bf16[224,256]{1,0:T(8,128)(2,1)S(1)}, bf16[224,256]{1,0:T(8,128)(2,1)S(1)}, u32[]{:S(2)}, u32[]{:S(2)}) collective-permute-start(bf16[224,256]{1,0:T(8,128)(2,1)S(1)} %get-tuple-element.26), channel_id=1, source_target_pairs={{0,96},{12,108},{24,120},{36,132},{48,144},{60,156},{72,168},{84,1... | collective-permute-start | bytes 344072 | tf_op jit(solution)/shard_map/ppermute | solution.py:24
  57.8 1.9 collective-permute-start.9
  60.0 5.2 %collective-permute-start.2 = (bf16[224,256]{1,0:T(8,128)(2,1)S(1)}, bf16[224,256]{1,0:T(8,128)(2,1)S(1)}, u32[]{:S(2)}, u32[]{:S(2)}) collective-permute-start(bf16[224,256]{1,0:T(8,128)(2,1)S(1)} %get-tuple-element.72), channel_id=1, source_target_pairs={{0,288},{12,300},{24,312},{36,324},{48,336},{60,348},{72,360},{84,... | collective-permute-start | bytes 344072 | tf_op jit(solution)/shard_map/ppermute | solution.py:24
  65.2 1.9 collective-permute-start.3
  67.2 2.2 collective-permute-start.4
  69.5 11.1 %collective-permute-start.12 = (bf16[224,256]{1,0:T(8,128)(2,1)S(1)}, bf16[224,256]{1,0:T(8,128)(2,1)S(1)}, u32[]{:S(2)}, u32[]{:S(2)}) collective-permute-start(bf16[224,256]{1,0:T(8,128)(2,1)S(1)} %fusion.138), channel_id=1, source_target_pairs={{0,48},{12,60},{24,72},{36,84},{48,0},{60,12},{72,24},{84,36},{96,... | collective-permute-start | bytes 344072 | tf_op jit(solution)/shard_map/ppermute | solution.py:19
  80.7 7.0 %collective-permute-start.5 = (bf16[224,256]{1,0:T(8,128)(2,1)S(1)}, bf16[224,256]{1,0:T(8,128)(2,1)S(1)}, u32[]{:S(2)}, u32[]{:S(2)}) collective-permute-start(bf16[224,256]{1,0:T(8,128)(2,1)S(1)} %fusion.139), channel_id=1, source_target_pairs={{0,48},{12,60},{24,72},{36,84},{48,0},{60,12},{72,24},{84,36},{96,... | collective-permute-start | bytes 344072 | tf_op jit(solution)/shard_map/ppermute | solution.py:19
  87.9 1.9 collective-permute-start.13
  89.8 3.9 %collective-permute-start.14 = (bf16[216,128]{1,0:T(8,128)(2,1)S(1)}, bf16[216,128]{1,0:T(8,128)(2,1)S(1)}, u32[]{:S(2)}, u32[]{:S(2)}) collective-permute-start(bf16[216,128]{1,0:T(8,128)(2,1)S(1)} %fusion.98), channel_id=1, source_target_pairs={{0,192},{12,204},{24,216},{36,228},{48,240},{60,252},{72,264},{84,... | collective-permute-start | bytes 165896 | tf_op jit(solution)/shard_map/ppermute | solution.py:24
  93.8 3.4 %collective-permute-start.15 = (bf16[216,128]{1,0:T(8,128)(2,1)S(1)}, bf16[216,128]{1,0:T(8,128)(2,1)S(1)}, u32[]{:S(2)}, u32[]{:S(2)}) collective-permute-start(bf16[216,128]{1,0:T(8,128)(2,1)S(1)} %fusion.98), channel_id=1, source_target_pairs={{0,288},{12,300},{24,312},{36,324},{48,336},{60,348},{72,360},{84,... | collective-permute-start | bytes 165896 | tf_op jit(solution)/shard_map/ppermute | solution.py:24
  97.5 2.2 collective-permute-start.6
  99.6 3.7 %collective-permute-start.7 = (bf16[216,128]{1,0:T(8,128)(2,1)S(1)}, bf16[216,128]{1,0:T(8,128)(2,1)S(1)}, u32[]{:S(2)}, u32[]{:S(2)}) collective-permute-start(bf16[216,128]{1,0:T(8,128)(2,1)S(1)} %fusion.99), channel_id=1, source_target_pairs={{0,192},{12,204},{24,216},{36,228},{48,240},{60,252},{72,264},{84,... | collective-permute-start | bytes 165896 | tf_op jit(solution)/shard_map/ppermute | solution.py:24
  103.3 3.4 %collective-permute-start.8 = (bf16[216,128]{1,0:T(8,128)(2,1)S(1)}, bf16[216,128]{1,0:T(8,128)(2,1)S(1)}, u32[]{:S(2)}, u32[]{:S(2)}) collective-permute-start(bf16[216,128]{1,0:T(8,128)(2,1)S(1)} %fusion.99), channel_id=1, source_target_pairs={{0,288},{12,300},{24,312},{36,324},{48,336},{60,348},{72,360},{84,... | collective-permute-start | bytes 165896 | tf_op jit(solution)/shard_map/ppermute | solution.py:24
  107.3 3.3 %collective-permute-done.8 = bf16[216,128]{1,0:T(8,128)(2,1)S(1)} collective-permute-done((bf16[216,128]{1,0:T(8,128)(2,1)S(1)}, bf16[216,128]{1,0:T(8,128)(2,1)S(1)}, u32[]{:S(2)}, u32[]{:S(2)}) %collective-permute-start.8) | collective-permute-done | bytes 55328 | tf_op jit(solution)/shard_map/ppermute | solution.py:24
  111.1 6.3 %collective-permute-start.16 = (bf16[432,512]{1,0:T(8,128)(2,1)S(1)}, bf16[432,512]{1,0:T(8,128)(2,1)S(1)}, u32[]{:S(2)}, u32[]{:S(2)}) collective-permute-start(bf16[432,512]{1,0:T(8,128)(2,1)S(1)} %fusion.27), channel_id=1, source_target_pairs={{0,12},{12,0},{24,36},{36,24},{48,60},{60,48},{72,84},{84,72},{96,... | collective-permute-start | bytes 1327112 | tf_op jit(solution)/shard_map/ppermute | solution.py:19
  117.4 1.4 collective-permute-done.16
  119.1 1.1 copy.88
  120.2 4.0 %all-to-all-start.1 = ((bf16[12,2,18,512]{3,1,2,0:T(2,128)(2,1)}), bf16[12,2,18,512]{3,1,2,0:T(2,128)(2,1)S(1)}, u32[]{:S(2)}, u32[]{:S(2)}) async-start(bf16[12,2,18,512]{3,1,2,0:T(2,128)(2,1)} %copy.88), calls=%async_computation.1 | async-start | bytes 884736 | tf_op jit(solution)/shard_map/all_to_all | solution.py:144
  124.6 1.2 reduce-window.16
  126.2 8.5 %all-to-all-done.1 = bf16[12,2,18,512]{3,1,2,0:T(2,128)(2,1)S(1)} async-done(((bf16[12,2,18,512]{3,1,2,0:T(2,128)(2,1)}), bf16[12,2,18,512]{3,1,2,0:T(2,128)(2,1)S(1)}, u32[]{:S(2)}, u32[]{:S(2)}) %all-to-all-start.1) | async-done | bytes 442400 | tf_op jit(solution)/shard_map/all_to_all | solution.py:144
  135.1 4.1 %collective-permute-start.17 = (bf16[2,96,256]{2,1,0:T(8,128)(2,1)S(1)}, bf16[2,96,256]{2,1,0:T(8,128)(2,1)S(1)}, u32[]{:S(2)}, u32[]{:S(2)}) collective-permute-start(bf16[2,96,256]{2,1,0:T(8,128)(2,1)S(1)} %slice.415), channel_id=1, source_target_pairs={{0,24},{12,36},{24,0},{36,12},{48,72},{60,84},{72,48},{84,60},{96,... | collective-permute-start | bytes 294920 | tf_op jit(solution)/shard_map/ppermute | solution.py:19
  139.4 2.9 collective-permute-done.17
  142.3 7.3 %collective-permute-start.18 = (bf16[2,96,224]{2,1,0:T(8,128)(2,1)S(1)}, bf16[2,96,224]{2,1,0:T(8,128)(2,1)S(1)}, u32[]{:S(2)}, u32[]{:S(2)}) collective-permute-start(bf16[2,96,224]{2,1,0:T(8,128)(2,1)S(1)} %fusion.92), channel_id=1, source_target_pairs={{0,384},{12,396},{24,408},{36,420},{48,432},{60,444},{72,456},{84,... | collective-permute-start | bytes 258056 | tf_op jit(solution)/shard_map/ppermute | solution.py:29
  149.7 1.9 collective-permute-done.18
  152.1 5.4 %collective-permute-start.19 = (bf16[2,96,256]{2,1,0:T(8,128)(2,1)S(1)}, bf16[2,96,256]{2,1,0:T(8,128)(2,1)S(1)}, u32[]{:S(2)}, u32[]{:S(2)}) collective-permute-start(bf16[2,96,256]{2,1,0:T(8,128)(2,1)S(1)} %pad_maximum_fusion.14), channel_id=1, source_target_pairs={{0,24},{12,36},{24,0},{36,12},{48,72},{60,84},{72,48},{84,60},{96,... | collective-permute-start | bytes 294920 | tf_op jit(solution)/shard_map/ppermute | solution.py:19
  157.7 1.8 collective-permute-done.19
  160.3 18.6 %all_to_all.21 = bf16[12,2,18,512]{3,1,2,0:T(2,128)(2,1)S(1)} all-to-all(bf16[12,2,18,512]{3,1,2,0:T(2,128)(2,1)S(1)} %bitcast.70), channel_id=1, replica_groups=mesh['pipe'=64,'expert'=12] {'expert'}, dimensions={0} | all-to-all | bytes 884736 | tf_op jit(solution)/shard_map/all_to_all | solution.py:92
  179.1 7.0 %collective-permute-start.20 = (bf16[432,512]{1,0:T(8,128)(2,1)S(1)}, bf16[432,512]{1,0:T(8,128)(2,1)S(1)}, u32[]{:S(2)}, u32[]{:S(2)}) collective-permute-start(bf16[432,512]{1,0:T(8,128)(2,1)S(1)} %reshape.220), channel_id=1, source_target_pairs={{0,12},{12,0},{24,36},{36,24},{48,60},{60,48},{72,84},{84,72},{96,... | collective-permute-start | bytes 1327112 | tf_op jit(solution)/shard_map/ppermute | solution.py:19
  186.2 1.2 collective-permute-done.20
  187.4 1.3 fusion.28
  190.5 4.0 %collective-permute-start.28 = (bf16[224,256]{1,0:T(8,128)(2,1)S(1)}, bf16[224,256]{1,0:T(8,128)(2,1)S(1)}, u32[]{:S(2)}, u32[]{:S(2)}) collective-permute-start(bf16[224,256]{1,0:T(8,128)(2,1)S(1)} %get-tuple-element.30), channel_id=1, source_target_pairs={{0,288},{12,300},{24,312},{36,324},{48,336},{60,348},{72,360},{84,... | collective-permute-start | bytes 344072 | tf_op jit(solution)/shard_map/ppermute | solution.py:24
  194.5 1.9 collective-permute-start.29
  196.4 3.4 %collective-permute-start.30 = (bf16[224,256]{1,0:T(8,128)(2,1)S(1)}, bf16[224,256]{1,0:T(8,128)(2,1)S(1)}, u32[]{:S(2)}, u32[]{:S(2)}) collective-permute-start(bf16[224,256]{1,0:T(8,128)(2,1)S(1)} %get-tuple-element.32), channel_id=1, source_target_pairs={{0,96},{12,108},{24,120},{36,132},{48,144},{60,156},{72,168},{84,1... | collective-permute-start | bytes 344072 | tf_op jit(solution)/shard_map/ppermute | solution.py:24
  200.1 4.0 %collective-permute-start.21 = (bf16[224,256]{1,0:T(8,128)(2,1)S(1)}, bf16[224,256]{1,0:T(8,128)(2,1)S(1)}, u32[]{:S(2)}, u32[]{:S(2)}) collective-permute-start(bf16[224,256]{1,0:T(8,128)(2,1)S(1)} %get-tuple-element.66), channel_id=1, source_target_pairs={{0,288},{12,300},{24,312},{36,324},{48,336},{60,348},{72,360},{84,... | collective-permute-start | bytes 344072 | tf_op jit(solution)/shard_map/ppermute | solution.py:24
  204.1 1.9 collective-permute-start.22
  206.0 3.4 %collective-permute-start.23 = (bf16[224,256]{1,0:T(8,128)(2,1)S(1)}, bf16[224,256]{1,0:T(8,128)(2,1)S(1)}, u32[]{:S(2)}, u32[]{:S(2)}) collective-permute-start(bf16[224,256]{1,0:T(8,128)(2,1)S(1)} %get-tuple-element.68), channel_id=1, source_target_pairs={{0,96},{12,108},{24,120},{36,132},{48,144},{60,156},{72,168},{84,1... | collective-permute-start | bytes 344072 | tf_op jit(solution)/shard_map/ppermute | solution.py:24
  209.5 15.4 %collective-permute-start.31 = (bf16[224,256]{1,0:T(8,128)(2,1)S(1)}, bf16[224,256]{1,0:T(8,128)(2,1)S(1)}, u32[]{:S(2)}, u32[]{:S(2)}) collective-permute-start(bf16[224,256]{1,0:T(8,128)(2,1)S(1)} %fusion.136), channel_id=1, source_target_pairs={{0,48},{12,60},{24,72},{36,84},{48,0},{60,12},{72,24},{84,36},{96,... | collective-permute-start | bytes 344072 | tf_op jit(solution)/shard_map/ppermute | solution.py:19
  225.1 4.8 %collective-permute-start.24 = (bf16[224,256]{1,0:T(8,128)(2,1)S(1)}, bf16[224,256]{1,0:T(8,128)(2,1)S(1)}, u32[]{:S(2)}, u32[]{:S(2)}) collective-permute-start(bf16[224,256]{1,0:T(8,128)(2,1)S(1)} %fusion.137), channel_id=1, source_target_pairs={{0,48},{12,60},{24,72},{36,84},{48,0},{60,12},{72,24},{84,36},{96,... | collective-permute-start | bytes 344072 | tf_op jit(solution)/shard_map/ppermute | solution.py:19
  230.1 1.9 collective-permute-start.32
  232.1 4.1 %collective-permute-start.33 = (bf16[216,128]{1,0:T(8,128)(2,1)S(1)}, bf16[216,128]{1,0:T(8,128)(2,1)S(1)}, u32[]{:S(2)}, u32[]{:S(2)}) collective-permute-start(bf16[216,128]{1,0:T(8,128)(2,1)S(1)} %fusion.96), channel_id=1, source_target_pairs={{0,192},{12,204},{24,216},{36,228},{48,240},{60,252},{72,264},{84,... | collective-permute-start | bytes 165896 | tf_op jit(solution)/shard_map/ppermute | solution.py:24
  236.1 3.3 %collective-permute-start.34 = (bf16[216,128]{1,0:T(8,128)(2,1)S(1)}, bf16[216,128]{1,0:T(8,128)(2,1)S(1)}, u32[]{:S(2)}, u32[]{:S(2)}) collective-permute-start(bf16[216,128]{1,0:T(8,128)(2,1)S(1)} %fusion.96), channel_id=1, source_target_pairs={{0,288},{12,300},{24,312},{36,324},{48,336},{60,348},{72,360},{84,... | collective-permute-start | bytes 165896 | tf_op jit(solution)/shard_map/ppermute | solution.py:24
  239.7 1.9 collective-permute-start.25
  241.6 4.1 %collective-permute-start.26 = (bf16[216,128]{1,0:T(8,128)(2,1)S(1)}, bf16[216,128]{1,0:T(8,128)(2,1)S(1)}, u32[]{:S(2)}, u32[]{:S(2)}) collective-permute-start(bf16[216,128]{1,0:T(8,128)(2,1)S(1)} %fusion.97), channel_id=1, source_target_pairs={{0,192},{12,204},{24,216},{36,228},{48,240},{60,252},{72,264},{84,... | collective-permute-start | bytes 165896 | tf_op jit(solution)/shard_map/ppermute | solution.py:24
  245.7 3.3 %collective-permute-start.27 = (bf16[216,128]{1,0:T(8,128)(2,1)S(1)}, bf16[216,128]{1,0:T(8,128)(2,1)S(1)}, u32[]{:S(2)}, u32[]{:S(2)}) collective-permute-start(bf16[216,128]{1,0:T(8,128)(2,1)S(1)} %fusion.97), channel_id=1, source_target_pairs={{0,288},{12,300},{24,312},{36,324},{48,336},{60,348},{72,360},{84,... | collective-permute-start | bytes 165896 | tf_op jit(solution)/shard_map/ppermute | solution.py:24
  249.5 2.9 collective-permute-done.27
  252.9 9.2 %collective-permute-start.35 = (bf16[432,512]{1,0:T(8,128)(2,1)S(1)}, bf16[432,512]{1,0:T(8,128)(2,1)S(1)}, u32[]{:S(2)}, u32[]{:S(2)}) collective-permute-start(bf16[432,512]{1,0:T(8,128)(2,1)S(1)} %fusion.26), channel_id=1, source_target_pairs={{0,12},{12,0},{24,36},{36,24},{48,60},{60,48},{72,84},{84,72},{96,... | collective-permute-start | bytes 1327112 | tf_op jit(solution)/shard_map/ppermute | solution.py:19
  262.1 1.4 collective-permute-done.35
  264.1 14.1 %all_to_all.22 = bf16[12,2,18,512]{3,1,2,0:T(2,128)(2,1)S(1)} all-to-all(bf16[12,2,18,512]{3,1,2,0:T(2,128)(2,1)S(1)} %copy.100), channel_id=1, replica_groups=mesh['pipe'=64,'expert'=12] {'expert'}, dimensions={0} | all-to-all | bytes 884736 | tf_op jit(solution)/shard_map/all_to_all | solution.py:144
  278.7 1.9 collective-permute-start.36
  280.6 9.9 %collective-permute-done.36 = bf16[2,96,256]{2,1,0:T(8,128)(2,1)S(1)} collective-permute-done((bf16[2,96,256]{2,1,0:T(8,128)(2,1)S(1)}, bf16[2,96,256]{2,1,0:T(8,128)(2,1)S(1)}, u32[]{:S(2)}, u32[]{:S(2)}) %collective-permute-start.36) | collective-permute-done | bytes 98336 | tf_op jit(solution)/shard_map/ppermute | solution.py:19
  290.6 0.7 fusion.95
  (163 shorter events, 14.9 us)
Async XLA Ops:
  0.0 9.9 %copy-start = (f32[1,2]{1,0:T(1,128)S(1)}, f32[1,2]{1,0:T(1,128)}, u32[]{:S(2)}) copy-start(f32[1,2]{1,0:T(1,128)} %param.13) | copy-start | bytes 28
  1.4 19.5 %collective-permute-start = (bf16[2,96,256]{2,1,0:T(8,128)(2,1)S(1)}, bf16[2,96,256]{2,1,0:T(8,128)(2,1)S(1)}, u32[]{:S(2)}, u32[]{:S(2)}) collective-permute-start(bf16[2,96,256]{2,1,0:T(8,128)(2,1)S(1)} %pad_maximum_fusion.15), channel_id=1, source_target_pairs={{0,24},{12,36},{24,0},{36,12},{48,72},{60,84},{72,48},{84,60},{96,... | collective-permute-start | bytes 294920 | tf_op jit(solution)/shard_map/ppermute | solution.py:19
  41.2 5.6 %collective-permute-start.1 = (bf16[432,512]{1,0:T(8,128)(2,1)S(1)}, bf16[432,512]{1,0:T(8,128)(2,1)S(1)}, u32[]{:S(2)}, u32[]{:S(2)}) collective-permute-start(bf16[432,512]{1,0:T(8,128)(2,1)S(1)} %reshape.214), channel_id=1, source_target_pairs={{0,12},{12,0},{24,36},{36,24},{48,60},{60,48},{72,84},{84,72},{96,... | collective-permute-start | bytes 1327112 | tf_op jit(solution)/shard_map/ppermute | solution.py:19
  45.5 3.3 %copy-start.4 = (bf16[1024,1024]{1,0:T(8,128)(2,1)S(1)}, bf16[1024,1024]{1,0:T(8,128)(2,1)}, u32[]{:S(2)}) copy-start(bf16[1024,1024]{1,0:T(8,128)(2,1)} %get-tuple-element.28) | copy-start | bytes 6291460
  50.3 16.8 %collective-permute-start.10 = (bf16[224,256]{1,0:T(8,128)(2,1)S(1)}, bf16[224,256]{1,0:T(8,128)(2,1)S(1)}, u32[]{:S(2)}, u32[]{:S(2)}) collective-permute-start(bf16[224,256]{1,0:T(8,128)(2,1)S(1)} %get-tuple-element.25), channel_id=1, source_target_pairs={{0,192},{12,204},{24,216},{36,228},{48,240},{60,252},{72,264},{84,... | collective-permute-start | bytes 344072 | tf_op jit(solution)/shard_map/ppermute | solution.py:24
  54.6 14.8 %collective-permute-start.11 = (bf16[224,256]{1,0:T(8,128)(2,1)S(1)}, bf16[224,256]{1,0:T(8,128)(2,1)S(1)}, u32[]{:S(2)}, u32[]{:S(2)}) collective-permute-start(bf16[224,256]{1,0:T(8,128)(2,1)S(1)} %get-tuple-element.26), channel_id=1, source_target_pairs={{0,96},{12,108},{24,120},{36,132},{48,144},{60,156},{72,168},{84,1... | collective-permute-start | bytes 344072 | tf_op jit(solution)/shard_map/ppermute | solution.py:24
  57.8 11.6 %collective-permute-start.9 = (bf16[224,256]{1,0:T(8,128)(2,1)S(1)}, bf16[224,256]{1,0:T(8,128)(2,1)S(1)}, u32[]{:S(2)}, u32[]{:S(2)}) collective-permute-start(bf16[224,256]{1,0:T(8,128)(2,1)S(1)} %get-tuple-element.24), channel_id=1, source_target_pairs={{0,288},{12,300},{24,312},{36,324},{48,336},{60,348},{72,360},{84,... | collective-permute-start | bytes 344072 | tf_op jit(solution)/shard_map/ppermute | solution.py:24
  60.0 20.5 %collective-permute-start.2 = (bf16[224,256]{1,0:T(8,128)(2,1)S(1)}, bf16[224,256]{1,0:T(8,128)(2,1)S(1)}, u32[]{:S(2)}, u32[]{:S(2)}) collective-permute-start(bf16[224,256]{1,0:T(8,128)(2,1)S(1)} %get-tuple-element.72), channel_id=1, source_target_pairs={{0,288},{12,300},{24,312},{36,324},{48,336},{60,348},{72,360},{84,... | collective-permute-start | bytes 344072 | tf_op jit(solution)/shard_map/ppermute | solution.py:24
  65.2 15.4 %collective-permute-start.3 = (bf16[224,256]{1,0:T(8,128)(2,1)S(1)}, bf16[224,256]{1,0:T(8,128)(2,1)S(1)}, u32[]{:S(2)}, u32[]{:S(2)}) collective-permute-start(bf16[224,256]{1,0:T(8,128)(2,1)S(1)} %get-tuple-element.73), channel_id=1, source_target_pairs={{0,192},{12,204},{24,216},{36,228},{48,240},{60,252},{72,264},{84,... | collective-permute-start | bytes 344072 | tf_op jit(solution)/shard_map/ppermute | solution.py:24
  67.2 13.4 %collective-permute-start.4 = (bf16[224,256]{1,0:T(8,128)(2,1)S(1)}, bf16[224,256]{1,0:T(8,128)(2,1)S(1)}, u32[]{:S(2)}, u32[]{:S(2)}) collective-permute-start(bf16[224,256]{1,0:T(8,128)(2,1)S(1)} %get-tuple-element.74), channel_id=1, source_target_pairs={{0,96},{12,108},{24,120},{36,132},{48,144},{60,156},{72,168},{84,1... | collective-permute-start | bytes 344072 | tf_op jit(solution)/shard_map/ppermute | solution.py:24
  69.4 37.3 %copy-start.1 = (bf16[1024,512]{1,0:T(8,128)(2,1)S(1)}, bf16[1024,512]{1,0:T(8,128)(2,1)}, u32[]{:S(2)}) copy-start(bf16[1024,512]{1,0:T(8,128)(2,1)} %get-tuple-element.29) | copy-start | bytes 3145732
  69.5 18.2 %collective-permute-start.12 = (bf16[224,256]{1,0:T(8,128)(2,1)S(1)}, bf16[224,256]{1,0:T(8,128)(2,1)S(1)}, u32[]{:S(2)}, u32[]{:S(2)}) collective-permute-start(bf16[224,256]{1,0:T(8,128)(2,1)S(1)} %fusion.138), channel_id=1, source_target_pairs={{0,48},{12,60},{24,72},{36,84},{48,0},{60,12},{72,24},{84,36},{96,... | collective-permute-start | bytes 344072 | tf_op jit(solution)/shard_map/ppermute | solution.py:19
  80.7 16.5 %collective-permute-start.5 = (bf16[224,256]{1,0:T(8,128)(2,1)S(1)}, bf16[224,256]{1,0:T(8,128)(2,1)S(1)}, u32[]{:S(2)}, u32[]{:S(2)}) collective-permute-start(bf16[224,256]{1,0:T(8,128)(2,1)S(1)} %fusion.139), channel_id=1, source_target_pairs={{0,48},{12,60},{24,72},{36,84},{48,0},{60,12},{72,24},{84,36},{96,... | collective-permute-start | bytes 344072 | tf_op jit(solution)/shard_map/ppermute | solution.py:19
  87.9 15.4 %collective-permute-start.13 = (bf16[216,128]{1,0:T(8,128)(2,1)S(1)}, bf16[216,128]{1,0:T(8,128)(2,1)S(1)}, u32[]{:S(2)}, u32[]{:S(2)}) collective-permute-start(bf16[216,128]{1,0:T(8,128)(2,1)S(1)} %fusion.98), channel_id=1, source_target_pairs={{0,96},{12,108},{24,120},{36,132},{48,144},{60,156},{72,168},{84,1... | collective-permute-start | bytes 165896 | tf_op jit(solution)/shard_map/ppermute | solution.py:24
  89.8 16.9 %collective-permute-start.14 = (bf16[216,128]{1,0:T(8,128)(2,1)S(1)}, bf16[216,128]{1,0:T(8,128)(2,1)S(1)}, u32[]{:S(2)}, u32[]{:S(2)}) collective-permute-start(bf16[216,128]{1,0:T(8,128)(2,1)S(1)} %fusion.98), channel_id=1, source_target_pairs={{0,192},{12,204},{24,216},{36,228},{48,240},{60,252},{72,264},{84,... | collective-permute-start | bytes 165896 | tf_op jit(solution)/shard_map/ppermute | solution.py:24
  93.8 13.0 %collective-permute-start.15 = (bf16[216,128]{1,0:T(8,128)(2,1)S(1)}, bf16[216,128]{1,0:T(8,128)(2,1)S(1)}, u32[]{:S(2)}, u32[]{:S(2)}) collective-permute-start(bf16[216,128]{1,0:T(8,128)(2,1)S(1)} %fusion.98), channel_id=1, source_target_pairs={{0,288},{12,300},{24,312},{36,324},{48,336},{60,348},{72,360},{84,... | collective-permute-start | bytes 165896 | tf_op jit(solution)/shard_map/ppermute | solution.py:24
  97.5 9.8 %collective-permute-start.6 = (bf16[216,128]{1,0:T(8,128)(2,1)S(1)}, bf16[216,128]{1,0:T(8,128)(2,1)S(1)}, u32[]{:S(2)}, u32[]{:S(2)}) collective-permute-start(bf16[216,128]{1,0:T(8,128)(2,1)S(1)} %fusion.99), channel_id=1, source_target_pairs={{0,96},{12,108},{24,120},{36,132},{48,144},{60,156},{72,168},{84,1... | collective-permute-start | bytes 165896 | tf_op jit(solution)/shard_map/ppermute | solution.py:24
  99.6 7.7 %collective-permute-start.7 = (bf16[216,128]{1,0:T(8,128)(2,1)S(1)}, bf16[216,128]{1,0:T(8,128)(2,1)S(1)}, u32[]{:S(2)}, u32[]{:S(2)}) collective-permute-start(bf16[216,128]{1,0:T(8,128)(2,1)S(1)} %fusion.99), channel_id=1, source_target_pairs={{0,192},{12,204},{24,216},{36,228},{48,240},{60,252},{72,264},{84,... | collective-permute-start | bytes 165896 | tf_op jit(solution)/shard_map/ppermute | solution.py:24
  103.3 7.2 %collective-permute-start.8 = (bf16[216,128]{1,0:T(8,128)(2,1)S(1)}, bf16[216,128]{1,0:T(8,128)(2,1)S(1)}, u32[]{:S(2)}, u32[]{:S(2)}) collective-permute-start(bf16[216,128]{1,0:T(8,128)(2,1)S(1)} %fusion.99), channel_id=1, source_target_pairs={{0,288},{12,300},{24,312},{36,324},{48,336},{60,348},{72,360},{84,... | collective-permute-start | bytes 165896 | tf_op jit(solution)/shard_map/ppermute | solution.py:24
  111.1 7.7 %collective-permute-start.16 = (bf16[432,512]{1,0:T(8,128)(2,1)S(1)}, bf16[432,512]{1,0:T(8,128)(2,1)S(1)}, u32[]{:S(2)}, u32[]{:S(2)}) collective-permute-start(bf16[432,512]{1,0:T(8,128)(2,1)S(1)} %fusion.27), channel_id=1, source_target_pairs={{0,12},{12,0},{24,36},{36,24},{48,60},{60,48},{72,84},{84,72},{96,... | collective-permute-start | bytes 1327112 | tf_op jit(solution)/shard_map/ppermute | solution.py:19
  120.2 22.1 %copy-start.2 = (bf16[2,96,224]{2,1,0:T(8,128)(2,1)S(1)}, bf16[2,96,224]{2,1,0:T(8,128)(2,1)}, u32[]{:S(2)}) copy-start(bf16[2,96,224]{2,1,0:T(8,128)(2,1)} %param.8) | copy-start | bytes 258052
  120.2 14.4 %all-to-all-start.1 = ((bf16[12,2,18,512]{3,1,2,0:T(2,128)(2,1)}), bf16[12,2,18,512]{3,1,2,0:T(2,128)(2,1)S(1)}, u32[]{:S(2)}, u32[]{:S(2)}) async-start(bf16[12,2,18,512]{3,1,2,0:T(2,128)(2,1)} %copy.88), calls=%async_computation.1 | async-start | bytes 884736 | tf_op jit(solution)/shard_map/all_to_all | solution.py:144
  124.4 27.2 %copy-start.3 = (f32[224]{0:T(256)S(1)}, f32[224]{0:T(256)}, u32[]{:S(2)}) copy-start(f32[224]{0:T(256)} %param.9) | copy-start | bytes 2692
  135.1 7.2 %collective-permute-start.17 = (bf16[2,96,256]{2,1,0:T(8,128)(2,1)S(1)}, bf16[2,96,256]{2,1,0:T(8,128)(2,1)S(1)}, u32[]{:S(2)}, u32[]{:S(2)}) collective-permute-start(bf16[2,96,256]{2,1,0:T(8,128)(2,1)S(1)} %slice.415), channel_id=1, source_target_pairs={{0,24},{12,36},{24,0},{36,12},{48,72},{60,84},{72,48},{84,60},{96,... | collective-permute-start | bytes 294920 | tf_op jit(solution)/shard_map/ppermute | solution.py:19
  142.3 9.3 %collective-permute-start.18 = (bf16[2,96,224]{2,1,0:T(8,128)(2,1)S(1)}, bf16[2,96,224]{2,1,0:T(8,128)(2,1)S(1)}, u32[]{:S(2)}, u32[]{:S(2)}) collective-permute-start(bf16[2,96,224]{2,1,0:T(8,128)(2,1)S(1)} %fusion.92), channel_id=1, source_target_pairs={{0,384},{12,396},{24,408},{36,420},{48,432},{60,444},{72,456},{84,... | collective-permute-start | bytes 258056 | tf_op jit(solution)/shard_map/ppermute | solution.py:29
  152.1 7.4 %collective-permute-start.19 = (bf16[2,96,256]{2,1,0:T(8,128)(2,1)S(1)}, bf16[2,96,256]{2,1,0:T(8,128)(2,1)S(1)}, u32[]{:S(2)}, u32[]{:S(2)}) collective-permute-start(bf16[2,96,256]{2,1,0:T(8,128)(2,1)S(1)} %pad_maximum_fusion.14), channel_id=1, source_target_pairs={{0,24},{12,36},{24,0},{36,12},{48,72},{60,84},{72,48},{84,60},{96,... | collective-permute-start | bytes 294920 | tf_op jit(solution)/shard_map/ppermute | solution.py:19
  179.1 9.6 %copy-start.5 = (bf16[1024,1024]{1,0:T(8,128)(2,1)S(1)}, bf16[1024,1024]{1,0:T(8,128)(2,1)}, u32[]{:S(2)}) copy-start(bf16[1024,1024]{1,0:T(8,128)(2,1)} %get-tuple-element.28) | copy-start | bytes 6291460
  179.1 8.2 %collective-permute-start.20 = (bf16[432,512]{1,0:T(8,128)(2,1)S(1)}, bf16[432,512]{1,0:T(8,128)(2,1)S(1)}, u32[]{:S(2)}, u32[]{:S(2)}) collective-permute-start(bf16[432,512]{1,0:T(8,128)(2,1)S(1)} %reshape.220), channel_id=1, source_target_pairs={{0,12},{12,0},{24,36},{36,24},{48,60},{60,48},{72,84},{84,72},{96,... | collective-permute-start | bytes 1327112 | tf_op jit(solution)/shard_map/ppermute | solution.py:19
  190.5 15.6 %collective-permute-start.28 = (bf16[224,256]{1,0:T(8,128)(2,1)S(1)}, bf16[224,256]{1,0:T(8,128)(2,1)S(1)}, u32[]{:S(2)}, u32[]{:S(2)}) collective-permute-start(bf16[224,256]{1,0:T(8,128)(2,1)S(1)} %get-tuple-element.30), channel_id=1, source_target_pairs={{0,288},{12,300},{24,312},{36,324},{48,336},{60,348},{72,360},{84,... | collective-permute-start | bytes 344072 | tf_op jit(solution)/shard_map/ppermute | solution.py:24
  194.5 15.0 %collective-permute-start.29 = (bf16[224,256]{1,0:T(8,128)(2,1)S(1)}, bf16[224,256]{1,0:T(8,128)(2,1)S(1)}, u32[]{:S(2)}, u32[]{:S(2)}) collective-permute-start(bf16[224,256]{1,0:T(8,128)(2,1)S(1)} %get-tuple-element.31), channel_id=1, source_target_pairs={{0,192},{12,204},{24,216},{36,228},{48,240},{60,252},{72,264},{84,... | collective-permute-start | bytes 344072 | tf_op jit(solution)/shard_map/ppermute | solution.py:24
  196.4 13.0 %collective-permute-start.30 = (bf16[224,256]{1,0:T(8,128)(2,1)S(1)}, bf16[224,256]{1,0:T(8,128)(2,1)S(1)}, u32[]{:S(2)}, u32[]{:S(2)}) collective-permute-start(bf16[224,256]{1,0:T(8,128)(2,1)S(1)} %get-tuple-element.32), channel_id=1, source_target_pairs={{0,96},{12,108},{24,120},{36,132},{48,144},{60,156},{72,168},{84,1... | collective-permute-start | bytes 344072 | tf_op jit(solution)/shard_map/ppermute | solution.py:24
  200.1 24.9 %collective-permute-start.21 = (bf16[224,256]{1,0:T(8,128)(2,1)S(1)}, bf16[224,256]{1,0:T(8,128)(2,1)S(1)}, u32[]{:S(2)}, u32[]{:S(2)}) collective-permute-start(bf16[224,256]{1,0:T(8,128)(2,1)S(1)} %get-tuple-element.66), channel_id=1, source_target_pairs={{0,288},{12,300},{24,312},{36,324},{48,336},{60,348},{72,360},{84,... | collective-permute-start | bytes 344072 | tf_op jit(solution)/shard_map/ppermute | solution.py:24
  204.1 20.9 %collective-permute-start.22 = (bf16[224,256]{1,0:T(8,128)(2,1)S(1)}, bf16[224,256]{1,0:T(8,128)(2,1)S(1)}, u32[]{:S(2)}, u32[]{:S(2)}) collective-permute-start(bf16[224,256]{1,0:T(8,128)(2,1)S(1)} %get-tuple-element.67), channel_id=1, source_target_pairs={{0,192},{12,204},{24,216},{36,228},{48,240},{60,252},{72,264},{84,... | collective-permute-start | bytes 344072 | tf_op jit(solution)/shard_map/ppermute | solution.py:24
  206.0 18.9 %collective-permute-start.23 = (bf16[224,256]{1,0:T(8,128)(2,1)S(1)}, bf16[224,256]{1,0:T(8,128)(2,1)S(1)}, u32[]{:S(2)}, u32[]{:S(2)}) collective-permute-start(bf16[224,256]{1,0:T(8,128)(2,1)S(1)} %get-tuple-element.68), channel_id=1, source_target_pairs={{0,96},{12,108},{24,120},{36,132},{48,144},{60,156},{72,168},{84,1... | collective-permute-start | bytes 344072 | tf_op jit(solution)/shard_map/ppermute | solution.py:24
  209.5 20.4 %collective-permute-start.31 = (bf16[224,256]{1,0:T(8,128)(2,1)S(1)}, bf16[224,256]{1,0:T(8,128)(2,1)S(1)}, u32[]{:S(2)}, u32[]{:S(2)}) collective-permute-start(bf16[224,256]{1,0:T(8,128)(2,1)S(1)} %fusion.136), channel_id=1, source_target_pairs={{0,48},{12,60},{24,72},{36,84},{48,0},{60,12},{72,24},{84,36},{96,... | collective-permute-start | bytes 344072 | tf_op jit(solution)/shard_map/ppermute | solution.py:19
  225.1 14.4 %collective-permute-start.24 = (bf16[224,256]{1,0:T(8,128)(2,1)S(1)}, bf16[224,256]{1,0:T(8,128)(2,1)S(1)}, u32[]{:S(2)}, u32[]{:S(2)}) collective-permute-start(bf16[224,256]{1,0:T(8,128)(2,1)S(1)} %fusion.137), channel_id=1, source_target_pairs={{0,48},{12,60},{24,72},{36,84},{48,0},{60,12},{72,24},{84,36},{96,... | collective-permute-start | bytes 344072 | tf_op jit(solution)/shard_map/ppermute | solution.py:19
  230.1 15.6 %collective-permute-start.32 = (bf16[216,128]{1,0:T(8,128)(2,1)S(1)}, bf16[216,128]{1,0:T(8,128)(2,1)S(1)}, u32[]{:S(2)}, u32[]{:S(2)}) collective-permute-start(bf16[216,128]{1,0:T(8,128)(2,1)S(1)} %fusion.96), channel_id=1, source_target_pairs={{0,96},{12,108},{24,120},{36,132},{48,144},{60,156},{72,168},{84,1... | collective-permute-start | bytes 165896 | tf_op jit(solution)/shard_map/ppermute | solution.py:24
  232.1 16.9 %collective-permute-start.33 = (bf16[216,128]{1,0:T(8,128)(2,1)S(1)}, bf16[216,128]{1,0:T(8,128)(2,1)S(1)}, u32[]{:S(2)}, u32[]{:S(2)}) collective-permute-start(bf16[216,128]{1,0:T(8,128)(2,1)S(1)} %fusion.96), channel_id=1, source_target_pairs={{0,192},{12,204},{24,216},{36,228},{48,240},{60,252},{72,264},{84,... | collective-permute-start | bytes 165896 | tf_op jit(solution)/shard_map/ppermute | solution.py:24
  236.1 12.9 %collective-permute-start.34 = (bf16[216,128]{1,0:T(8,128)(2,1)S(1)}, bf16[216,128]{1,0:T(8,128)(2,1)S(1)}, u32[]{:S(2)}, u32[]{:S(2)}) collective-permute-start(bf16[216,128]{1,0:T(8,128)(2,1)S(1)} %fusion.96), channel_id=1, source_target_pairs={{0,288},{12,300},{24,312},{36,324},{48,336},{60,348},{72,360},{84,... | collective-permute-start | bytes 165896 | tf_op jit(solution)/shard_map/ppermute | solution.py:24
  239.7 9.8 %collective-permute-start.25 = (bf16[216,128]{1,0:T(8,128)(2,1)S(1)}, bf16[216,128]{1,0:T(8,128)(2,1)S(1)}, u32[]{:S(2)}, u32[]{:S(2)}) collective-permute-start(bf16[216,128]{1,0:T(8,128)(2,1)S(1)} %fusion.97), channel_id=1, source_target_pairs={{0,96},{12,108},{24,120},{36,132},{48,144},{60,156},{72,168},{84,1... | collective-permute-start | bytes 165896 | tf_op jit(solution)/shard_map/ppermute | solution.py:24
  241.6 7.9 %collective-permute-start.26 = (bf16[216,128]{1,0:T(8,128)(2,1)S(1)}, bf16[216,128]{1,0:T(8,128)(2,1)S(1)}, u32[]{:S(2)}, u32[]{:S(2)}) collective-permute-start(bf16[216,128]{1,0:T(8,128)(2,1)S(1)} %fusion.97), channel_id=1, source_target_pairs={{0,192},{12,204},{24,216},{36,228},{48,240},{60,252},{72,264},{84,... | collective-permute-start | bytes 165896 | tf_op jit(solution)/shard_map/ppermute | solution.py:24
  245.7 6.7 %collective-permute-start.27 = (bf16[216,128]{1,0:T(8,128)(2,1)S(1)}, bf16[216,128]{1,0:T(8,128)(2,1)S(1)}, u32[]{:S(2)}, u32[]{:S(2)}) collective-permute-start(bf16[216,128]{1,0:T(8,128)(2,1)S(1)} %fusion.97), channel_id=1, source_target_pairs={{0,288},{12,300},{24,312},{36,324},{48,336},{60,348},{72,360},{84,... | collective-permute-start | bytes 165896 | tf_op jit(solution)/shard_map/ppermute | solution.py:24
  252.9 10.6 %collective-permute-start.35 = (bf16[432,512]{1,0:T(8,128)(2,1)S(1)}, bf16[432,512]{1,0:T(8,128)(2,1)S(1)}, u32[]{:S(2)}, u32[]{:S(2)}) collective-permute-start(bf16[432,512]{1,0:T(8,128)(2,1)S(1)} %fusion.26), channel_id=1, source_target_pairs={{0,12},{12,0},{24,36},{36,24},{48,60},{60,48},{72,84},{84,72},{96,... | collective-permute-start | bytes 1327112 | tf_op jit(solution)/shard_map/ppermute | solution.py:19
  278.7 11.9 %collective-permute-start.36 = (bf16[2,96,256]{2,1,0:T(8,128)(2,1)S(1)}, bf16[2,96,256]{2,1,0:T(8,128)(2,1)S(1)}, u32[]{:S(2)}, u32[]{:S(2)}) collective-permute-start(bf16[2,96,256]{2,1,0:T(8,128)(2,1)S(1)} %slice.414), channel_id=1, source_target_pairs={{0,24},{12,36},{24,0},{36,12},{48,72},{60,84},{72,48},{84,60},{96,... | collective-permute-start | bytes 294920 | tf_op jit(solution)/shard_map/ppermute | solution.py:19

commit v6 on v3

--- a/solution.py
+++ b/solution.py
@@ -106,18 +106,20 @@
     sums[1] = jnp.pad(sums[1], ((0, 0), (0, 2 * half - slots)))
     index = jnp.arange(SQ_TILE)[:, None]
     sums = jnp.where(index == 0, sums[0], jnp.where(index == 1, sums[1], 0.0))
-    partial = jnp.dot(inputs, w_in, preferred_element_type=jnp.float32)
+    partial = jnp.dot(inputs, w_in[:, :256], preferred_element_type=jnp.float32)
+    blocks = jnp.dot(inputs, w_in[:, 256:], preferred_element_type=jnp.float32)
+    blocks = blocks.astype(jnp.bfloat16)
     got = [
         along_y(
             jnp.concatenate(
-                [partial[:, apart * 256 : apart * 256 + 256].astype(jnp.bfloat16), sums.astype(jnp.bfloat16)]
+                [blocks[:, apart * 256 - 256 : apart * 256], sums.astype(jnp.bfloat16)]
             ),
             apart,
         )
         for apart in (3, 2, 1)
     ]
     got = sum(part.astype(jnp.float32) for part in got)
-    partial = partial[:, :256] + got[:slots]
+    partial = partial + got[:slots]
     sums = sums + got[slots:]
     message = jnp.concatenate([partial, sums], axis=0).astype(jnp.bfloat16)
     got = exchange(message, 2).astype(jnp.float32)

time: 290 us -> 291 us (level)
  starting transfers between devices: 120 us -> 114 us
  blocking collectives: 49.6 us -> 53 us
  waiting for transfers between devices: 92.9 us -> 96 us
    ppermute x12, waiting for transfers between devices: 33.3 us -> 37.5 us  [along_y(): return lax.ppermute(x, 'pipe', [(i, i ^ apart << 3) for i in range(size)])]
    all_to_all x2, blocking collectives: 35.5 us -> 38.9 us  [layer(): lax.all_to_all(buffer.transpose(1, 0, 2, 3), 'expert', split_axis=0, conc...]
  transfers between devices with their start and end apart: 24 -> 24, of which waited for: 18 -> 19; matrix products, arithmetic and copies ran while one was open for 3% -> 2% of each run, Pallas kernels for 2% -> 2%
where the time goes in v6:
time: 291 us; the launch traced here: 290 us
  starting transfers between devices  114 us (39%)
  waiting for transfers between devices  96 us (33%)
  blocking collectives  53 us (18%)
  other arithmetic  7.04 us (2%)
  local copies, waits for them, and re-layouts  7.01 us (2%)
  matrix products  6.32 us (2%)
  Pallas kernels  5.22 us (2%)
    ppermute x10, starting transfers between devices, exchange(): return lax.ppermute(x, 'pipe', [(i, i ^ 1 << bit) for i in range(size)])  63.1 us
    ppermute x10, waiting for transfers between devices, exchange(): return lax.ppermute(x, 'pipe', [(i, i ^ 1 << bit) for i in range(size)])  46.3 us
    ppermute x12, starting transfers between devices, along_y(): return lax.ppermute(x, 'pipe', [(i, i ^ apart << 3) for i in range(size)])  42 us
    all_to_all x2, blocking collectives, layer(): lax.all_to_all(buffer.transpose(1, 0, 2, 3), 'expert', split_axis=0, conc...  38.9 us
    ppermute x12, waiting for transfers between devices, along_y(): return lax.ppermute(x, 'pipe', [(i, i ^ apart << 3) for i in range(size)])  37.5 us
    all_to_all x1, blocking collectives, layer(): lax.all_to_all(expert_out, 'expert', split_axis=0, concat_axis=0, tiled=T...  14.1 us
    all_to_all x1, waiting for transfers between devices, layer(): lax.all_to_all(expert_out, 'expert', split_axis=0, concat_axis=0, tiled=T...  8.69 us
  transfers between devices with their start and end apart: 24, of which 19 were waited for; matrix products, arithmetic and copies ran while one was open for 2% of the time, Pallas kernels for 2%

profile of v6, /device:TPU:1, one launch (start us, length us, event | category | flops | bytes accessed | tf_op | source)
XLA Modules:
  0.0 289.8 jit_solution(12721009163327139436)
XLA Ops:
  0.0 1.0 fusion.46
  1.5 8.4 %collective-permute-start = (bf16[2,96,256]{2,1,0:T(8,128)(2,1)S(1)}, bf16[2,96,256]{2,1,0:T(8,128)(2,1)S(1)}, u32[]{:S(2)}, u32[]{:S(2)}) collective-permute-start(bf16[2,96,256]{2,1,0:T(8,128)(2,1)S(1)} %pad_maximum_fusion.9), channel_id=1, source_target_pairs={{0,24},{12,36},{24,0},{36,12},{48,72},{60,84},{72,48},{84,60},{96,... | collective-permute-start | bytes 294920 | tf_op jit(solution)/shard_map/ppermute | solution.py:19
  9.9 0.7 constant_dynamic-slice_fusion.1
  10.6 0.7 constant_dynamic-slice_fusion.3
  11.7 1.2 reduce-window.14
  13.5 0.7 pad_add_fusion.where
  14.2 5.2 %shard_map.82 = (bf16[1024,1024]{1,0:T(8,128)(2,1)}, bf16[1024,512]{1,0:T(8,128)(2,1)}) custom-call(s32[2]{0:T(128)} %pad_add_fusion.where, bf16[896,1024]{1,0:T(8,128)(2,1)} %bitcast.70, bf16[896,512]{1,0:T(8,128)(2,1)} %bitcast.73, bf16[896,512]{1,0:T(8,128)(2,1)} %bitcast.74, f32[1]{0:T(128)} %bitcast.9.rate), custom_call_target="tpu_custom_call" | custom-call | flops 2000000 | bytes 8000000 | tf_op jit(solution)/shard_map/pallas_call | solution.py:55
  20.1 0.3 copy.86
  20.4 19.2 %all_to_all.20 = bf16[12,2,18,512]{3,1,2,0:T(2,128)(2,1)S(1)} all-to-all(bf16[12,2,18,512]{3,1,2,0:T(2,128)(2,1)S(1)} %bitcast.71), channel_id=1, replica_groups=mesh['pipe'=64,'expert'=12] {'expert'}, dimensions={0} | all-to-all | bytes 884736 | tf_op jit(solution)/shard_map/all_to_all | solution.py:92
  39.9 4.4 %collective-permute-start.1 = (bf16[432,512]{1,0:T(8,128)(2,1)S(1)}, bf16[432,512]{1,0:T(8,128)(2,1)S(1)}, u32[]{:S(2)}, u32[]{:S(2)}) collective-permute-start(bf16[432,512]{1,0:T(8,128)(2,1)S(1)} %reshape.214), channel_id=1, source_target_pairs={{0,12},{12,0},{24,36},{36,24},{48,60},{60,48},{72,84},{84,72},{96,... | collective-permute-start | bytes 1327112 | tf_op jit(solution)/shard_map/ppermute | solution.py:19
  44.3 1.3 collective-permute-done.1
  45.7 0.9 fusion.4
  47.2 5.2 %collective-permute-start.2 = (bf16[448,256]{1,0:T(8,128)(2,1)S(1)}, bf16[448,256]{1,0:T(8,128)(2,1)S(1)}, u32[]{:S(2)}, u32[]{:S(2)}) collective-permute-start(bf16[448,256]{1,0:T(8,128)(2,1)S(1)} %get-tuple-element.48), channel_id=1, source_target_pairs={{0,288},{12,300},{24,312},{36,324},{48,336},{60,348},{72,360},{84,... | collective-permute-start | bytes 688136 | tf_op jit(solution)/shard_map/ppermute | solution.py:24
  52.4 1.9 collective-permute-start.3
  54.3 2.2 collective-permute-start.4
  56.5 1.3 collective-permute-done.2
  57.8 13.8 %collective-permute-done.3 = bf16[448,256]{1,0:T(8,128)(2,1)S(1)} collective-permute-done((bf16[448,256]{1,0:T(8,128)(2,1)S(1)}, bf16[448,256]{1,0:T(8,128)(2,1)S(1)}, u32[]{:S(2)}, u32[]{:S(2)}) %collective-permute-start.3) | collective-permute-done | bytes 229408 | tf_op jit(solution)/shard_map/ppermute | solution.py:24
  71.7 0.4 fusion.87
  72.2 11.1 %collective-permute-start.5 = (bf16[448,256]{1,0:T(8,128)(2,1)S(1)}, bf16[448,256]{1,0:T(8,128)(2,1)S(1)}, u32[]{:S(2)}, u32[]{:S(2)}) collective-permute-start(bf16[448,256]{1,0:T(8,128)(2,1)S(1)} %pad_maximum_fusion.6), channel_id=1, source_target_pairs={{0,48},{12,60},{24,72},{36,84},{48,0},{60,12},{72,24},{84,36},{96,... | collective-permute-start | bytes 688136 | tf_op jit(solution)/shard_map/ppermute | solution.py:19
  83.3 10.6 %collective-permute-done.5 = bf16[448,256]{1,0:T(8,128)(2,1)S(1)} collective-permute-done((bf16[448,256]{1,0:T(8,128)(2,1)S(1)}, bf16[448,256]{1,0:T(8,128)(2,1)S(1)}, u32[]{:S(2)}, u32[]{:S(2)}) %collective-permute-start.5) | collective-permute-done | bytes 229408 | tf_op jit(solution)/shard_map/ppermute | solution.py:19
  94.2 1.9 collective-permute-start.6
  96.2 4.4 %collective-permute-start.7 = (bf16[432,128]{1,0:T(8,128)(2,1)S(1)}, bf16[432,128]{1,0:T(8,128)(2,1)S(1)}, u32[]{:S(2)}, u32[]{:S(2)}) collective-permute-start(bf16[432,128]{1,0:T(8,128)(2,1)S(1)} %fusion.45), channel_id=1, source_target_pairs={{0,192},{12,204},{24,216},{36,228},{48,240},{60,252},{72,264},{84,... | collective-permute-start | bytes 331784 | tf_op jit(solution)/shard_map/ppermute | solution.py:24
  100.6 3.0 %collective-permute-start.8 = (bf16[432,128]{1,0:T(8,128)(2,1)S(1)}, bf16[432,128]{1,0:T(8,128)(2,1)S(1)}, u32[]{:S(2)}, u32[]{:S(2)}) collective-permute-start(bf16[432,128]{1,0:T(8,128)(2,1)S(1)} %fusion.45), channel_id=1, source_target_pairs={{0,288},{12,300},{24,312},{36,324},{48,336},{60,348},{72,360},{84,... | collective-permute-start | bytes 331784 | tf_op jit(solution)/shard_map/ppermute | solution.py:24
  103.5 0.3 collective-permute-done.7
  103.9 4.0 %collective-permute-done.8 = bf16[432,128]{1,0:T(8,128)(2,1)S(1)} collective-permute-done((bf16[432,128]{1,0:T(8,128)(2,1)S(1)}, bf16[432,128]{1,0:T(8,128)(2,1)S(1)}, u32[]{:S(2)}, u32[]{:S(2)}) %collective-permute-start.8) | collective-permute-done | bytes 110624 | tf_op jit(solution)/shard_map/ppermute | solution.py:24
  107.9 0.7 fusion.18
  108.6 9.4 %collective-permute-start.9 = (bf16[432,512]{1,0:T(8,128)(2,1)S(1)}, bf16[432,512]{1,0:T(8,128)(2,1)S(1)}, u32[]{:S(2)}, u32[]{:S(2)}) collective-permute-start(bf16[432,512]{1,0:T(8,128)(2,1)S(1)} %slice.329), channel_id=1, source_target_pairs={{0,12},{12,0},{24,36},{36,24},{48,60},{60,48},{72,84},{84,72},{96,... | collective-permute-start | bytes 1327112 | tf_op jit(solution)/shard_map/ppermute | solution.py:19
  118.0 1.4 collective-permute-done.9
  119.7 1.1 copy.88
  120.8 3.6 %all-to-all-start.1 = ((bf16[12,2,18,512]{3,1,2,0:T(2,128)(2,1)}), bf16[12,2,18,512]{3,1,2,0:T(2,128)(2,1)S(1)}, u32[]{:S(2)}, u32[]{:S(2)}) async-start(bf16[12,2,18,512]{3,1,2,0:T(2,128)(2,1)} %copy.88), calls=%async_computation.1 | async-start | bytes 884736 | tf_op jit(solution)/shard_map/all_to_all | solution.py:137
  124.7 1.2 reduce-window.16
  126.3 8.7 %all-to-all-done.1 = bf16[12,2,18,512]{3,1,2,0:T(2,128)(2,1)S(1)} async-done(((bf16[12,2,18,512]{3,1,2,0:T(2,128)(2,1)}), bf16[12,2,18,512]{3,1,2,0:T(2,128)(2,1)S(1)}, u32[]{:S(2)}, u32[]{:S(2)}) %all-to-all-start.1) | async-done | bytes 442400 | tf_op jit(solution)/shard_map/all_to_all | solution.py:137
  135.5 1.9 collective-permute-start.10
  137.6 5.1 %collective-permute-done.10 = bf16[2,96,256]{2,1,0:T(8,128)(2,1)S(1)} collective-permute-done((bf16[2,96,256]{2,1,0:T(8,128)(2,1)S(1)}, bf16[2,96,256]{2,1,0:T(8,128)(2,1)S(1)}, u32[]{:S(2)}, u32[]{:S(2)}) %collective-permute-start.10) | collective-permute-done | bytes 98336 | tf_op jit(solution)/shard_map/ppermute | solution.py:19
  142.7 5.6 %collective-permute-start.11 = (bf16[2,96,224]{2,1,0:T(8,128)(2,1)S(1)}, bf16[2,96,224]{2,1,0:T(8,128)(2,1)S(1)}, u32[]{:S(2)}, u32[]{:S(2)}) collective-permute-start(bf16[2,96,224]{2,1,0:T(8,128)(2,1)S(1)} %fusion.48), channel_id=1, source_target_pairs={{0,384},{12,396},{24,408},{36,420},{48,432},{60,444},{72,456},{84,... | collective-permute-start | bytes 258056 | tf_op jit(solution)/shard_map/ppermute | solution.py:29
  148.4 3.5 %collective-permute-done.11 = bf16[2,96,224]{2,1,0:T(8,128)(2,1)S(1)} collective-permute-done((bf16[2,96,224]{2,1,0:T(8,128)(2,1)S(1)}, bf16[2,96,224]{2,1,0:T(8,128)(2,1)S(1)}, u32[]{:S(2)}, u32[]{:S(2)}) %collective-permute-start.11) | collective-permute-done | bytes 86048 | tf_op jit(solution)/shard_map/ppermute | solution.py:29
  152.5 2.1 collective-permute-start.12
  154.8 4.9 %collective-permute-done.12 = bf16[2,96,256]{2,1,0:T(8,128)(2,1)S(1)} collective-permute-done((bf16[2,96,256]{2,1,0:T(8,128)(2,1)S(1)}, bf16[2,96,256]{2,1,0:T(8,128)(2,1)S(1)}, u32[]{:S(2)}, u32[]{:S(2)}) %collective-permute-start.12) | collective-permute-done | bytes 98336 | tf_op jit(solution)/shard_map/ppermute | solution.py:19
  160.1 0.3 copy.98
  160.5 19.7 %all_to_all.21 = bf16[12,2,18,512]{3,1,2,0:T(2,128)(2,1)S(1)} all-to-all(bf16[12,2,18,512]{3,1,2,0:T(2,128)(2,1)S(1)} %bitcast.72), channel_id=1, replica_groups=mesh['pipe'=64,'expert'=12] {'expert'}, dimensions={0} | all-to-all | bytes 884736 | tf_op jit(solution)/shard_map/all_to_all | solution.py:92
  180.4 6.1 %collective-permute-start.13 = (bf16[432,512]{1,0:T(8,128)(2,1)S(1)}, bf16[432,512]{1,0:T(8,128)(2,1)S(1)}, u32[]{:S(2)}, u32[]{:S(2)}) collective-permute-start(bf16[432,512]{1,0:T(8,128)(2,1)S(1)} %reshape.220), channel_id=1, source_target_pairs={{0,12},{12,0},{24,36},{36,24},{48,60},{60,48},{72,84},{84,72},{96,... | collective-permute-start | bytes 1327112 | tf_op jit(solution)/shard_map/ppermute | solution.py:19
  186.5 1.3 collective-permute-done.13
  188.1 0.9 fusion.7
  189.3 2.6 collective-permute-start.14
  192.0 1.9 collective-permute-start.15
  193.9 4.9 %collective-permute-start.16 = (bf16[448,256]{1,0:T(8,128)(2,1)S(1)}, bf16[448,256]{1,0:T(8,128)(2,1)S(1)}, u32[]{:S(2)}, u32[]{:S(2)}) collective-permute-start(bf16[448,256]{1,0:T(8,128)(2,1)S(1)} %get-tuple-element.43), channel_id=1, source_target_pairs={{0,96},{12,108},{24,120},{36,132},{48,144},{60,156},{72,168},{84,1... | collective-permute-start | bytes 688136 | tf_op jit(solution)/shard_map/ppermute | solution.py:24
  198.8 1.0 collective-permute-done.14
  199.9 11.6 %collective-permute-done.15 = bf16[448,256]{1,0:T(8,128)(2,1)S(1)} collective-permute-done((bf16[448,256]{1,0:T(8,128)(2,1)S(1)}, bf16[448,256]{1,0:T(8,128)(2,1)S(1)}, u32[]{:S(2)}, u32[]{:S(2)}) %collective-permute-start.15) | collective-permute-done | bytes 229408 | tf_op jit(solution)/shard_map/ppermute | solution.py:24
  211.6 0.4 fusion.89
  212.0 13.1 %collective-permute-start.17 = (bf16[448,256]{1,0:T(8,128)(2,1)S(1)}, bf16[448,256]{1,0:T(8,128)(2,1)S(1)}, u32[]{:S(2)}, u32[]{:S(2)}) collective-permute-start(bf16[448,256]{1,0:T(8,128)(2,1)S(1)} %pad_maximum_fusion.7), channel_id=1, source_target_pairs={{0,48},{12,60},{24,72},{36,84},{48,0},{60,12},{72,24},{84,36},{96,... | collective-permute-start | bytes 688136 | tf_op jit(solution)/shard_map/ppermute | solution.py:19
  225.2 10.4 %collective-permute-done.17 = bf16[448,256]{1,0:T(8,128)(2,1)S(1)} collective-permute-done((bf16[448,256]{1,0:T(8,128)(2,1)S(1)}, bf16[448,256]{1,0:T(8,128)(2,1)S(1)}, u32[]{:S(2)}, u32[]{:S(2)}) %collective-permute-start.17) | collective-permute-done | bytes 229408 | tf_op jit(solution)/shard_map/ppermute | solution.py:19
  235.8 7.0 %collective-permute-start.18 = (bf16[432,128]{1,0:T(8,128)(2,1)S(1)}, bf16[432,128]{1,0:T(8,128)(2,1)S(1)}, u32[]{:S(2)}, u32[]{:S(2)}) collective-permute-start(bf16[432,128]{1,0:T(8,128)(2,1)S(1)} %fusion.44), channel_id=1, source_target_pairs={{0,96},{12,108},{24,120},{36,132},{48,144},{60,156},{72,168},{84,1... | collective-permute-start | bytes 331784 | tf_op jit(solution)/shard_map/ppermute | solution.py:24
  242.8 5.0 %collective-permute-start.19 = (bf16[432,128]{1,0:T(8,128)(2,1)S(1)}, bf16[432,128]{1,0:T(8,128)(2,1)S(1)}, u32[]{:S(2)}, u32[]{:S(2)}) collective-permute-start(bf16[432,128]{1,0:T(8,128)(2,1)S(1)} %fusion.44), channel_id=1, source_target_pairs={{0,192},{12,204},{24,216},{36,228},{48,240},{60,252},{72,264},{84,... | collective-permute-start | bytes 331784 | tf_op jit(solution)/shard_map/ppermute | solution.py:24
  247.8 1.9 collective-permute-start.20
  249.8 3.4 %collective-permute-done.19 = bf16[432,128]{1,0:T(8,128)(2,1)S(1)} collective-permute-done((bf16[432,128]{1,0:T(8,128)(2,1)S(1)}, bf16[432,128]{1,0:T(8,128)(2,1)S(1)}, u32[]{:S(2)}, u32[]{:S(2)}) %collective-permute-start.19) | collective-permute-done | bytes 110624 | tf_op jit(solution)/shard_map/ppermute | solution.py:24
  253.2 2.0 collective-permute-done.20
  255.2 0.7 fusion.26
  256.0 4.7 %collective-permute-start.21 = (bf16[432,512]{1,0:T(8,128)(2,1)S(1)}, bf16[432,512]{1,0:T(8,128)(2,1)S(1)}, u32[]{:S(2)}, u32[]{:S(2)}) collective-permute-start(bf16[432,512]{1,0:T(8,128)(2,1)S(1)} %slice.328), channel_id=1, source_target_pairs={{0,12},{12,0},{24,36},{36,24},{48,60},{60,48},{72,84},{84,72},{96,... | collective-permute-start | bytes 1327112 | tf_op jit(solution)/shard_map/ppermute | solution.py:19
  260.7 1.4 collective-permute-done.21
  262.4 0.3 copy.100
  262.7 14.1 %all_to_all.22 = bf16[12,2,18,512]{3,1,2,0:T(2,128)(2,1)S(1)} all-to-all(bf16[12,2,18,512]{3,1,2,0:T(2,128)(2,1)S(1)} %copy.100), channel_id=1, replica_groups=mesh['pipe'=64,'expert'=12] {'expert'}, dimensions={0} | all-to-all | bytes 884736 | tf_op jit(solution)/shard_map/all_to_all | solution.py:137
  277.3 1.9 collective-permute-start.22
  279.2 9.9 %collective-permute-done.22 = bf16[2,96,256]{2,1,0:T(8,128)(2,1)S(1)} collective-permute-done((bf16[2,96,256]{2,1,0:T(8,128)(2,1)S(1)}, bf16[2,96,256]{2,1,0:T(8,128)(2,1)S(1)}, u32[]{:S(2)}, u32[]{:S(2)}) %collective-permute-start.22) | collective-permute-done | bytes 98336 | tf_op jit(solution)/shard_map/ppermute | solution.py:19
  289.1 0.7 fusion.51
  (122 shorter events, 8.3 us)
Async XLA Ops:
  0.0 9.9 %copy-start = (f32[1,2]{1,0:T(1,128)S(1)}, f32[1,2]{1,0:T(1,128)}, u32[]{:S(2)}) copy-start(f32[1,2]{1,0:T(1,128)} %param.13) | copy-start | bytes 28
  0.0 13.5 %copy-start.4 = (f32[2,2,2,96,2]{3,4,2,1,0:T(2,128)S(1)}, f32[2,2,2,96,2]{3,4,2,1,0:T(2,128)}, u32[]{:S(2)}) copy-start(f32[2,2,2,96,2]{3,4,2,1,0:T(2,128)} %param.15) | copy-start | bytes 18436
  1.5 18.1 %collective-permute-start = (bf16[2,96,256]{2,1,0:T(8,128)(2,1)S(1)}, bf16[2,96,256]{2,1,0:T(8,128)(2,1)S(1)}, u32[]{:S(2)}, u32[]{:S(2)}) collective-permute-start(bf16[2,96,256]{2,1,0:T(8,128)(2,1)S(1)} %pad_maximum_fusion.9), channel_id=1, source_target_pairs={{0,24},{12,36},{24,0},{36,12},{48,72},{60,84},{72,48},{84,60},{96,... | collective-permute-start | bytes 294920 | tf_op jit(solution)/shard_map/ppermute | solution.py:19
  39.6 6.0 %copy-start.1 = (bf16[1024,1024]{1,0:T(8,128)(2,1)S(1)}, bf16[1024,1024]{1,0:T(8,128)(2,1)}, u32[]{:S(2)}) copy-start(bf16[1024,1024]{1,0:T(8,128)(2,1)} %get-tuple-element.19) | copy-start | bytes 6291460
  39.9 5.8 %collective-permute-start.1 = (bf16[432,512]{1,0:T(8,128)(2,1)S(1)}, bf16[432,512]{1,0:T(8,128)(2,1)S(1)}, u32[]{:S(2)}, u32[]{:S(2)}) collective-permute-start(bf16[432,512]{1,0:T(8,128)(2,1)S(1)} %reshape.214), channel_id=1, source_target_pairs={{0,12},{12,0},{24,36},{36,24},{48,60},{60,48},{72,84},{84,72},{96,... | collective-permute-start | bytes 1327112 | tf_op jit(solution)/shard_map/ppermute | solution.py:19
  47.2 10.6 %collective-permute-start.2 = (bf16[448,256]{1,0:T(8,128)(2,1)S(1)}, bf16[448,256]{1,0:T(8,128)(2,1)S(1)}, u32[]{:S(2)}, u32[]{:S(2)}) collective-permute-start(bf16[448,256]{1,0:T(8,128)(2,1)S(1)} %get-tuple-element.48), channel_id=1, source_target_pairs={{0,288},{12,300},{24,312},{36,324},{48,336},{60,348},{72,360},{84,... | collective-permute-start | bytes 688136 | tf_op jit(solution)/shard_map/ppermute | solution.py:24
  52.4 19.2 %collective-permute-start.3 = (bf16[448,256]{1,0:T(8,128)(2,1)S(1)}, bf16[448,256]{1,0:T(8,128)(2,1)S(1)}, u32[]{:S(2)}, u32[]{:S(2)}) collective-permute-start(bf16[448,256]{1,0:T(8,128)(2,1)S(1)} %get-tuple-element.49), channel_id=1, source_target_pairs={{0,192},{12,204},{24,216},{36,228},{48,240},{60,252},{72,264},{84,... | collective-permute-start | bytes 688136 | tf_op jit(solution)/shard_map/ppermute | solution.py:24
  54.3 17.3 %collective-permute-start.4 = (bf16[448,256]{1,0:T(8,128)(2,1)S(1)}, bf16[448,256]{1,0:T(8,128)(2,1)S(1)}, u32[]{:S(2)}, u32[]{:S(2)}) collective-permute-start(bf16[448,256]{1,0:T(8,128)(2,1)S(1)} %get-tuple-element.50), channel_id=1, source_target_pairs={{0,96},{12,108},{24,120},{36,132},{48,144},{60,156},{72,168},{84,1... | collective-permute-start | bytes 688136 | tf_op jit(solution)/shard_map/ppermute | solution.py:24
  72.1 35.7 %copy-start.6 = (bf16[1024,512]{1,0:T(8,128)(2,1)S(1)}, bf16[1024,512]{1,0:T(8,128)(2,1)}, u32[]{:S(2)}) copy-start(bf16[1024,512]{1,0:T(8,128)(2,1)} %get-tuple-element.20) | copy-start | bytes 3145732
  72.2 21.8 %collective-permute-start.5 = (bf16[448,256]{1,0:T(8,128)(2,1)S(1)}, bf16[448,256]{1,0:T(8,128)(2,1)S(1)}, u32[]{:S(2)}, u32[]{:S(2)}) collective-permute-start(bf16[448,256]{1,0:T(8,128)(2,1)S(1)} %pad_maximum_fusion.6), channel_id=1, source_target_pairs={{0,48},{12,60},{24,72},{36,84},{48,0},{60,12},{72,24},{84,36},{96,... | collective-permute-start | bytes 688136 | tf_op jit(solution)/shard_map/ppermute | solution.py:19
  94.2 9.3 %collective-permute-start.6 = (bf16[432,128]{1,0:T(8,128)(2,1)S(1)}, bf16[432,128]{1,0:T(8,128)(2,1)S(1)}, u32[]{:S(2)}, u32[]{:S(2)}) collective-permute-start(bf16[432,128]{1,0:T(8,128)(2,1)S(1)} %fusion.45), channel_id=1, source_target_pairs={{0,96},{12,108},{24,120},{36,132},{48,144},{60,156},{72,168},{84,1... | collective-permute-start | bytes 331784 | tf_op jit(solution)/shard_map/ppermute | solution.py:24
  96.2 7.7 %collective-permute-start.7 = (bf16[432,128]{1,0:T(8,128)(2,1)S(1)}, bf16[432,128]{1,0:T(8,128)(2,1)S(1)}, u32[]{:S(2)}, u32[]{:S(2)}) collective-permute-start(bf16[432,128]{1,0:T(8,128)(2,1)S(1)} %fusion.45), channel_id=1, source_target_pairs={{0,192},{12,204},{24,216},{36,228},{48,240},{60,252},{72,264},{84,... | collective-permute-start | bytes 331784 | tf_op jit(solution)/shard_map/ppermute | solution.py:24
  100.6 7.3 %collective-permute-start.8 = (bf16[432,128]{1,0:T(8,128)(2,1)S(1)}, bf16[432,128]{1,0:T(8,128)(2,1)S(1)}, u32[]{:S(2)}, u32[]{:S(2)}) collective-permute-start(bf16[432,128]{1,0:T(8,128)(2,1)S(1)} %fusion.45), channel_id=1, source_target_pairs={{0,288},{12,300},{24,312},{36,324},{48,336},{60,348},{72,360},{84,... | collective-permute-start | bytes 331784 | tf_op jit(solution)/shard_map/ppermute | solution.py:24
  108.6 10.8 %collective-permute-start.9 = (bf16[432,512]{1,0:T(8,128)(2,1)S(1)}, bf16[432,512]{1,0:T(8,128)(2,1)S(1)}, u32[]{:S(2)}, u32[]{:S(2)}) collective-permute-start(bf16[432,512]{1,0:T(8,128)(2,1)S(1)} %slice.329), channel_id=1, source_target_pairs={{0,12},{12,0},{24,36},{36,24},{48,60},{60,48},{72,84},{84,72},{96,... | collective-permute-start | bytes 1327112 | tf_op jit(solution)/shard_map/ppermute | solution.py:19
  120.8 14.2 %all-to-all-start.1 = ((bf16[12,2,18,512]{3,1,2,0:T(2,128)(2,1)}), bf16[12,2,18,512]{3,1,2,0:T(2,128)(2,1)S(1)}, u32[]{:S(2)}, u32[]{:S(2)}) async-start(bf16[12,2,18,512]{3,1,2,0:T(2,128)(2,1)} %copy.88), calls=%async_computation.1 | async-start | bytes 884736 | tf_op jit(solution)/shard_map/all_to_all | solution.py:137
  124.4 18.3 %copy-start.3 = (bf16[2,96,224]{2,1,0:T(8,128)(2,1)S(1)}, bf16[2,96,224]{2,1,0:T(8,128)(2,1)}, u32[]{:S(2)}) copy-start(bf16[2,96,224]{2,1,0:T(8,128)(2,1)} %param.8) | copy-start | bytes 258052
  135.0 17.0 %copy-start.5 = (f32[224]{0:T(256)S(1)}, f32[224]{0:T(256)}, u32[]{:S(2)}) copy-start(f32[224]{0:T(256)} %param.9) | copy-start | bytes 2692
  135.5 7.2 %collective-permute-start.10 = (bf16[2,96,256]{2,1,0:T(8,128)(2,1)S(1)}, bf16[2,96,256]{2,1,0:T(8,128)(2,1)S(1)}, u32[]{:S(2)}, u32[]{:S(2)}) collective-permute-start(bf16[2,96,256]{2,1,0:T(8,128)(2,1)S(1)} %slice.331), channel_id=1, source_target_pairs={{0,24},{12,36},{24,0},{36,12},{48,72},{60,84},{72,48},{84,60},{96,... | collective-permute-start | bytes 294920 | tf_op jit(solution)/shard_map/ppermute | solution.py:19
  142.7 9.3 %collective-permute-start.11 = (bf16[2,96,224]{2,1,0:T(8,128)(2,1)S(1)}, bf16[2,96,224]{2,1,0:T(8,128)(2,1)S(1)}, u32[]{:S(2)}, u32[]{:S(2)}) collective-permute-start(bf16[2,96,224]{2,1,0:T(8,128)(2,1)S(1)} %fusion.48), channel_id=1, source_target_pairs={{0,384},{12,396},{24,408},{36,420},{48,432},{60,444},{72,456},{84,... | collective-permute-start | bytes 258056 | tf_op jit(solution)/shard_map/ppermute | solution.py:29
  152.5 7.2 %collective-permute-start.12 = (bf16[2,96,256]{2,1,0:T(8,128)(2,1)S(1)}, bf16[2,96,256]{2,1,0:T(8,128)(2,1)S(1)}, u32[]{:S(2)}, u32[]{:S(2)}) collective-permute-start(bf16[2,96,256]{2,1,0:T(8,128)(2,1)S(1)} %pad_maximum_fusion.8), channel_id=1, source_target_pairs={{0,24},{12,36},{24,0},{36,12},{48,72},{60,84},{72,48},{84,60},{96,... | collective-permute-start | bytes 294920 | tf_op jit(solution)/shard_map/ppermute | solution.py:19
  180.2 7.9 %copy-start.2 = (bf16[1024,1024]{1,0:T(8,128)(2,1)S(1)}, bf16[1024,1024]{1,0:T(8,128)(2,1)}, u32[]{:S(2)}) copy-start(bf16[1024,1024]{1,0:T(8,128)(2,1)} %get-tuple-element.19) | copy-start | bytes 6291460
  180.4 7.5 %collective-permute-start.13 = (bf16[432,512]{1,0:T(8,128)(2,1)S(1)}, bf16[432,512]{1,0:T(8,128)(2,1)S(1)}, u32[]{:S(2)}, u32[]{:S(2)}) collective-permute-start(bf16[432,512]{1,0:T(8,128)(2,1)S(1)} %reshape.220), channel_id=1, source_target_pairs={{0,12},{12,0},{24,36},{36,24},{48,60},{60,48},{72,84},{84,72},{96,... | collective-permute-start | bytes 1327112 | tf_op jit(solution)/shard_map/ppermute | solution.py:19
  189.3 10.5 %collective-permute-start.14 = (bf16[448,256]{1,0:T(8,128)(2,1)S(1)}, bf16[448,256]{1,0:T(8,128)(2,1)S(1)}, u32[]{:S(2)}, u32[]{:S(2)}) collective-permute-start(bf16[448,256]{1,0:T(8,128)(2,1)S(1)} %get-tuple-element.41), channel_id=1, source_target_pairs={{0,288},{12,300},{24,312},{36,324},{48,336},{60,348},{72,360},{84,... | collective-permute-start | bytes 688136 | tf_op jit(solution)/shard_map/ppermute | solution.py:24
  192.0 19.5 %collective-permute-start.15 = (bf16[448,256]{1,0:T(8,128)(2,1)S(1)}, bf16[448,256]{1,0:T(8,128)(2,1)S(1)}, u32[]{:S(2)}, u32[]{:S(2)}) collective-permute-start(bf16[448,256]{1,0:T(8,128)(2,1)S(1)} %get-tuple-element.42), channel_id=1, source_target_pairs={{0,192},{12,204},{24,216},{36,228},{48,240},{60,252},{72,264},{84,... | collective-permute-start | bytes 688136 | tf_op jit(solution)/shard_map/ppermute | solution.py:24
  193.9 17.5 %collective-permute-start.16 = (bf16[448,256]{1,0:T(8,128)(2,1)S(1)}, bf16[448,256]{1,0:T(8,128)(2,1)S(1)}, u32[]{:S(2)}, u32[]{:S(2)}) collective-permute-start(bf16[448,256]{1,0:T(8,128)(2,1)S(1)} %get-tuple-element.43), channel_id=1, source_target_pairs={{0,96},{12,108},{24,120},{36,132},{48,144},{60,156},{72,168},{84,1... | collective-permute-start | bytes 688136 | tf_op jit(solution)/shard_map/ppermute | solution.py:24
  212.0 43.2 %copy-start.7 = (bf16[1024,512]{1,0:T(8,128)(2,1)S(1)}, bf16[1024,512]{1,0:T(8,128)(2,1)}, u32[]{:S(2)}) copy-start(bf16[1024,512]{1,0:T(8,128)(2,1)} %get-tuple-element.20) | copy-start | bytes 3145732
  212.0 23.5 %collective-permute-start.17 = (bf16[448,256]{1,0:T(8,128)(2,1)S(1)}, bf16[448,256]{1,0:T(8,128)(2,1)S(1)}, u32[]{:S(2)}, u32[]{:S(2)}) collective-permute-start(bf16[448,256]{1,0:T(8,128)(2,1)S(1)} %pad_maximum_fusion.7), channel_id=1, source_target_pairs={{0,48},{12,60},{24,72},{36,84},{48,0},{60,12},{72,24},{84,36},{96,... | collective-permute-start | bytes 688136 | tf_op jit(solution)/shard_map/ppermute | solution.py:19
  235.8 13.9 %collective-permute-start.18 = (bf16[432,128]{1,0:T(8,128)(2,1)S(1)}, bf16[432,128]{1,0:T(8,128)(2,1)S(1)}, u32[]{:S(2)}, u32[]{:S(2)}) collective-permute-start(bf16[432,128]{1,0:T(8,128)(2,1)S(1)} %fusion.44), channel_id=1, source_target_pairs={{0,96},{12,108},{24,120},{36,132},{48,144},{60,156},{72,168},{84,1... | collective-permute-start | bytes 331784 | tf_op jit(solution)/shard_map/ppermute | solution.py:24
  242.8 10.4 %collective-permute-start.19 = (bf16[432,128]{1,0:T(8,128)(2,1)S(1)}, bf16[432,128]{1,0:T(8,128)(2,1)S(1)}, u32[]{:S(2)}, u32[]{:S(2)}) collective-permute-start(bf16[432,128]{1,0:T(8,128)(2,1)S(1)} %fusion.44), channel_id=1, source_target_pairs={{0,192},{12,204},{24,216},{36,228},{48,240},{60,252},{72,264},{84,... | collective-permute-start | bytes 331784 | tf_op jit(solution)/shard_map/ppermute | solution.py:24
  247.8 7.4 %collective-permute-start.20 = (bf16[432,128]{1,0:T(8,128)(2,1)S(1)}, bf16[432,128]{1,0:T(8,128)(2,1)S(1)}, u32[]{:S(2)}, u32[]{:S(2)}) collective-permute-start(bf16[432,128]{1,0:T(8,128)(2,1)S(1)} %fusion.44), channel_id=1, source_target_pairs={{0,288},{12,300},{24,312},{36,324},{48,336},{60,348},{72,360},{84,... | collective-permute-start | bytes 331784 | tf_op jit(solution)/shard_map/ppermute | solution.py:24
  256.0 6.1 %collective-permute-start.21 = (bf16[432,512]{1,0:T(8,128)(2,1)S(1)}, bf16[432,512]{1,0:T(8,128)(2,1)S(1)}, u32[]{:S(2)}, u32[]{:S(2)}) collective-permute-start(bf16[432,512]{1,0:T(8,128)(2,1)S(1)} %slice.328), channel_id=1, source_target_pairs={{0,12},{12,0},{24,36},{36,24},{48,60},{60,48},{72,84},{84,72},{96,... | collective-permute-start | bytes 1327112 | tf_op jit(solution)/shard_map/ppermute | solution.py:19
  277.3 11.9 %collective-permute-start.22 = (bf16[2,96,256]{2,1,0:T(8,128)(2,1)S(1)}, bf16[2,96,256]{2,1,0:T(8,128)(2,1)S(1)}, u32[]{:S(2)}, u32[]{:S(2)}) collective-permute-start(bf16[2,96,256]{2,1,0:T(8,128)(2,1)S(1)} %slice.330), channel_id=1, source_target_pairs={{0,24},{12,36},{24,0},{36,12},{48,72},{60,84},{72,48},{84,60},{96,... | collective-permute-start | bytes 294920 | tf_op jit(solution)/shard_map/ppermute | solution.py:19
